TPU v7x, 32 devices: a whole 2x2x4 slice. The times are simulated.
32 devices in a mesh: groups: 2 (over y), seq: 4 (over z), tp: 4 (over x, core).
Axes of the slice: x: 2, y: 2, z: 4, core: 2. Of those that a mesh axis runs over, the one named last changes fastest.
Arguments:
- activations: bfloat16 [1024, 8192], P(('groups', 'seq'), 'tp'), parts along dimension 0, may hold values from -24 to 24
- queries: bfloat16 [1024, 8192], P(('groups', 'seq'), 'tp'), parts along dimension 0, may hold values from -24 to 24
- key_weight: bfloat16 [8192, 1024], P(None, 'tp'), may hold values from -0.0625 to 0.0625
- value_weight: bfloat16 [8192, 1024], P(None, 'tp'), may hold values from -0.0625 to 0.0625
- lengths: int32 [8], P('groups'), parts along dimension 0, may hold values from 1 to 320, 512 in all
- owners: int32 [32], P('groups'), parts along dimension 0, may hold values from 0 to 3, as said below
Outputs:
- attention: bfloat16 [1024, 8192], P(('groups', 'seq'), 'tp'), parts along dimension 0
- kv_cache: bfloat16 [1024, 8, 256], P(('groups', 'seq'), 'tp'), parts along dimension 0
There are 2 independent parts, one for each index of `groups`. A program takes and returns all parts, laid end to end along the dimension named above; an argument that names none is the same for every part. Nothing has to cross between parts.
Inputs may be any that keep to these rules, and one draw needn't show every extreme that they name: `owners`: every decode device is named by exactly 4 blocks; among the 4 blocks of the rows of one index of seq, no decode device is named more than 2 times, and some is named exactly 2 times.
All inputs are finite; a program needn't handle non-finite values.
Results may differ from a plain program's by a relative error of at most 0.0045.
The roundings to bfloat16 on the way count: a program that leaves them out, or rounds other values in their place, can miss the bound.
Values may be sent and summed in bfloat16 or wider, within the bound.
No kernel may reach another device: no remote copies, remote signals or barrier semaphores. Data moves between devices by JAX's collectives and lax.ppermute only.
A program may use at most 64 MiB of HBM per device.

v0:
```python
import jax
import jax.numpy as jnp
from jax import lax
from jax.sharding import PartitionSpec as P

HD = 128


def locate(row_ids, lengths):
    prompt_ends = jnp.cumsum(lengths)
    prompt_starts = prompt_ends - lengths
    segment = jnp.sum((row_ids[:, None] >= prompt_ends[None, :]).astype(jnp.int32), axis=1)
    numbers = jnp.arange(lengths.shape[0], dtype=jnp.int32)
    prompt_first = jnp.sum(
        jnp.where(segment[:, None] == numbers[None, :], prompt_starts[None, :], 0), axis=1
    )
    return (segment, row_ids - prompt_first)


def rotate(vectors, positions):
    half_size = vectors.shape[-1] // 2
    exponent = jnp.arange(half_size, dtype=jnp.float32) * (2.0 / vectors.shape[-1])
    inverse = jnp.exp(-exponent * jnp.log(jnp.float32(500000.0)))
    angles = positions.astype(jnp.float32)[:, None] * inverse[None, :]
    cosines = jnp.cos(angles)[:, None, :]
    sine_values = jnp.sin(angles)[:, None, :]
    lower_half = vectors[..., :half_size]
    upper_half = vectors[..., half_size:]
    return jnp.concatenate(
        [
            lower_half * cosines - upper_half * sine_values,
            upper_half * cosines + lower_half * sine_values,
        ],
        axis=-1,
    )


def per_device(activations, queries, key_weight, value_weight, lengths, owners):
    local_rows = activations.shape[0]
    devices = lax.axis_size("seq")
    own_index = lax.axis_index("seq")
    kv_width = key_weight.shape[1]
    kv_heads = kv_width // HD
    query_heads = queries.shape[1] // HD
    group_size = query_heads // kv_heads
    row_ids = own_index * local_rows + jnp.arange(local_rows, dtype=jnp.int32)
    segment, positions = locate(row_ids, lengths)
    portion = lax.all_gather(activations, "tp", axis=1, tiled=True)
    key_rows = key_weight
    key_sums = jnp.dot(portion, key_rows, preferred_element_type=jnp.float32)
    value_sums = jnp.dot(portion, value_weight, preferred_element_type=jnp.float32)
    keys_local = rotate(key_sums.reshape(local_rows, kv_heads, HD), positions).astype(jnp.bfloat16)
    values_local = value_sums.astype(jnp.bfloat16).reshape(local_rows, kv_heads, HD)
    packed = jnp.concatenate([keys_local, values_local], axis=-1).reshape(
        local_rows, kv_heads * 2 * HD
    )
    rotated = rotate(queries.astype(jnp.float32).reshape(local_rows, query_heads, HD), positions)
    rotated = rotated.astype(jnp.bfloat16).reshape(local_rows, kv_heads, group_size, HD)

    def attend_block(running, portion, offset):
        running_max, running_sum, running_out = running
        amount = portion.shape[0]
        paired = portion.reshape(amount, kv_heads, 2 * HD)
        key_part = paired[:, :, :HD]
        value_part = paired[:, :, HD:]
        key_rows = offset + jnp.arange(amount, dtype=jnp.int32)
        key_segment, unused = locate(key_rows, lengths)
        allowed = (
            (key_segment[None, :] == segment[:, None])
            & (key_rows[None, :] <= row_ids[:, None])
            & (key_rows[None, :] >= 0)
        )
        allowed = allowed[:, None, None, :]
        scores = jnp.einsum(
            "qhgd,khd->qhgk", rotated, key_part, preferred_element_type=jnp.float32
        ) / jnp.sqrt(jnp.float32(HD))
        new_max = jnp.maximum(running_max, jnp.max(jnp.where(allowed, scores, -1e30), axis=-1))
        weights = jnp.where(allowed, jnp.exp(scores - new_max[..., None]), 0.0)
        factor = jnp.exp(running_max - new_max)
        running_sum = running_sum * factor + jnp.sum(weights, axis=-1)
        running_out = running_out * factor[..., None] + jnp.einsum(
            "qhgk,khd->qhgd",
            weights.astype(jnp.bfloat16),
            value_part,
            preferred_element_type=jnp.float32,
        )
        return (new_max, running_sum, running_out)

    def attend(running, portion, offset):
        amount = portion.shape[0]
        if amount > 512 and amount % 512 == 0:

            def advance(carried, entry):
                sub_portion, sub_offset = entry
                return (attend_block(carried, sub_portion, offset + sub_offset), None)

            offsets = jnp.arange(amount // 512, dtype=jnp.int32) * 512
            running, unused = lax.scan(
                advance, running, (portion.reshape(amount // 512, 512, portion.shape[1]), offsets)
            )
            return running
        return attend_block(running, portion, offset)

    initial = (
        jnp.full((local_rows, kv_heads, group_size), -1e30, jnp.float32),
        jnp.zeros((local_rows, kv_heads, group_size), jnp.float32),
        jnp.zeros((local_rows, kv_heads, group_size, HD), jnp.float32),
    )
    blocks_dev = owners.shape[0] // devices
    block_len = local_rows // blocks_dev
    is_own = owners == own_index
    ordinal = jnp.cumsum(is_own.astype(jnp.int32)) - 1
    matches = is_own[None, :] & (
        ordinal[None, :] == jnp.arange(blocks_dev, dtype=jnp.int32)[:, None]
    )
    leading = jnp.sum(
        jnp.where(matches, jnp.arange(owners.shape[0], dtype=jnp.int32)[None, :], 0), axis=1
    )
    within = jnp.arange(local_rows, dtype=jnp.int32)
    wanted = jnp.repeat(leading, block_len) * block_len + within % block_len
    portion = lax.all_gather(packed, "seq", axis=0, tiled=True)
    amount = portion.shape[0]
    choose = (wanted[:, None] == jnp.arange(amount, dtype=jnp.int32)[None, :]).astype(jnp.bfloat16)
    running = attend(
        (initial, jnp.zeros((local_rows, packed.shape[1]), jnp.float32))[0], portion, jnp.int32(0)
    )
    taken = jnp.dot(choose, portion, preferred_element_type=jnp.float32)
    kv_cache = taken.astype(jnp.bfloat16).reshape(local_rows, kv_heads, 2 * HD)
    running_max, running_sum, running_out = running
    attention = (
        (running_out / running_sum[..., None])
        .astype(jnp.bfloat16)
        .reshape(local_rows, query_heads * HD)
    )
    return (attention, kv_cache)


def solution(mesh):
    in_specs = (
        P(("groups", "seq"), "tp"),
        P(("groups", "seq"), "tp"),
        P(None, "tp"),
        P(None, "tp"),
        P("groups"),
        P("groups"),
    )
    out_specs = (P(("groups", "seq"), "tp"), P(("groups", "seq"), "tp", None))
    return jax.shard_map(
        per_device, mesh=mesh, in_specs=in_specs, out_specs=out_specs, check_vma=False
    )
```

profile of v0, /device:TPU:0, one launch (start us, length us, event | category | flops | bytes accessed | tf_op | source)
XLA Modules:
  0.0 71.7 jit_solution(17123226598475692947)
XLA Ops:
  7.2 0.0 copy-start.2
  7.2 0.0 copy-start.3
  7.2 0.0 all-gather.2.cloned.1.call-start
  7.2 0.7 all-gather.2.cloned.1.call-update
  7.9 1.1 %convert_bitcast_fusion = f32[16,8,16,128]{3,1,2,0:T(8,128)S(1)} fusion(bf16[128,2048]{1,0:T(8,128)(2,1)} %param.7), kind=kLoop, calls=%fused_computation.16 | loop fusion | flops 262144 | bytes 1572864
  9.1 0.2 copy.34
  9.3 0.0 copy-done.2
  9.3 0.1 copy.26
  9.4 0.0 copy-done.3
  9.4 0.2 reduce-window.16
  9.6 0.1 add_reduce_fusion
  9.7 0.1 select_reduce_fusion
  9.8 0.1 broadcast_in_dim.57
  9.9 0.1 mul.144
  10.0 0.1 convert_reduce_fusion
  10.1 0.1 convert_reduce_fusion.1
  10.2 0.1 select_reduce_fusion.1
  10.3 0.1 fusion.23
  10.4 0.3 multiply_cosine_fusion
  10.7 0.3 fusion.31
  11.1 0.7 subtract_convert_fusion
  11.8 23.1 %all-gather.2.cloned.1.call-done = bf16[128,8192]{1,0:T(8,128)(2,1)} async-done(((bf16[128,2048]{1,0:T(8,128)(2,1)}), bf16[128,8192]{1,0:T(8,128)(2,1)}) %all-gather.2.cloned.1.call-update) | async-done | bytes 2097168 | tf_op jit(solution)/shard_map/all_gather | solution.py:48
  34.9 0.0 copy-start
  34.9 4.3 %fusion.32 = f32[128,256]{1,0:T(8,128)} fusion(bf16[128,8192]{1,0:T(8,128)(2,1)} %all-gather.2.cloned.1.call-done, bf16[8192,256]{1,0:T(8,128)(2,1)} %param.8), kind=kOutput, calls=%fused_computation.60 | convolution fusion | flops 536870912 | bytes 6422528 | tf_op jit(solution)/shard_map/dot_general | solution.py:50
  39.2 1.0 %reshape.227 = f32[128,2,128]{2,1,0:T(2,128)S(1)} reshape(f32[128,256]{1,0:T(8,128)} %fusion.32) | data formatting | bytes 262144 | tf_op jit(solution)/shard_map/reshape | solution.py:52
  40.2 0.9 %subtract_convert_fusion.1 = (bf16[128,2,64]{2,1,0:T(2,128)(2,1)S(1)}, bf16[128,2,64]{2,1,0:T(2,128)(2,1)}) fusion(f32[128,2,128]{2,1,0:T(2,128)S(1)} %reshape.227, f32[128,64]{1,0:T(8,128)S(1)} %get-tuple-element.19, f32[128,64]{1,0:T(8,128)S(1)} %get-tuple-element.18), kind=kLoop, calls=%fused_computation.32 | loop fusion | flops 131072 | bytes 262144 | tf_op jit(solution)/shard_map/convert.6
  41.1 0.0 copy-done
  41.1 0.0 copy-start.1
  41.1 2.9 %convolution_convert_fusion.1 = bf16[128,256]{1,0:T(8,128)(2,1)S(1)} fusion(bf16[128,8192]{1,0:T(8,128)(2,1)S(1)} %copy-done, bf16[8192,256]{1,0:T(8,128)(2,1)} %param.9), kind=kOutput, calls=%fused_computation.15 | convolution fusion | flops 536903680 | bytes 6356992 | tf_op jit(solution)/shard_map/dot_general | solution.py:51
  44.0 0.0 copy-done.1
  44.0 0.3 pad_maximum_fusion
  44.3 0.1 copy.21
  44.5 15.3 %all_gather.7 = bf16[512,512]{0,1:T(8,128)(2,1)S(1)} all-gather(bf16[128,512]{0,1:T(8,128)(2,1)S(1)} %bitcast.62), channel_id=1, replica_groups=mesh['groups'=2,'seq'=4,'tp'=4] {'seq'}, dimensions={0}, use_global_device_ids=true | all-gather | bytes 655360 | tf_op jit(solution)/shard_map/all_gather | solution.py:121
  59.8 1.1 %fusion = (f32[128,2,8]{0,2,1:T(8,128)S(1)}, f32[2,512,128,8]{2,1,3,0:T(8,128)S(1)}) fusion(pred[128,512]{0,1:T(8,128)(4,1)S(1)} %fusion.23, bf16[128,2,8,64]{3,0,2,1:T(8,128)(2,1)S(1)} %bitcast.61, bf16[128,2,8,64]{3,0,2,1:T(8,128)(2,1)S(1)} %bitcast.60, bf16[512,2,256]{0,2,1:T(8,128)(2,1)S(1)} %bitcast.58), kind=kOutput, calls=%fused_computation.2 | convolution fusion | flops 272627712 | bytes 5578752 | tf_op jit(solution)/shard_map/qhgd,khd->qhgk/dot_general | solution.py:74
  60.9 0.9 %fusion.3 = f32[128,2,8]{0,2,1:T(8,128)S(1)} fusion(f32[2,512,128,8]{2,1,3,0:T(8,128)S(1)} %get-tuple-element.21, f32[128,2,8]{0,2,1:T(8,128)S(1)} %broadcast_maximum_fusion, pred[128,512]{0,1:T(8,128)(4,1)S(1)} %fusion.23), kind=kLoop, calls=%fused_computation.5 | loop fusion | flops 4192256 | bytes 4276224 | tf_op jit(solution)/shard_map/reduce_sum | solution.py:80
  61.8 1.0 %divide_convert_fusion = bf16[128,2,8,128]{0,3,2,1:T(8,128)(2,1)S(1)} fusion(f32[2,512,128,8]{2,1,3,0:T(8,128)S(1)} %get-tuple-element.21, f32[128,2,8]{0,2,1:T(8,128)S(1)} %broadcast_maximum_fusion, pred[128,512]{0,1:T(8,128)(4,1)S(1)} %fusion.23, f32[128,2,8]{0,2,1:T(8,128)S(1)} %get-tuple-element.17, f32[128,2,8]{0,2,1:T(8,128)S(1)} %get-tuple-element.16, ...), kind=kOutput, calls=%fused_computation.17 | convolution fusion | flops 273416192 | bytes 5070848 | tf_op jit(solution)/shard_map/qhgk,khd->qhgd/dot_general | solution.py:81
  62.8 1.0 %copy.27 = bf16[128,2048]{1,0:T(8,128)(2,1)} copy(bf16[128,2048]{0,1:T(8,128)(2,1)S(1)} %bitcast.63) | data formatting | bytes 1048576
  63.8 0.3 convolution_convert_fusion
  64.1 0.7 reshape.235
  (11 shorter events, 0.1 us)
Async XLA Ops:
  7.2 2.1 %copy-start.2 = (s32[16]{0:T(128)S(1)}, s32[16]{0:T(128)}, u32[]{:S(2)}) copy-start(s32[16]{0:T(128)} %param.11) | copy-start | bytes 196
  7.2 2.2 %copy-start.3 = (s32[4]{0:T(128)S(1)}, s32[4]{0:T(128)}, u32[]{:S(2)}) copy-start(s32[4]{0:T(128)} %param.10) | copy-start | bytes 52
  7.2 27.7 %all-gather.2.cloned.1.call-start = ((), (), s32[]{:S(2)}) async-start(), calls=%async_computation | async-start | bytes 2621440 | tf_op jit(solution)/shard_map/all_gather | solution.py:48
  34.9 6.2 %copy-start = (bf16[128,8192]{1,0:T(8,128)(2,1)S(1)}, bf16[128,8192]{1,0:T(8,128)(2,1)}, u32[]{:S(2)}) copy-start(bf16[128,8192]{1,0:T(8,128)(2,1)} %all-gather.2.cloned.1.call-done) | copy-start | bytes 6291460
  41.1 3.0 %copy-start.1 = (bf16[128,2,64]{2,1,0:T(2,128)(2,1)S(1)}, bf16[128,2,64]{2,1,0:T(2,128)(2,1)}, u32[]{:S(2)}) copy-start(bf16[128,2,64]{2,1,0:T(2,128)(2,1)} %get-tuple-element.15) | copy-start | bytes 98308
Sparse Core Ops, SparseCore 0:
  9.6 25.2 all-gather.1
where the time goes:
time: 71.9 us; the launch traced here: 71.7 us
  waiting for transfers between devices  23.8 us (33%)
  blocking collectives  15.3 us (21%)
  between operations  14.2 us (20%)
  matrix products  9.66 us (13%)
  other arithmetic  5.07 us (7%)
  local copies, waits for them, and re-layouts  3.61 us (5%)
    all_gather x1, waiting for transfers between devices, per_device(): portion = lax.all_gather(activations, 'tp', axis=1, tiled=True)  23.1 us
    all_gather x1, blocking collectives, per_device(): portion = lax.all_gather(packed, 'seq', axis=0, tiled=True)  15.3 us
    dot_general x1, matrix products, per_device(): key_sums = jnp.dot(portion, key_rows, preferred_element_type=jnp.float32)  4.34 us
    dot_general x1, matrix products, per_device(): jnp.dot(portion, value_weight, preferred_element_type=jnp.float32)  2.93 us
    another operation x5, other arithmetic  1.78 us
  transfers between devices with their start and end apart: 1, of which 1 were waited for; matrix products, arithmetic and copies ran while one was open for 5% of the time, Pallas kernels for 0%

commit v1 on v0

--- a/solution.py
+++ b/solution.py
@@ -35,6 +35,45 @@
     )
 
 
+def swap(array, axis, distance):
+    count = lax.axis_size(axis)
+    return lax.ppermute(array, axis, [(i, i ^ distance) for i in range(count)])
+
+
+def is_power(count):
+    return count & (count - 1) == 0
+
+
+def split_rows(rows):
+    half = rows // 2
+    return [(0, half), (half, rows - half)] if half % 16 == 0 and half else [(0, rows)]
+
+
+def project(activations, weights, chunks):
+    parts = lax.axis_size("tp")
+    own = lax.axis_index("tp")
+    width = activations.shape[1]
+
+    def rows_of(offset):
+        return lax.dynamic_slice_in_dim(weights, (own ^ offset) * width, width, 0)
+
+    pieces = {c: {0: activations[start : start + size]} for c, (start, size) in enumerate(chunks)}
+    distance = parts // 2
+    while distance:
+        for c in pieces:
+            for offset in list(pieces[c]):
+                pieces[c][offset ^ distance] = swap(pieces[c][offset], "tp", distance)
+        distance //= 2
+    sums = []
+    for c in pieces:
+        total = None
+        for offset in sorted(pieces[c]):
+            term = jnp.dot(pieces[c][offset], rows_of(offset), preferred_element_type=jnp.float32)
+            total = term if total is None else total + term
+        sums.append(total)
+    return sums
+
+
 def per_device(activations, queries, key_weight, value_weight, lengths, owners):
     local_rows = activations.shape[0]
     devices = lax.axis_size("seq")
@@ -45,15 +84,25 @@
     group_size = query_heads // kv_heads
     row_ids = own_index * local_rows + jnp.arange(local_rows, dtype=jnp.int32)
     segment, positions = locate(row_ids, lengths)
-    portion = lax.all_gather(activations, "tp", axis=1, tiled=True)
-    key_rows = key_weight
-    key_sums = jnp.dot(portion, key_rows, preferred_element_type=jnp.float32)
-    value_sums = jnp.dot(portion, value_weight, preferred_element_type=jnp.float32)
-    keys_local = rotate(key_sums.reshape(local_rows, kv_heads, HD), positions).astype(jnp.bfloat16)
-    values_local = value_sums.astype(jnp.bfloat16).reshape(local_rows, kv_heads, HD)
-    packed = jnp.concatenate([keys_local, values_local], axis=-1).reshape(
-        local_rows, kv_heads * 2 * HD
-    )
+    chunks = split_rows(local_rows)
+    weights = jnp.concatenate([key_weight, value_weight], axis=1)
+    arrived = []
+    for (start, size), sums in zip(chunks, project(activations, weights, chunks)):
+        keys_local = rotate(
+            sums[:, :kv_width].reshape(size, kv_heads, HD), positions[start : start + size]
+        ).astype(jnp.bfloat16)
+        values_local = sums[:, kv_width:].astype(jnp.bfloat16).reshape(size, kv_heads, HD)
+        packed = jnp.concatenate([keys_local, values_local], axis=-1).reshape(
+            size, kv_heads * 2 * HD
+        )
+        by_offset = [packed] + [swap(packed, "seq", k) for k in range(1, devices)]
+        arrived.append(by_offset)
+    by_offset = [jnp.concatenate([part[k] for part in arrived], axis=0) for k in range(devices)]
+    stacked = jnp.stack(by_offset, axis=0)
+    order = own_index ^ jnp.arange(devices, dtype=jnp.int32)
+    key_row_ids = (
+        order[:, None] * local_rows + jnp.arange(local_rows, dtype=jnp.int32)[None, :]
+    ).reshape(-1)
     rotated = rotate(queries.astype(jnp.float32).reshape(local_rows, query_heads, HD), positions)
     rotated = rotated.astype(jnp.bfloat16).reshape(local_rows, kv_heads, group_size, HD)
 
@@ -63,7 +112,7 @@
         paired = portion.reshape(amount, kv_heads, 2 * HD)
         key_part = paired[:, :, :HD]
         value_part = paired[:, :, HD:]
-        key_rows = offset + jnp.arange(amount, dtype=jnp.int32)
+        key_rows = offset
         key_segment, unused = locate(key_rows, lengths)
         allowed = (
             (key_segment[None, :] == segment[:, None])
@@ -86,21 +135,6 @@
         )
         return (new_max, running_sum, running_out)
 
-    def attend(running, portion, offset):
-        amount = portion.shape[0]
-        if amount > 512 and amount % 512 == 0:
-
-            def advance(carried, entry):
-                sub_portion, sub_offset = entry
-                return (attend_block(carried, sub_portion, offset + sub_offset), None)
-
-            offsets = jnp.arange(amount // 512, dtype=jnp.int32) * 512
-            running, unused = lax.scan(
-                advance, running, (portion.reshape(amount // 512, 512, portion.shape[1]), offsets)
-            )
-            return running
-        return attend_block(running, portion, offset)
-
     initial = (
         jnp.full((local_rows, kv_heads, group_size), -1e30, jnp.float32),
         jnp.zeros((local_rows, kv_heads, group_size), jnp.float32),
@@ -118,12 +152,9 @@
     )
     within = jnp.arange(local_rows, dtype=jnp.int32)
     wanted = jnp.repeat(leading, block_len) * block_len + within % block_len
-    portion = lax.all_gather(packed, "seq", axis=0, tiled=True)
-    amount = portion.shape[0]
-    choose = (wanted[:, None] == jnp.arange(amount, dtype=jnp.int32)[None, :]).astype(jnp.bfloat16)
-    running = attend(
-        (initial, jnp.zeros((local_rows, packed.shape[1]), jnp.float32))[0], portion, jnp.int32(0)
-    )
+    portion = stacked.reshape(devices * local_rows, -1)
+    choose = (wanted[:, None] == key_row_ids[None, :]).astype(jnp.bfloat16)
+    running = attend_block(initial, portion, key_row_ids)
     taken = jnp.dot(choose, portion, preferred_element_type=jnp.float32)
     kv_cache = taken.astype(jnp.bfloat16).reshape(local_rows, kv_heads, 2 * HD)
     running_max, running_sum, running_out = running

time: 71.9 us -> 63.1 us (0.88)
  waiting for transfers between devices: 23.8 us -> 5.61 us
  blocking collectives: 15.3 us -> 0 us
  starting transfers between devices: 0.04 us -> 13.6 us
  between operations: 14.2 us -> 1.05 us
  local copies, waits for them, and re-layouts: 3.61 us -> 16.1 us
  matrix products: 9.66 us -> 21.5 us
    all_gather x1 -> x0, waiting for transfers between devices: 23.1 us -> none  [per_device(): portion = lax.all_gather(activations, 'tp', axis=1, tiled=True)]
    all_gather x1 -> x0, blocking collectives: 15.3 us -> none  [per_device(): portion = lax.all_gather(packed, 'seq', axis=0, tiled=True)]
    ppermute x0 -> x12, starting transfers between devices: none -> 13.6 us  [swap(): return lax.ppermute(array, axis, [(i, i ^ distance) for i in range(count)])]
    dot_general x2 -> x8, matrix products: 7.27 us -> 17 us  [project(): jnp.dot(pieces[c][offset], rows_of(offset), preferred_element_type=jnp.fl...]
    unnamed x10 -> x20, local copies, waits for them, and re-layouts: 1.21 us -> 7.8 us
    ppermute x0 -> x12, waiting for transfers between devices: none -> 5.61 us  [swap(): return lax.ppermute(array, axis, [(i, i ^ distance) for i in range(count)])]
    concatenate x1, local copies, waits for them, and re-layouts: 0.14 us -> 4.54 us  [per_device(): weights = jnp.concatenate([key_weight, value_weight], axis=1)]
    slice x0 -> x6, local copies, waits for them, and re-layouts: none -> 2.27 us  [the longest x1 1.88 us: project(): activations[start:start + size]]
  transfers between devices with their start and end apart: 1 -> 12, of which waited for: 1 -> 2; matrix products, arithmetic and copies ran while one was open for 5% -> 45% of each run, Pallas kernels for 0% -> 0%
where the time goes in v1:
time: 63.1 us; the launch traced here: 62.6 us
  matrix products  21.5 us (34%)
  local copies, waits for them, and re-layouts  16.1 us (26%)
  starting transfers between devices  13.6 us (22%)
  waiting for transfers between devices  5.61 us (9%)
  other arithmetic  4.74 us (8%)
  between operations  1.05 us (2%)
    dot_general x8, matrix products, project(): jnp.dot(pieces[c][offset], rows_of(offset), preferred_element_type=jnp.fl...  17 us
    ppermute x12, starting transfers between devices, swap(): return lax.ppermute(array, axis, [(i, i ^ distance) for i in range(count)])  13.6 us
    unnamed x20, local copies, waits for them, and re-layouts  7.8 us
    ppermute x12, waiting for transfers between devices, swap(): return lax.ppermute(array, axis, [(i, i ^ distance) for i in range(count)])  5.61 us
    concatenate x1, local copies, waits for them, and re-layouts, per_device(): weights = jnp.concatenate([key_weight, value_weight], axis=1)  4.54 us
    dot_general x1, matrix products, attend_block(): jnp.einsum('qhgk,khd->qhgd', weights.astype(jnp.bfloat16), value_part, pr...  3.19 us
    slice x1, local copies, waits for them, and re-layouts, project(): activations[start:start + size]  1.88 us
  transfers between devices with their start and end apart: 12, of which 2 were waited for; matrix products, arithmetic and copies ran while one was open for 45% of the time, Pallas kernels for 0%

profile of v1, /device:TPU:0, one launch (start us, length us, event | category | flops | bytes accessed | tf_op | source)
XLA Modules:
  0.0 62.6 jit_solution(15574737952714710041)
XLA Ops:
  0.6 1.9 %fusion.88 = (bf16[64,2048]{1,0:T(8,128)(2,1)}, bf16[64,2048]{1,0:T(8,128)(2,1)}) fusion(bf16[128,2048]{1,0:T(8,128)(2,1)} %param.6), kind=kLoop, calls=%fused_computation.115 | loop fusion | bytes 1048576 | tf_op jit(solution)/shard_map/slice | solution.py:60
  2.5 3.0 %collective-permute-start.1 = (bf16[64,2048]{1,0:T(8,128)(2,1)}, bf16[64,2048]{1,0:T(8,128)(2,1)}, u32[]{:S(2)}, u32[]{:S(2)}) collective-permute-start(bf16[64,2048]{1,0:T(8,128)(2,1)} %get-tuple-element.18), channel_id=1, source_target_pairs={{0,2},{1,3},{2,0},{3,1},{4,6},{5,7},{6,4},{7,5},{8,10},{9,11},{10,... | collective-permute-start | bytes 786440 | tf_op jit(solution)/shard_map/ppermute | solution.py:40
  5.5 0.4 collective-permute-start.3
  6.0 4.5 %constant_dynamic-update-slice_fusion.1 = bf16[8192,512]{1,0:T(8,128)(2,1)} fusion(bf16[8192,256]{1,0:T(8,128)(2,1)} %param.8), kind=kLoop, calls=%fused_computation.76 | loop fusion | bytes 8388608
  10.5 4.5 %constant_dynamic-update-slice_fusion = bf16[8192,512]{1,0:T(8,128)(2,1)} fusion(bf16[8192,512]{1,0:T(8,128)(2,1)} %constant_dynamic-update-slice_fusion.1, bf16[8192,256]{1,0:T(8,128)(2,1)} %param.9), kind=kLoop, calls=%fused_computation.75 | loop fusion | bytes 8388608 | tf_op jit(solution)/shard_map/concatenate | solution.py:88
  15.0 2.1 %fusion.23 = f32[512,64]{0,1:T(8,128)S(1)} fusion(bf16[8192,512]{1,0:T(8,128)(2,1)} %constant_dynamic-update-slice_fusion, s32[]{:T(128)S(6)} %select_n.42, bf16[128,2048]{1,0:T(8,128)(2,1)S(1)} %copy-done.1), kind=kOutput, calls=%fused_computation.24 | convolution fusion | flops 134217728 | bytes 2490372 | tf_op jit(solution)/shard_map/dot_general | solution.py:71
  17.1 2.1 %fusion.25 = f32[512,64]{0,1:T(8,128)S(1)} fusion(bf16[8192,512]{1,0:T(8,128)(2,1)} %constant_dynamic-update-slice_fusion, s32[]{:T(128)S(6)} %select_n.42, bf16[128,2048]{1,0:T(8,128)(2,1)S(1)} %copy-done.1), kind=kOutput, calls=%fused_computation.26 | convolution fusion | flops 134217728 | bytes 2490372 | tf_op jit(solution)/shard_map/dot_general | solution.py:71
  19.4 0.2 reduce-window.16
  19.7 0.1 select_reduce_fusion.1
  19.9 0.1 convert_bitcast_fusion
  20.0 0.2 copy.37
  20.1 0.3 fusion.86
  20.5 0.1 convert_reduce_fusion
  20.7 0.1 add_reduce_fusion
  20.8 0.3 multiply_cosine_fusion
  21.1 0.8 %multiply_cosine_fusion.2 = (f32[64,64]{1,0:T(8,128)S(1)}, f32[64,64]{1,0:T(8,128)S(1)}, f32[64,64]{1,0:T(8,128)}, f32[64,64]{1,0:T(8,128)}) fusion(f32[64]{0:T(128)S(1)} %multiply_exponential_fusion, f32[64]{0:T(128)S(1)} %get-tuple-element.34, f32[64]{0:T(128)S(1)} %get-tuple-element.35), kind=kLoop, calls=%fused_computation.71 | loop fusion | flops 8192 | bytes 66304 | tf_op jit(solution)/shard_map/cos | solution.py:25
  22.0 0.3 and_and_fusion
  22.2 0.1 select_reduce_fusion
  22.4 0.7 %subtract_convert_fusion = (bf16[128,16,64]{2,0,1:T(8,128)(2,1)S(1)}, bf16[128,16,64]{2,0,1:T(8,128)(2,1)S(1)}) fusion(f32[128,16,64]{2,1,0:T(8,128)S(1)} %get-tuple-element.15, f32[128,16,64]{2,1,0:T(8,128)S(1)} %get-tuple-element.14, f32[128,64]{1,0:T(8,128)S(1)} %get-tuple-element.31, f32[128,64]{1,0:T(8,128)S(1)} %get-tuple-element.30), kind=kLoop, calls=%fused_computation.42 | loop fusion | flops 1048576 | bytes 1638400 | tf_op jit(solution)/shard_map/convert.5
  23.1 0.1 mul.255
  23.2 0.1 collective-permute-start.2
  23.4 0.4 collective-permute-start.5
  23.8 2.2 %fusion.15 = f32[512,64]{0,1:T(8,128)S(1)} fusion(bf16[64,2048]{1,0:T(8,128)(2,1)} %collective-permute-done.1, bf16[8192,512]{1,0:T(8,128)(2,1)} %constant_dynamic-update-slice_fusion, s32[]{:T(128)S(6)} %select_n.44), kind=kOutput, calls=%fused_computation.16 | convolution fusion | flops 134217728 | bytes 2490372 | tf_op jit(solution)/shard_map/dot_general | solution.py:71
  26.0 2.2 %fusion.42 = f32[512,64]{0,1:T(8,128)S(1)} fusion(f32[512,64]{0,1:T(8,128)S(1)} %fusion.15, f32[512,64]{0,1:T(8,128)S(1)} %fusion.23, bf16[64,2048]{1,0:T(8,128)(2,1)} %collective-permute-done, bf16[8192,512]{1,0:T(8,128)(2,1)} %constant_dynamic-update-slice_fusion, s32[]{:T(128)S(6)} %select_n.43), kind=kOutput, calls=%fused_computation.34 | convolution fusion | flops 134283264 | bytes 2752516 | tf_op jit(solution)/shard_map/dot_general | solution.py:71
  28.2 2.2 %fusion.17 = f32[512,64]{0,1:T(8,128)S(1)} fusion(bf16[64,2048]{1,0:T(8,128)(2,1)} %collective-permute-done.4, bf16[8192,512]{1,0:T(8,128)(2,1)} %constant_dynamic-update-slice_fusion, s32[]{:T(128)S(6)} %select_n.44), kind=kOutput, calls=%fused_computation.18 | convolution fusion | flops 134217728 | bytes 2490372 | tf_op jit(solution)/shard_map/dot_general | solution.py:71
  30.4 2.2 %fusion.36 = f32[512,64]{0,1:T(8,128)S(1)} fusion(f32[512,64]{0,1:T(8,128)S(1)} %fusion.17, f32[512,64]{0,1:T(8,128)S(1)} %fusion.25, bf16[64,2048]{1,0:T(8,128)(2,1)} %collective-permute-done.3, bf16[8192,512]{1,0:T(8,128)(2,1)} %constant_dynamic-update-slice_fusion, s32[]{:T(128)S(6)} %select_n.43), kind=kOutput, calls=%fused_computation.32 | convolution fusion | flops 134283264 | bytes 2752516 | tf_op jit(solution)/shard_map/dot_general | solution.py:71
  32.6 2.1 %fusion.54 = f32[64,512]{1,0:T(8,128)S(1)} fusion(f32[512,64]{0,1:T(8,128)S(1)} %fusion.42, bf16[64,2048]{1,0:T(8,128)(2,1)S(1)} %collective-permute-done.2, bf16[8192,512]{1,0:T(8,128)(2,1)} %constant_dynamic-update-slice_fusion, s32[]{:T(128)S(6)} %select_n.45), kind=kOutput, calls=%fused_computation.38 | convolution fusion | flops 134250496 | bytes 2621444 | tf_op jit(solution)/shard_map/dot_general | solution.py:71
  34.7 2.1 %fusion.48 = f32[64,512]{1,0:T(8,128)S(1)} fusion(f32[512,64]{0,1:T(8,128)S(1)} %fusion.36, bf16[64,2048]{1,0:T(8,128)(2,1)S(1)} %collective-permute-done.5, bf16[8192,512]{1,0:T(8,128)(2,1)} %constant_dynamic-update-slice_fusion, s32[]{:T(128)S(6)} %select_n.45), kind=kOutput, calls=%fused_computation.36 | convolution fusion | flops 134250496 | bytes 2621444 | tf_op jit(solution)/shard_map/dot_general | solution.py:71
  36.9 0.3 subtract_convert_fusion.1
  37.2 0.1 pad_maximum_fusion.1
  37.4 1.9 %collective-permute-start.6 = (bf16[64,512]{1,0:T(8,128)(2,1)S(1)}, bf16[64,512]{1,0:T(8,128)(2,1)S(1)}, u32[]{:S(2)}, u32[]{:S(2)}) collective-permute-start(bf16[64,512]{1,0:T(8,128)(2,1)S(1)} %bitcast.84), channel_id=1, source_target_pairs={{0,4},{4,0},{8,12},{12,8},{1,5},{5,1},{9,13},{13,9},{2,6},{6,2},{1... | collective-permute-start | bytes 196616 | tf_op jit(solution)/shard_map/ppermute | solution.py:40
  39.3 2.6 %collective-permute-start.8 = (bf16[64,512]{1,0:T(8,128)(2,1)S(1)}, bf16[64,512]{1,0:T(8,128)(2,1)S(1)}, u32[]{:S(2)}, u32[]{:S(2)}) collective-permute-start(bf16[64,512]{1,0:T(8,128)(2,1)S(1)} %bitcast.85), channel_id=1, source_target_pairs={{0,8},{4,12},{8,0},{12,4},{1,9},{5,13},{9,1},{13,5},{2,10},{6,14},... | collective-permute-start | bytes 196616 | tf_op jit(solution)/shard_map/ppermute | solution.py:40
  41.9 0.1 pad_maximum_fusion.2
  42.1 0.5 collective-permute-start.7
  42.7 3.9 %collective-permute-start.10 = (bf16[64,512]{1,0:T(8,128)(2,1)S(1)}, bf16[64,512]{1,0:T(8,128)(2,1)S(1)}, u32[]{:S(2)}, u32[]{:S(2)}) collective-permute-start(bf16[64,512]{1,0:T(8,128)(2,1)S(1)} %bitcast.86), channel_id=1, source_target_pairs={{0,12},{4,8},{8,4},{12,0},{1,13},{5,9},{9,5},{13,1},{2,14},{6,10},... | collective-permute-start | bytes 196616 | tf_op jit(solution)/shard_map/ppermute | solution.py:40
  46.5 0.6 collective-permute-start.11
  47.2 4.5 %collective-permute-done.9 = bf16[64,512]{1,0:T(8,128)(2,1)S(1)} collective-permute-done((bf16[64,512]{1,0:T(8,128)(2,1)S(1)}, bf16[64,512]{1,0:T(8,128)(2,1)S(1)}, u32[]{:S(2)}, u32[]{:S(2)}) %collective-permute-start.9) | collective-permute-done | bytes 65568 | tf_op jit(solution)/shard_map/ppermute | solution.py:40
  51.7 1.1 %collective-permute-done.11 = bf16[64,512]{1,0:T(8,128)(2,1)S(1)} collective-permute-done((bf16[64,512]{1,0:T(8,128)(2,1)S(1)}, bf16[64,512]{1,0:T(8,128)(2,1)S(1)}, u32[]{:S(2)}, u32[]{:S(2)}) %collective-permute-start.11) | collective-permute-done | bytes 65568 | tf_op jit(solution)/shard_map/ppermute | solution.py:40
  52.9 0.1 reshape_reshape.3
  53.0 0.4 fusion.87
  53.4 1.0 %fusion = (f32[128,2,8]{0,2,1:T(8,128)S(1)}, f32[2,512,128,8]{2,1,3,0:T(8,128)S(1)}) fusion(pred[128,512]{0,1:T(8,128)(4,1)S(1)} %and_and_fusion, bf16[128,2,8,64]{3,0,2,1:T(8,128)(2,1)S(1)} %bitcast.80, bf16[128,2,8,64]{3,0,2,1:T(8,128)(2,1)S(1)} %bitcast.79, bf16[512,2,128]{2,1,0:T(2,128)(2,1)S(1)} %get-tuple-element.17), kind=kOutput, calls=%fused_computation.2 | convolution fusion | flops 272627712 | bytes 5054464 | tf_op jit(solution)/shard_map/qhgd,khd->qhgk/dot_general | solution.py:123
  54.4 1.9 %copy-done = f32[2,512,128,8]{2,1,3,0:T(8,128)} copy-done((f32[2,512,128,8]{2,1,3,0:T(8,128)}, f32[2,512,128,8]{2,1,3,0:T(8,128)S(1)}, u32[]{:S(2)}) %copy-start) | copy-done | bytes 4194328
  56.3 0.9 %fusion.3 = f32[128,2,8]{0,2,1:T(8,128)S(1)} fusion(f32[2,512,128,8]{2,1,3,0:T(8,128)S(1)} %get-tuple-element.37, f32[128,2,8]{0,2,1:T(8,128)S(1)} %broadcast_maximum_fusion, pred[128,512]{0,1:T(8,128)(4,1)S(1)} %and_and_fusion), kind=kLoop, calls=%fused_computation.5 | loop fusion | flops 4192256 | bytes 4276224 | tf_op jit(solution)/shard_map/reduce_sum | solution.py:129
  57.2 0.2 copy.34
  57.4 3.2 %divide_convert_fusion = bf16[128,2,8,128]{0,3,2,1:T(8,128)(2,1)S(1)} fusion(f32[2,512,128,8]{2,1,3,0:T(8,128)} %copy-done, f32[128,2,8]{0,2,1:T(8,128)S(1)} %broadcast_maximum_fusion, pred[128,512]{0,1:T(8,128)(4,1)S(1)} %and_and_fusion, f32[128,2,8]{0,2,1:T(8,128)S(1)} %get-tuple-element.25, f32[128,2,8]{0,2,1:T(8,128)S(1)} %get-tuple-element.24, ...), kind=kOutput, calls=%fused_computation.40 | convolution fusion | flops 273416192 | bytes 5070848 | tf_op jit(solution)/shard_map/qhgk,khd->qhgd/dot_general | solution.py:130
  60.6 1.0 %copy.27 = bf16[128,2048]{1,0:T(8,128)(2,1)} copy(bf16[128,2048]{0,1:T(8,128)(2,1)S(1)} %bitcast.81) | data formatting | bytes 1048576
  61.6 0.4 convolution_convert_fusion
  61.9 0.7 %reshape.396 = bf16[128,2,256]{2,1,0:T(2,128)(2,1)} reshape(bf16[128,512]{1,0:T(8,128)(2,1)S(1)} %convolution_convert_fusion) | data formatting | bytes 262144 | tf_op jit(solution)/shard_map/reshape | solution.py:159
  (58 shorter events, 1.0 us)
Async XLA Ops:
  2.5 20.7 %collective-permute-start.1 = (bf16[64,2048]{1,0:T(8,128)(2,1)}, bf16[64,2048]{1,0:T(8,128)(2,1)}, u32[]{:S(2)}, u32[]{:S(2)}) collective-permute-start(bf16[64,2048]{1,0:T(8,128)(2,1)} %get-tuple-element.18), channel_id=1, source_target_pairs={{0,2},{1,3},{2,0},{3,1},{4,6},{5,7},{6,4},{7,5},{8,10},{9,11},{10,... | collective-permute-start | bytes 786440 | tf_op jit(solution)/shard_map/ppermute | solution.py:40
  5.5 20.5 %collective-permute-start = (bf16[64,2048]{1,0:T(8,128)(2,1)}, bf16[64,2048]{1,0:T(8,128)(2,1)}, u32[]{:S(2)}, u32[]{:S(2)}) collective-permute-start(bf16[64,2048]{1,0:T(8,128)(2,1)} %get-tuple-element.18), channel_id=1, source_target_pairs={{0,1},{1,0},{2,3},{3,2},{4,5},{5,4},{6,7},{7,6},{8,9},{9,8},{10,11... | collective-permute-start | bytes 786440 | tf_op jit(solution)/shard_map/ppermute | solution.py:40
  5.5 17.9 %collective-permute-start.4 = (bf16[64,2048]{1,0:T(8,128)(2,1)}, bf16[64,2048]{1,0:T(8,128)(2,1)}, u32[]{:S(2)}, u32[]{:S(2)}) collective-permute-start(bf16[64,2048]{1,0:T(8,128)(2,1)} %get-tuple-element.19), channel_id=1, source_target_pairs={{0,2},{1,3},{2,0},{3,1},{4,6},{5,7},{6,4},{7,5},{8,10},{9,11},{10,... | collective-permute-start | bytes 786440 | tf_op jit(solution)/shard_map/ppermute | solution.py:40
  5.5 24.8 %collective-permute-start.3 = (bf16[64,2048]{1,0:T(8,128)(2,1)}, bf16[64,2048]{1,0:T(8,128)(2,1)}, u32[]{:S(2)}, u32[]{:S(2)}) collective-permute-start(bf16[64,2048]{1,0:T(8,128)(2,1)} %get-tuple-element.19), channel_id=1, source_target_pairs={{0,1},{1,0},{2,3},{3,2},{4,5},{5,4},{6,7},{7,6},{8,9},{9,8},{10,11... | collective-permute-start | bytes 786440 | tf_op jit(solution)/shard_map/ppermute | solution.py:40
  10.5 4.5 %copy-start.1 = (bf16[128,2048]{1,0:T(8,128)(2,1)S(1)}, bf16[128,2048]{1,0:T(8,128)(2,1)}, u32[]{:S(2)}) copy-start(bf16[128,2048]{1,0:T(8,128)(2,1)} %param.6) | copy-start | bytes 1572868
  15.0 4.4 %copy-start.6 = (s32[4]{0:T(128)S(1)}, s32[4]{0:T(128)}, u32[]{:S(2)}) copy-start(s32[4]{0:T(128)} %param.10) | copy-start | bytes 52
  15.0 4.8 %copy-start.2 = (bf16[128,2048]{1,0:T(8,128)(2,1)S(1)}, bf16[128,2048]{1,0:T(8,128)(2,1)}, u32[]{:S(2)}) copy-start(bf16[128,2048]{1,0:T(8,128)(2,1)} %param.7) | copy-start | bytes 1572868
  19.2 1.4 %copy-start.5 = (s32[16]{0:T(128)S(1)}, s32[16]{0:T(128)}, u32[]{:S(2)}) copy-start(s32[16]{0:T(128)} %param.11) | copy-start | bytes 196
  23.2 9.3 %collective-permute-start.2 = (bf16[64,2048]{1,0:T(8,128)(2,1)}, bf16[64,2048]{1,0:T(8,128)(2,1)S(1)}, u32[]{:S(2)}, u32[]{:S(2)}) collective-permute-start(bf16[64,2048]{1,0:T(8,128)(2,1)} %collective-permute-done.1), channel_id=1, source_target_pairs={{0,1},{1,0},{2,3},{3,2},{4,5},{5,4},{6,7},{7,6},{8,9},{9,8},{10,11... | collective-permute-start | bytes 786440 | tf_op jit(solution)/shard_map/ppermute | solution.py:40
  23.4 11.3 %collective-permute-start.5 = (bf16[64,2048]{1,0:T(8,128)(2,1)}, bf16[64,2048]{1,0:T(8,128)(2,1)S(1)}, u32[]{:S(2)}, u32[]{:S(2)}) collective-permute-start(bf16[64,2048]{1,0:T(8,128)(2,1)} %collective-permute-done.4), channel_id=1, source_target_pairs={{0,1},{1,0},{2,3},{3,2},{4,5},{5,4},{6,7},{7,6},{8,9},{9,8},{10,11... | collective-permute-start | bytes 786440 | tf_op jit(solution)/shard_map/ppermute | solution.py:40
  30.3 6.6 %copy-start.3 = (f32[64,64]{1,0:T(8,128)S(1)}, f32[64,64]{1,0:T(8,128)}, u32[]{:S(2)}) copy-start(f32[64,64]{1,0:T(8,128)} %get-tuple-element.32) | copy-start | bytes 49156
  30.3 6.6 %copy-start.4 = (f32[64,64]{1,0:T(8,128)S(1)}, f32[64,64]{1,0:T(8,128)}, u32[]{:S(2)}) copy-start(f32[64,64]{1,0:T(8,128)} %get-tuple-element.33) | copy-start | bytes 49156
  37.4 9.1 %collective-permute-start.6 = (bf16[64,512]{1,0:T(8,128)(2,1)S(1)}, bf16[64,512]{1,0:T(8,128)(2,1)S(1)}, u32[]{:S(2)}, u32[]{:S(2)}) collective-permute-start(bf16[64,512]{1,0:T(8,128)(2,1)S(1)} %bitcast.84), channel_id=1, source_target_pairs={{0,4},{4,0},{8,12},{12,8},{1,5},{5,1},{9,13},{13,9},{2,6},{6,2},{1... | collective-permute-start | bytes 196616 | tf_op jit(solution)/shard_map/ppermute | solution.py:40
  39.3 7.9 %collective-permute-start.8 = (bf16[64,512]{1,0:T(8,128)(2,1)S(1)}, bf16[64,512]{1,0:T(8,128)(2,1)S(1)}, u32[]{:S(2)}, u32[]{:S(2)}) collective-permute-start(bf16[64,512]{1,0:T(8,128)(2,1)S(1)} %bitcast.85), channel_id=1, source_target_pairs={{0,8},{4,12},{8,0},{12,4},{1,9},{5,13},{9,1},{13,5},{2,10},{6,14},... | collective-permute-start | bytes 196616 | tf_op jit(solution)/shard_map/ppermute | solution.py:40
  42.1 5.1 %collective-permute-start.7 = (bf16[64,512]{1,0:T(8,128)(2,1)S(1)}, bf16[64,512]{1,0:T(8,128)(2,1)S(1)}, u32[]{:S(2)}, u32[]{:S(2)}) collective-permute-start(bf16[64,512]{1,0:T(8,128)(2,1)S(1)} %bitcast.88), channel_id=1, source_target_pairs={{0,4},{4,0},{8,12},{12,8},{1,5},{5,1},{9,13},{13,9},{2,6},{6,2},{1... | collective-permute-start | bytes 196616 | tf_op jit(solution)/shard_map/ppermute | solution.py:40
  42.6 9.1 %collective-permute-start.9 = (bf16[64,512]{1,0:T(8,128)(2,1)S(1)}, bf16[64,512]{1,0:T(8,128)(2,1)S(1)}, u32[]{:S(2)}, u32[]{:S(2)}) collective-permute-start(bf16[64,512]{1,0:T(8,128)(2,1)S(1)} %bitcast.89), channel_id=1, source_target_pairs={{0,8},{4,12},{8,0},{12,4},{1,9},{5,13},{9,1},{13,5},{2,10},{6,14},... | collective-permute-start | bytes 196616 | tf_op jit(solution)/shard_map/ppermute | solution.py:40
  42.7 9.1 %collective-permute-start.10 = (bf16[64,512]{1,0:T(8,128)(2,1)S(1)}, bf16[64,512]{1,0:T(8,128)(2,1)S(1)}, u32[]{:S(2)}, u32[]{:S(2)}) collective-permute-start(bf16[64,512]{1,0:T(8,128)(2,1)S(1)} %bitcast.86), channel_id=1, source_target_pairs={{0,12},{4,8},{8,4},{12,0},{1,13},{5,9},{9,5},{13,1},{2,14},{6,10},... | collective-permute-start | bytes 196616 | tf_op jit(solution)/shard_map/ppermute | solution.py:40
  46.5 6.2 %collective-permute-start.11 = (bf16[64,512]{1,0:T(8,128)(2,1)S(1)}, bf16[64,512]{1,0:T(8,128)(2,1)S(1)}, u32[]{:S(2)}, u32[]{:S(2)}) collective-permute-start(bf16[64,512]{1,0:T(8,128)(2,1)S(1)} %bitcast.91), channel_id=1, source_target_pairs={{0,12},{4,8},{8,4},{12,0},{1,13},{5,9},{9,5},{13,1},{2,14},{6,10},... | collective-permute-start | bytes 196616 | tf_op jit(solution)/shard_map/ppermute | solution.py:40
  54.4 1.9 %copy-start = (f32[2,512,128,8]{2,1,3,0:T(8,128)}, f32[2,512,128,8]{2,1,3,0:T(8,128)S(1)}, u32[]{:S(2)}) copy-start(f32[2,512,128,8]{2,1,3,0:T(8,128)S(1)} %get-tuple-element.37) | copy-start | bytes 12582916

commit v2 on v0

--- a/solution.py
+++ b/solution.py
@@ -1,9 +1,18 @@
+import functools
+
 import jax
 import jax.numpy as jnp
+import numpy as np
 from jax import lax
+from jax.experimental import pallas as pl
+from jax.experimental.pallas import tpu as pltpu
 from jax.sharding import PartitionSpec as P
 
 HD = 128
+LOW = -1e30
+MIB = 1 << 20
+VMEM = pl.BlockSpec(memory_space=pltpu.VMEM)
+SMEM = pl.BlockSpec(memory_space=pltpu.SMEM)
 
 
 def locate(row_ids, lengths):
@@ -35,7 +44,99 @@
     )
 
 
-def per_device(activations, queries, key_weight, value_weight, lengths, owners):
+def swap(array, axis, distance):
+    count = lax.axis_size(axis)
+    return lax.ppermute(array, axis, [(i, i ^ distance) for i in range(count)])
+
+
+def is_power(count):
+    return count & (count - 1) == 0
+
+
+def call(body, out_shape, in_specs, vmem=8 * MIB, scratch=(), out_specs=None):
+    multiple = isinstance(out_shape, (list, tuple))
+    return pl.pallas_call(
+        body,
+        out_shape=out_shape,
+        in_specs=in_specs,
+        out_specs=out_specs or ([VMEM] * len(out_shape) if multiple else VMEM),
+        scratch_shapes=list(scratch),
+        compiler_params=pltpu.CompilerParams(vmem_limit_bytes=vmem),
+    )
+
+
+def first_rows(rows, lengths_ref):
+    first = jnp.zeros_like(rows)
+    start = jnp.int32(0)
+    for p in range(lengths_ref.shape[0]):
+        first = jnp.where(rows >= start, start, first)
+        start = start + lengths_ref[p]
+    return first
+
+
+def turn(vectors, cosines, sines):
+    return vectors * cosines + pltpu.roll(vectors, HD // 2, 1) * sines
+
+
+def prepare_body(place_ref, lengths_ref, inverse_ref, queries_ref, cos_ref, sin_ref, rotated_ref):
+    local_rows, width = queries_ref.shape
+    rows = place_ref[0] * local_rows + lax.broadcasted_iota(jnp.int32, (local_rows, HD), 0)
+    positions = rows - first_rows(rows, lengths_ref)
+    angles = positions.astype(jnp.float32) * inverse_ref[...]
+    lanes = lax.broadcasted_iota(jnp.int32, (local_rows, HD), 1)
+    cosines = jnp.cos(angles)
+    sines = jnp.sin(angles)
+    sines = jnp.where(lanes < HD // 2, -sines, sines)
+    cos_ref[...] = cosines
+    sin_ref[...] = sines
+    for h in range(width // HD):
+        vectors = queries_ref[:, h * HD : (h + 1) * HD].astype(jnp.float32)
+        rotated_ref[:, h * HD : (h + 1) * HD] = turn(vectors, cosines, sines).astype(jnp.bfloat16)
+
+
+def products(pieces, offsets, place_ref, key_ref, value_ref):
+    keys = values = None
+    for ref, offset in zip(pieces, offsets):
+        width = ref.shape[1]
+        start = pl.multiple_of((place_ref[1] ^ offset) * width, width)
+        piece = ref[...]
+        key_term = jnp.dot(
+            piece, key_ref[pl.ds(start, width), :], preferred_element_type=jnp.float32
+        )
+        value_term = jnp.dot(
+            piece, value_ref[pl.ds(start, width), :], preferred_element_type=jnp.float32
+        )
+        keys = key_term if keys is None else keys + key_term
+        values = value_term if values is None else values + value_term
+    return keys, values
+
+
+def early_body(offsets, place_ref, key_ref, value_ref, *refs):
+    key_sums_ref, value_sums_ref = refs[-2:]
+    keys, values = products(refs[:-2], offsets, place_ref, key_ref, value_ref)
+    key_sums_ref[...] = keys
+    value_sums_ref[...] = values
+
+
+def late_body(
+    offsets, start, place_ref, key_ref, value_ref, key_sums_ref, value_sums_ref, cos_ref, sin_ref, *refs
+):
+    packed_ref = refs[-1]
+    size = packed_ref.shape[0]
+    rows = slice(start, start + size)
+    keys, values = products(refs[:-1], offsets, place_ref, key_ref, value_ref)
+    keys = keys + key_sums_ref[rows, :]
+    values = values + value_sums_ref[rows, :]
+    cosines = cos_ref[rows, :]
+    sines = sin_ref[rows, :]
+    for h in range(keys.shape[1] // HD):
+        part = slice(h * HD, (h + 1) * HD)
+        base = 2 * h * HD
+        packed_ref[:, base : base + HD] = turn(keys[:, part], cosines, sines).astype(jnp.bfloat16)
+        packed_ref[:, base + HD : base + 2 * HD] = values[:, part].astype(jnp.bfloat16)
+
+
+def gathered_device(activations, queries, key_weight, value_weight, lengths, owners):
     local_rows = activations.shape[0]
     devices = lax.axis_size("seq")
     own_index = lax.axis_index("seq")
@@ -64,7 +165,7 @@
         key_part = paired[:, :, :HD]
         value_part = paired[:, :, HD:]
         key_rows = offset + jnp.arange(amount, dtype=jnp.int32)
-        key_segment, unused = locate(key_rows, lengths)
+        key_segment, _ = locate(key_rows, lengths)
         allowed = (
             (key_segment[None, :] == segment[:, None])
             & (key_rows[None, :] <= row_ids[:, None])
@@ -95,7 +196,7 @@
                 return (attend_block(carried, sub_portion, offset + sub_offset), None)
 
             offsets = jnp.arange(amount // 512, dtype=jnp.int32) * 512
-            running, unused = lax.scan(
+            running, _ = lax.scan(
                 advance, running, (portion.reshape(amount // 512, 512, portion.shape[1]), offsets)
             )
             return running
@@ -126,7 +227,7 @@
     )
     taken = jnp.dot(choose, portion, preferred_element_type=jnp.float32)
     kv_cache = taken.astype(jnp.bfloat16).reshape(local_rows, kv_heads, 2 * HD)
-    running_max, running_sum, running_out = running
+    _, running_sum, running_out = running
     attention = (
         (running_out / running_sum[..., None])
         .astype(jnp.bfloat16)
@@ -135,16 +236,198 @@
     return (attention, kv_cache)
 
 
+def attend_body(starts, carried, final, place_ref, lengths_ref, owners_ref, rotated_ref, *refs):
+    local_rows, width = rotated_ref.shape
+    own = place_ref[0]
+    devices = place_ref.shape[0] - 2
+    chunks = len(starts) if final else 1
+    groups = [refs[c * devices : (c + 1) * devices] for c in range(chunks)]
+    rest = refs[chunks * devices :]
+    if carried:
+        old_max_ref, old_sum_ref, old_out_ref = rest[:3]
+        rest = rest[3:]
+    parts = groups[-1]
+    size = parts[0].shape[0]
+    amount = devices * size
+    columns = lax.broadcasted_iota(jnp.int32, (local_rows, amount), 1)
+    rows = own * local_rows + lax.broadcasted_iota(jnp.int32, (local_rows, amount), 0)
+    key_rows = columns + ((own * local_rows) + starts[-1])
+    for k in range(1, devices):
+        base = (own ^ k) * local_rows + (starts[-1] - k * size)
+        key_rows = jnp.where(columns >= k * size, columns + base, key_rows)
+    allowed = (key_rows >= first_rows(rows, lengths_ref)) & (key_rows <= rows)
+    scale = float(HD) ** -0.5
+    kv_heads = parts[0].shape[1] // (2 * HD)
+    query_heads = width // HD
+    group_size = query_heads // kv_heads
+    for j in range(kv_heads):
+        base = 2 * j * HD
+        keys = jnp.concatenate([ref[:, base : base + HD] for ref in parts], axis=0)
+        values = jnp.concatenate([ref[:, base + HD : base + 2 * HD] for ref in parts], axis=0)
+        for h in range(j * group_size, (j + 1) * group_size):
+            lanes = slice(h * HD, (h + 1) * HD)
+            scores = lax.dot_general(
+                rotated_ref[:, lanes],
+                keys,
+                (((1,), (1,)), ((), ())),
+                preferred_element_type=jnp.float32,
+            )
+            scores = jnp.where(allowed, scores, LOW)
+            largest = jnp.max(scores, axis=1, keepdims=True)
+            if carried:
+                old_max = old_max_ref[:, h : h + 1]
+                largest = jnp.maximum(largest, old_max)
+            weights = jnp.exp((scores - largest) * scale)
+            total = jnp.sum(weights, axis=1, keepdims=True)
+            out = jnp.dot(weights.astype(jnp.bfloat16), values, preferred_element_type=jnp.float32)
+            if carried:
+                factor = jnp.exp((old_max - largest) * scale)
+                total = total + old_sum_ref[:, h : h + 1] * factor
+                out = out + old_out_ref[:, lanes] * factor
+            if final:
+                rest[0][:, lanes] = (out / total).astype(jnp.bfloat16)
+            else:
+                rest[0][:, h : h + 1] = largest
+                rest[1][:, h : h + 1] = total
+                rest[2][:, lanes] = out
+    if final:
+        cache_ref, leading_ref = rest[1:]
+        total_blocks = owners_ref.shape[0]
+        blocks_dev = total_blocks // devices
+        block_len = local_rows // blocks_dev
+        count = jnp.int32(0)
+        for b in range(total_blocks):
+            hit = owners_ref[b] == own
+
+            @pl.when(hit)
+            def _(b=b, count=count):
+                leading_ref[count] = b
+
+            count = count + hit.astype(jnp.int32)
+        for r in range(blocks_dev):
+            block = leading_ref[r]
+            distance = (block // blocks_dev) ^ own
+            row = (block % blocks_dev) * block_len
+            for group, start in zip(groups, starts):
+                for k, ref in enumerate(group):
+                    inside = (distance == k) & (row >= start) & (row < start + ref.shape[0])
+
+                    @pl.when(inside)
+                    def _(ref=ref, start=start, row=row, r=r):
+                        source = pl.ds(pl.multiple_of(row - start, block_len), block_len)
+                        cache_ref[r * block_len : (r + 1) * block_len, :] = ref[source, :]
+
+
+def chunked_device(activations, queries, key_weight, value_weight, lengths, owners, sizes):
+    local_rows, _ = activations.shape
+    query_width = queries.shape[1]
+    devices = lax.axis_size("seq")
+    parts = lax.axis_size("tp")
+    kv_width = key_weight.shape[1]
+    query_heads = query_width // HD
+    place = jnp.stack(
+        [lax.axis_index("seq"), lax.axis_index("tp")] + [jnp.int32(0)] * devices
+    ).astype(jnp.int32)
+    starts = [sum(sizes[:c]) for c in range(len(sizes))]
+    far = parts // 2
+    reached = [{0: activations[at : at + size]} for at, size in zip(starts, sizes)]
+    for held in reached:
+        if far:
+            held[far] = swap(held[0], "tp", far)
+    near = {0: activations}
+    distance = far // 2
+    while distance:
+        for offset in list(near):
+            near[offset ^ distance] = swap(near[offset], "tp", distance)
+        distance //= 2
+
+    exponent = np.arange(HD // 2) * (2.0 / HD)
+    inverse = np.exp(-exponent * np.log(500000.0)).astype(np.float32)
+    inverse = jnp.asarray(np.concatenate([inverse, inverse])[None, :])
+    table = jax.ShapeDtypeStruct((local_rows, HD), jnp.float32)
+    cosines, sines, rotated = call(
+        prepare_body,
+        [table, table, jax.ShapeDtypeStruct(queries.shape, jnp.bfloat16)],
+        [SMEM, SMEM, VMEM, VMEM],
+    )(place, lengths, inverse, queries)
+    offsets = sorted(near)
+    sums = jax.ShapeDtypeStruct((local_rows, kv_width), jnp.float32)
+    key_sums, value_sums = call(
+        functools.partial(early_body, offsets), [sums, sums], [SMEM] + [VMEM] * (2 + len(offsets))
+    )(place, key_weight, value_weight, *[near[o] for o in offsets])
+
+    arrived = []
+    ready = key_sums
+    for held, start, size in zip(reached, starts, sizes):
+        late = {far: lax.optimization_barrier((held[far], ready))[0]}
+        distance = far // 2
+        while distance:
+            for offset in list(late):
+                late[offset ^ distance] = swap(late[offset], "tp", distance)
+            distance //= 2
+        offsets = sorted(late)
+        packed = call(
+            functools.partial(late_body, offsets, start),
+            jax.ShapeDtypeStruct((size, 2 * kv_width), jnp.bfloat16),
+            [SMEM] + [VMEM] * (6 + len(offsets)),
+        )(
+            place,
+            key_weight,
+            value_weight,
+            key_sums,
+            value_sums,
+            cosines,
+            sines,
+            *[late[o] for o in offsets],
+        )
+        ready = packed
+        arrived.append([packed] + [swap(packed, "seq", k) for k in range(1, devices)])
+
+    state = ()
+    for c in range(len(sizes)):
+        final = c == len(sizes) - 1
+        groups = arrived if final else arrived[c : c + 1]
+        taken = [part for group in groups for part in group]
+        if final:
+            results = [
+                jax.ShapeDtypeStruct(queries.shape, jnp.bfloat16),
+                jax.ShapeDtypeStruct((local_rows, 2 * kv_width), jnp.bfloat16),
+            ]
+        else:
+            column = jax.ShapeDtypeStruct((local_rows, query_heads), jnp.float32)
+            results = [column, column, jax.ShapeDtypeStruct(queries.shape, jnp.float32)]
+        state = call(
+            functools.partial(attend_body, tuple(starts[: c + 1]), c > 0, final),
+            results,
+            [SMEM] * 3 + [VMEM] * (1 + len(taken) + len(state)),
+            scratch=[pltpu.SMEM((owners.shape[0] // devices,), jnp.int32)] if final else (),
+        )(place, lengths, owners, rotated, *taken, *state)
+    attention, cache = state
+    return attention, cache.reshape(local_rows, kv_width // HD, 2 * HD)
+
+
+def per_device(activations, queries, key_weight, value_weight, lengths, owners):
+    local_rows = activations.shape[0]
+    devices = lax.axis_size("seq")
+    parts = lax.axis_size("tp")
+    block_len = local_rows * devices // owners.shape[0]
+    blocks_dev = owners.shape[0] // devices
+    few = devices <= 8 and 1 < parts <= 8 and is_power(devices) and is_power(parts)
+    if not few or block_len % 16 or blocks_dev < 2:
+        return gathered_device(activations, queries, key_weight, value_weight, lengths, owners)
+    first = (blocks_dev // 2) * block_len
+    sizes = [first, local_rows - first]
+    return chunked_device(activations, queries, key_weight, value_weight, lengths, owners, sizes)
+
+
 def solution(mesh):
-    in_specs = (
-        P(("groups", "seq"), "tp"),
-        P(("groups", "seq"), "tp"),
-        P(None, "tp"),
-        P(None, "tp"),
-        P("groups"),
-        P("groups"),
-    )
-    out_specs = (P(("groups", "seq"), "tp"), P(("groups", "seq"), "tp", None))
+    rows = P(("groups", "seq"), "tp")
+    columns = P(None, "tp")
+
     return jax.shard_map(
-        per_device, mesh=mesh, in_specs=in_specs, out_specs=out_specs, check_vma=False
-    )
+        per_device,
+        mesh=mesh,
+        in_specs=(rows, rows, columns, columns, P("groups"), P("groups")),
+        out_specs=(rows, P(("groups", "seq"), "tp", None)),
+        check_vma=False,
+    )

time: 71.9 us -> 44.1 us (0.61)
  waiting for transfers between devices: 23.8 us -> 7.98 us
  blocking collectives: 15.3 us -> 0 us
  Pallas kernels: 0 us -> 14 us
  starting transfers between devices: 0.04 us -> 13.8 us
  between operations: 14.2 us -> 0.71 us
  matrix products: 9.66 us -> 0 us
  other arithmetic: 5.07 us -> 0.08 us
  local copies, waits for them, and re-layouts: 3.61 us -> 7.19 us
    all_gather x1 -> x0, waiting for transfers between devices: 23.1 us -> none  [per_device(): portion = lax.all_gather(activations, 'tp', axis=1, tiled=True)]
    all_gather x1 -> x0, blocking collectives: 15.3 us -> none  [per_device(): portion = lax.all_gather(packed, 'seq', axis=0, tiled=True)]
    pallas_call x0 -> x6, Pallas kernels: none -> 14 us  [the longest x2 8.78 us: chunked_device(): call(functools.partial(attend_body, tuple(starts[:c + 1]), c > 0, final),...]
    ppermute x0 -> x11, starting transfers between devices: none -> 13.8 us  [swap(): return lax.ppermute(array, axis, [(i, i ^ distance) for i in range(count)])]
    dot_general x5 -> x0, matrix products: 9.66 us -> none  [the longest x1 4.34 us: per_device(): key_sums = jnp.dot(portion, key_rows, preferred_element_type=jnp.float32)]
    ppermute x0 -> x11, waiting for transfers between devices: none -> 7.98 us  [swap(): return lax.ppermute(array, axis, [(i, i ^ distance) for i in range(count)])]
    unnamed x10 -> x16, local copies, waits for them, and re-layouts: 1.21 us -> 5.44 us
    another operation x7 -> x1, other arithmetic: 1.79 us -> 0.08 us  [chunked_device(): jnp.stack([lax.axis_index('seq'), lax.axis_index('tp')] + [jnp.int32(0)]...]
  transfers between devices with their start and end apart: 1 -> 11, of which waited for: 1 -> 5; matrix products, arithmetic and copies ran while one was open for 5% -> 3% of each run, Pallas kernels for 0% -> 16%
where the time goes in v2:
time: 44.1 us; the launch traced here: 43.8 us
  Pallas kernels  14 us (32%)
  starting transfers between devices  13.8 us (31%)
  waiting for transfers between devices  7.98 us (18%)
  local copies, waits for them, and re-layouts  7.19 us (16%)
  between operations  0.71 us (2%)
    ppermute x11, starting transfers between devices, swap(): return lax.ppermute(array, axis, [(i, i ^ distance) for i in range(count)])  13.8 us
    pallas_call x2, Pallas kernels, chunked_device(): call(functools.partial(attend_body, tuple(starts[:c + 1]), c > 0, final),...  8.78 us
    ppermute x11, waiting for transfers between devices, swap(): return lax.ppermute(array, axis, [(i, i ^ distance) for i in range(count)])  7.98 us
    unnamed x16, local copies, waits for them, and re-layouts  5.44 us
    pallas_call x2, Pallas kernels, chunked_device(): call(functools.partial(late_body, offsets, start), jax.ShapeDtypeStruct((...  2.92 us
    pallas_call x1, Pallas kernels, chunked_device(): call(functools.partial(early_body, offsets), [sums, sums], [SMEM] + [VMEM...  1.27 us
    pallas_call x1, Pallas kernels, chunked_device(): call(prepare_body, [table, table, jax.ShapeDtypeStruct(queries.shape, jnp...  1.08 us
    slice x1, local copies, waits for them, and re-layouts, chunked_device(): activations[at:at + size]  1.06 us
  transfers between devices with their start and end apart: 11, of which 5 were waited for; matrix products, arithmetic and copies ran while one was open for 3% of the time, Pallas kernels for 16%

profile of v2, /device:TPU:0, one launch (start us, length us, event | category | flops | bytes accessed | tf_op | source)
XLA Modules:
  0.0 43.8 jit_solution(8051157083604405125)
XLA Ops:
  0.6 0.6 %collective-permute-start = (bf16[128,2048]{1,0:T(8,128)(2,1)}, bf16[128,2048]{1,0:T(8,128)(2,1)S(1)}, u32[]{:S(2)}, u32[]{:S(2)}) collective-permute-start(bf16[128,2048]{1,0:T(8,128)(2,1)} %refs_0_.1), channel_id=1, source_target_pairs={{0,1},{1,0},{2,3},{3,2},{4,5},{5,4},{6,7},{7,6},{8,9},{9,8},{10,11... | collective-permute-start | bytes 1572872 | tf_op jit(solution)/shard_map/ppermute | solution.py:49
  1.2 1.1 %fusion = (bf16[64,2048]{1,0:T(8,128)(2,1)S(1)}, bf16[64,2048]{1,0:T(8,128)(2,1)S(1)}) fusion(bf16[128,2048]{1,0:T(8,128)(2,1)} %refs_0_.1), kind=kLoop, calls=%fused_computation.1 | loop fusion | bytes 1048576 | tf_op jit(solution)/shard_map/slice | solution.py:333
  2.3 2.6 %collective-permute-start.1 = (bf16[64,2048]{1,0:T(8,128)(2,1)S(1)}, bf16[64,2048]{1,0:T(8,128)(2,1)S(1)}, u32[]{:S(2)}, u32[]{:S(2)}) collective-permute-start(bf16[64,2048]{1,0:T(8,128)(2,1)S(1)} %get-tuple-element.27), channel_id=1, source_target_pairs={{0,2},{1,3},{2,0},{3,1},{4,6},{5,7},{6,4},{7,5},{8,10},{9,11},{10,... | collective-permute-start | bytes 786440 | tf_op jit(solution)/shard_map/ppermute | solution.py:49
  4.8 0.1 pad_add_fusion.place_ref
  4.9 0.0 collective-permute-done.refs_1_
  4.9 0.0 copy-start
  4.9 2.2 %copy-done = bf16[8192,256]{1,0:T(8,128)(2,1)S(1)} copy-done((bf16[8192,256]{1,0:T(8,128)(2,1)S(1)}, bf16[8192,256]{1,0:T(8,128)(2,1)}, u32[]{:S(2)}) %copy-start) | copy-done | bytes 4194328
  7.1 0.0 copy-start.2
  7.1 2.2 %copy-done.2 = bf16[8192,256]{1,0:T(8,128)(2,1)S(1)} copy-done((bf16[8192,256]{1,0:T(8,128)(2,1)S(1)}, bf16[8192,256]{1,0:T(8,128)(2,1)}, u32[]{:S(2)}) %copy-start.2) | copy-done | bytes 4194328
  9.3 0.0 copy-start.3
  9.3 1.0 %copy-done.3 = bf16[128,2048]{1,0:T(8,128)(2,1)S(1)} copy-done((bf16[128,2048]{1,0:T(8,128)(2,1)S(1)}, bf16[128,2048]{1,0:T(8,128)(2,1)}, u32[]{:S(2)}) %copy-start.3) | copy-done | bytes 524312
  10.3 0.0 copy-start.4
  10.3 0.0 copy-start.5
  10.3 0.0 copy-start.7
  10.3 0.0 copy-start.1
  10.3 1.3 %shard_map.87 = (f32[128,256]{1,0:T(8,128)S(1)}, f32[128,256]{1,0:T(8,128)S(1)}) custom-call(s32[6]{0:T(128)S(1)} %pad_add_fusion.place_ref, bf16[8192,256]{1,0:T(8,128)(2,1)S(1)} %copy-done, bf16[8192,256]{1,0:T(8,128)(2,1)S(1)} %copy-done.2, bf16[128,2048]{1,0:T(8,128)(2,1)S(1)} %copy-done.3, bf16[128,2048]{1,0:T(8,128)(2,1)S(1)} %collective-permute-done.refs_1_), custom_call_target="tpu_custom_call" | custom-call | tf_op jit(solution)/shard_map/pallas_call | solution.py:355
  11.6 0.2 collective-permute-done.1.refs_0_
  11.8 0.1 collective-permute-start.2
  11.9 1.6 %collective-permute-start.6 = (bf16[64,2048]{1,0:T(8,128)(2,1)S(1)}, bf16[64,2048]{1,0:T(8,128)(2,1)S(1)}, u32[]{:S(2)}, u32[]{:S(2)}) collective-permute-start(bf16[64,2048]{1,0:T(8,128)(2,1)S(1)} %get-tuple-element.26), channel_id=1, source_target_pairs={{0,2},{1,3},{2,0},{3,1},{4,6},{5,7},{6,4},{7,5},{8,10},{9,11},{10,... | collective-permute-start | bytes 786440 | tf_op jit(solution)/shard_map/ppermute | solution.py:49
  13.5 0.0 copy-done.4
  13.5 0.0 copy-done.5
  13.5 0.0 copy-done.7
  13.5 1.1 %shard_map.86 = (f32[128,128]{1,0:T(8,128)S(1)}, f32[128,128]{1,0:T(8,128)S(1)}, bf16[128,2048]{1,0:T(8,128)(2,1)S(1)}) custom-call(s32[6]{0:T(128)S(1)} %pad_add_fusion.place_ref, s32[4]{0:T(128)S(1)} %copy-done.5, f32[1,128]{1,0:T(1,128)S(1)} %copy-done.7, bf16[128,2048]{1,0:T(8,128)(2,1)S(1)} %copy-done.4), custom_call_target="tpu_custom_call" | custom-call | tf_op jit(solution)/shard_map/pallas_call | solution.py:348
  14.6 0.0 collective-permute-done.2.refs_1_
  14.6 0.0 copy-done.1
  14.6 1.5 %shard_map.88.refs_0_ = bf16[64,512]{1,0:T(8,128)(2,1)S(1)} custom-call(s32[6]{0:T(128)S(1)} %pad_add_fusion.place_ref, bf16[8192,256]{1,0:T(8,128)(2,1)S(1)} %copy-done.1, bf16[8192,256]{1,0:T(8,128)(2,1)S(1)} %copy-done.2, f32[128,256]{1,0:T(8,128)S(1)} %get-tuple-element.15.key_sums_ref, f32[128,256]{1,0:T(8,128)S(1)} %get-tuple-element.16.value_sums_ref, ...), custom_call_target="tpu_custom_call" | custom-call | tf_op jit(solution)/shard_map/pallas_call | solution.py:369
  16.1 0.0 copy-start.6
  16.1 4.4 %collective-permute-done.6.refs_0_ = bf16[64,2048]{1,0:T(8,128)(2,1)S(1)} collective-permute-done((bf16[64,2048]{1,0:T(8,128)(2,1)S(1)}, bf16[64,2048]{1,0:T(8,128)(2,1)S(1)}, u32[]{:S(2)}, u32[]{:S(2)}) %collective-permute-start.6) | collective-permute-done | bytes 262176 | tf_op jit(solution)/shard_map/ppermute | solution.py:49
  20.5 0.0 collective-permute-start.7
  20.5 3.9 %collective-permute-start.5 = (bf16[64,512]{1,0:T(8,128)(2,1)S(1)}, bf16[64,512]{1,0:T(8,128)(2,1)S(1)}, u32[]{:S(2)}, u32[]{:S(2)}) collective-permute-start(bf16[64,512]{1,0:T(8,128)(2,1)S(1)} %shard_map.88.refs_0_), channel_id=1, source_target_pairs={{0,12},{4,8},{8,4},{12,0},{1,13},{5,9},{9,5},{13,1},{2,14},{6,10},... | collective-permute-start | bytes 196616 | tf_op jit(solution)/shard_map/ppermute | solution.py:49
  24.4 0.0 collective-permute-start.4
  24.4 0.6 %collective-permute-start.3 = (bf16[64,512]{1,0:T(8,128)(2,1)S(1)}, bf16[64,512]{1,0:T(8,128)(2,1)S(1)}, u32[]{:S(2)}, u32[]{:S(2)}) collective-permute-start(bf16[64,512]{1,0:T(8,128)(2,1)S(1)} %shard_map.88.refs_0_), channel_id=1, source_target_pairs={{0,4},{4,0},{8,12},{12,8},{1,5},{5,1},{9,13},{13,9},{2,6},{6,2},{1... | collective-permute-start | bytes 196616 | tf_op jit(solution)/shard_map/ppermute | solution.py:49
  24.9 0.0 collective-permute-done.7.refs_1_
  24.9 1.5 %shard_map.89.refs_4_ = bf16[64,512]{1,0:T(8,128)(2,1)S(1)} custom-call(s32[6]{0:T(128)S(1)} %pad_add_fusion.place_ref, bf16[8192,256]{1,0:T(8,128)(2,1)S(1)} %copy-done.1, bf16[8192,256]{1,0:T(8,128)(2,1)S(1)} %copy-done.2, f32[128,256]{1,0:T(8,128)S(1)} %get-tuple-element.15.key_sums_ref, f32[128,256]{1,0:T(8,128)S(1)} %get-tuple-element.16.value_sums_ref, ...), custom_call_target="tpu_custom_call" | custom-call | tf_op jit(solution)/shard_map/pallas_call | solution.py:369
  26.4 3.9 %collective-permute-start.10 = (bf16[64,512]{1,0:T(8,128)(2,1)S(1)}, bf16[64,512]{1,0:T(8,128)(2,1)S(1)}, u32[]{:S(2)}, u32[]{:S(2)}) collective-permute-start(bf16[64,512]{1,0:T(8,128)(2,1)S(1)} %shard_map.89.refs_4_), channel_id=1, source_target_pairs={{0,12},{4,8},{8,4},{12,0},{1,13},{5,9},{9,5},{13,1},{2,14},{6,10},... | collective-permute-start | bytes 196616 | tf_op jit(solution)/shard_map/ppermute | solution.py:49
  30.3 0.0 collective-permute-start.9
  30.3 0.0 collective-permute-done.5.refs_3_
  30.3 0.6 %collective-permute-start.8 = (bf16[64,512]{1,0:T(8,128)(2,1)S(1)}, bf16[64,512]{1,0:T(8,128)(2,1)S(1)}, u32[]{:S(2)}, u32[]{:S(2)}) collective-permute-start(bf16[64,512]{1,0:T(8,128)(2,1)S(1)} %shard_map.89.refs_4_), channel_id=1, source_target_pairs={{0,4},{4,0},{8,12},{12,8},{1,5},{5,1},{9,13},{13,9},{2,6},{6,2},{1... | collective-permute-start | bytes 196616 | tf_op jit(solution)/shard_map/ppermute | solution.py:49
  30.9 0.1 collective-permute-done.4.refs_2_
  31.1 0.0 collective-permute-done.3.refs_1_
  31.1 0.0 copy-done.6
  31.1 1.8 %shard_map.90 = (f32[128,16]{1,0:T(8,128)S(1)}, f32[128,16]{1,0:T(8,128)S(1)}, f32[128,2048]{1,0:T(8,128)S(1)}) custom-call(s32[6]{0:T(128)S(1)} %pad_add_fusion.place_ref, s32[4]{0:T(128)S(1)} %copy-done.5, s32[16]{0:T(128)S(1)} %copy-done.6, bf16[128,2048]{1,0:T(8,128)(2,1)S(1)} %get-tuple-element.14.rotated_ref, bf16[64,512]{1,0:T(8,128)(2,1)S(1)} %shard_map.88.refs_0_, ...), custom_call_target="tpu_custom_call" | custom-call | tf_op jit(solution)/shard_map/pallas_call | solution.py:399
  32.8 0.2 collective-permute-done.10.refs_7_
  33.1 3.0 %collective-permute-done.9.refs_6_ = bf16[64,512]{1,0:T(8,128)(2,1)S(1)} collective-permute-done((bf16[64,512]{1,0:T(8,128)(2,1)S(1)}, bf16[64,512]{1,0:T(8,128)(2,1)S(1)}, u32[]{:S(2)}, u32[]{:S(2)}) %collective-permute-start.9) | collective-permute-done | bytes 65568 | tf_op jit(solution)/shard_map/ppermute | solution.py:49
  36.1 0.0 collective-permute-done.8.refs_5_
  36.1 7.0 %shard_map.91 = (bf16[128,2048]{1,0:T(8,128)(2,1)}, bf16[128,512]{1,0:T(8,128)(2,1)S(1)}) custom-call(s32[6]{0:T(128)S(1)} %pad_add_fusion.place_ref, s32[4]{0:T(128)S(1)} %copy-done.5, s32[16]{0:T(128)S(1)} %copy-done.6, bf16[128,2048]{1,0:T(8,128)(2,1)S(1)} %get-tuple-element.14.rotated_ref, bf16[64,512]{1,0:T(8,128)(2,1)S(1)} %shard_map.88.refs_0_, ...), custom_call_target="tpu_custom_call" | custom-call | tf_op jit(solution)/shard_map/pallas_call | solution.py:399
  43.1 0.7 %reshape.7 = bf16[128,2,256]{2,1,0:T(2,128)(2,1)} reshape(bf16[128,512]{1,0:T(8,128)(2,1)S(1)} %get-tuple-element.25) | data formatting | bytes 262144 | tf_op jit(solution)/shard_map/reshape | solution.py:406
  (1 shorter events, 0.0 us)
Async XLA Ops:
  0.6 4.3 %collective-permute-start = (bf16[128,2048]{1,0:T(8,128)(2,1)}, bf16[128,2048]{1,0:T(8,128)(2,1)S(1)}, u32[]{:S(2)}, u32[]{:S(2)}) collective-permute-start(bf16[128,2048]{1,0:T(8,128)(2,1)} %refs_0_.1), channel_id=1, source_target_pairs={{0,1},{1,0},{2,3},{3,2},{4,5},{5,4},{6,7},{7,6},{8,9},{9,8},{10,11... | collective-permute-start | bytes 1572872 | tf_op jit(solution)/shard_map/ppermute | solution.py:49
  2.3 9.5 %collective-permute-start.1 = (bf16[64,2048]{1,0:T(8,128)(2,1)S(1)}, bf16[64,2048]{1,0:T(8,128)(2,1)S(1)}, u32[]{:S(2)}, u32[]{:S(2)}) collective-permute-start(bf16[64,2048]{1,0:T(8,128)(2,1)S(1)} %get-tuple-element.27), channel_id=1, source_target_pairs={{0,2},{1,3},{2,0},{3,1},{4,6},{5,7},{6,4},{7,5},{8,10},{9,11},{10,... | collective-permute-start | bytes 786440 | tf_op jit(solution)/shard_map/ppermute | solution.py:49
  4.9 2.2 %copy-start = (bf16[8192,256]{1,0:T(8,128)(2,1)S(1)}, bf16[8192,256]{1,0:T(8,128)(2,1)}, u32[]{:S(2)}) copy-start(bf16[8192,256]{1,0:T(8,128)(2,1)} %key_ref.5) | copy-start | bytes 12582916
  7.1 2.2 %copy-start.2 = (bf16[8192,256]{1,0:T(8,128)(2,1)S(1)}, bf16[8192,256]{1,0:T(8,128)(2,1)}, u32[]{:S(2)}) copy-start(bf16[8192,256]{1,0:T(8,128)(2,1)} %value_ref.5) | copy-start | bytes 12582916
  9.3 1.0 %copy-start.3 = (bf16[128,2048]{1,0:T(8,128)(2,1)S(1)}, bf16[128,2048]{1,0:T(8,128)(2,1)}, u32[]{:S(2)}) copy-start(bf16[128,2048]{1,0:T(8,128)(2,1)} %refs_0_.1) | copy-start | bytes 1572868
  10.3 3.2 %copy-start.4 = (bf16[128,2048]{1,0:T(8,128)(2,1)S(1)}, bf16[128,2048]{1,0:T(8,128)(2,1)}, u32[]{:S(2)}) copy-start(bf16[128,2048]{1,0:T(8,128)(2,1)} %queries_ref.1) | copy-start | bytes 1572868
  10.3 3.2 %copy-start.5 = (s32[4]{0:T(128)S(1)}, s32[4]{0:T(128)}, u32[]{:S(2)}) copy-start(s32[4]{0:T(128)} %lengths_ref.5) | copy-start | bytes 52
  10.3 3.2 %copy-start.7 = (f32[1,128]{1,0:T(1,128)S(1)}, f32[1,128]{1,0:T(1,128)}, u32[]{:S(2)}) copy-start(f32[1,128]{1,0:T(1,128)} %constant.11.clone.inverse_ref) | copy-start | bytes 1540
  10.3 4.3 %copy-start.1 = (bf16[8192,256]{1,0:T(8,128)(2,1)S(1)}, bf16[8192,256]{1,0:T(8,128)(2,1)}, u32[]{:S(2)}) copy-start(bf16[8192,256]{1,0:T(8,128)(2,1)} %key_ref.5) | copy-start | bytes 12582916
  11.8 2.8 %collective-permute-start.2 = (bf16[64,2048]{1,0:T(8,128)(2,1)S(1)}, bf16[64,2048]{1,0:T(8,128)(2,1)S(1)}, u32[]{:S(2)}, u32[]{:S(2)}) collective-permute-start(bf16[64,2048]{1,0:T(8,128)(2,1)S(1)} %collective-permute-done.1.refs_0_), channel_id=1, source_target_pairs={{0,1},{1,0},{2,3},{3,2},{4,5},{5,4},{6,7},{7,6},{8,9},{9,8},{10,11... | collective-permute-start | bytes 786440 | tf_op jit(solution)/shard_map/ppermute | solution.py:49
  11.9 8.6 %collective-permute-start.6 = (bf16[64,2048]{1,0:T(8,128)(2,1)S(1)}, bf16[64,2048]{1,0:T(8,128)(2,1)S(1)}, u32[]{:S(2)}, u32[]{:S(2)}) collective-permute-start(bf16[64,2048]{1,0:T(8,128)(2,1)S(1)} %get-tuple-element.26), channel_id=1, source_target_pairs={{0,2},{1,3},{2,0},{3,1},{4,6},{5,7},{6,4},{7,5},{8,10},{9,11},{10,... | collective-permute-start | bytes 786440 | tf_op jit(solution)/shard_map/ppermute | solution.py:49
  16.1 15.0 %copy-start.6 = (s32[16]{0:T(128)S(1)}, s32[16]{0:T(128)}, u32[]{:S(2)}) copy-start(s32[16]{0:T(128)} %owners_ref.3) | copy-start | bytes 196
  20.5 4.4 %collective-permute-start.7 = (bf16[64,2048]{1,0:T(8,128)(2,1)S(1)}, bf16[64,2048]{1,0:T(8,128)(2,1)S(1)}, u32[]{:S(2)}, u32[]{:S(2)}) collective-permute-start(bf16[64,2048]{1,0:T(8,128)(2,1)S(1)} %collective-permute-done.6.refs_0_), channel_id=1, source_target_pairs={{0,1},{1,0},{2,3},{3,2},{4,5},{5,4},{6,7},{7,6},{8,9},{9,8},{10,11... | collective-permute-start | bytes 786440 | tf_op jit(solution)/shard_map/ppermute | solution.py:49
  20.5 9.8 %collective-permute-start.5 = (bf16[64,512]{1,0:T(8,128)(2,1)S(1)}, bf16[64,512]{1,0:T(8,128)(2,1)S(1)}, u32[]{:S(2)}, u32[]{:S(2)}) collective-permute-start(bf16[64,512]{1,0:T(8,128)(2,1)S(1)} %shard_map.88.refs_0_), channel_id=1, source_target_pairs={{0,12},{4,8},{8,4},{12,0},{1,13},{5,9},{9,5},{13,1},{2,14},{6,10},... | collective-permute-start | bytes 196616 | tf_op jit(solution)/shard_map/ppermute | solution.py:49
  24.4 6.7 %collective-permute-start.4 = (bf16[64,512]{1,0:T(8,128)(2,1)S(1)}, bf16[64,512]{1,0:T(8,128)(2,1)S(1)}, u32[]{:S(2)}, u32[]{:S(2)}) collective-permute-start(bf16[64,512]{1,0:T(8,128)(2,1)S(1)} %shard_map.88.refs_0_), channel_id=1, source_target_pairs={{0,8},{4,12},{8,0},{12,4},{1,9},{5,13},{9,1},{13,5},{2,10},{6,14},... | collective-permute-start | bytes 196616 | tf_op jit(solution)/shard_map/ppermute | solution.py:49
  24.4 6.7 %collective-permute-start.3 = (bf16[64,512]{1,0:T(8,128)(2,1)S(1)}, bf16[64,512]{1,0:T(8,128)(2,1)S(1)}, u32[]{:S(2)}, u32[]{:S(2)}) collective-permute-start(bf16[64,512]{1,0:T(8,128)(2,1)S(1)} %shard_map.88.refs_0_), channel_id=1, source_target_pairs={{0,4},{4,0},{8,12},{12,8},{1,5},{5,1},{9,13},{13,9},{2,6},{6,2},{1... | collective-permute-start | bytes 196616 | tf_op jit(solution)/shard_map/ppermute | solution.py:49
  26.4 6.7 %collective-permute-start.10 = (bf16[64,512]{1,0:T(8,128)(2,1)S(1)}, bf16[64,512]{1,0:T(8,128)(2,1)S(1)}, u32[]{:S(2)}, u32[]{:S(2)}) collective-permute-start(bf16[64,512]{1,0:T(8,128)(2,1)S(1)} %shard_map.89.refs_4_), channel_id=1, source_target_pairs={{0,12},{4,8},{8,4},{12,0},{1,13},{5,9},{9,5},{13,1},{2,14},{6,10},... | collective-permute-start | bytes 196616 | tf_op jit(solution)/shard_map/ppermute | solution.py:49
  30.3 5.8 %collective-permute-start.9 = (bf16[64,512]{1,0:T(8,128)(2,1)S(1)}, bf16[64,512]{1,0:T(8,128)(2,1)S(1)}, u32[]{:S(2)}, u32[]{:S(2)}) collective-permute-start(bf16[64,512]{1,0:T(8,128)(2,1)S(1)} %shard_map.89.refs_4_), channel_id=1, source_target_pairs={{0,8},{4,12},{8,0},{12,4},{1,9},{5,13},{9,1},{13,5},{2,10},{6,14},... | collective-permute-start | bytes 196616 | tf_op jit(solution)/shard_map/ppermute | solution.py:49
  30.3 5.8 %collective-permute-start.8 = (bf16[64,512]{1,0:T(8,128)(2,1)S(1)}, bf16[64,512]{1,0:T(8,128)(2,1)S(1)}, u32[]{:S(2)}, u32[]{:S(2)}) collective-permute-start(bf16[64,512]{1,0:T(8,128)(2,1)S(1)} %shard_map.89.refs_4_), channel_id=1, source_target_pairs={{0,4},{4,0},{8,12},{12,8},{1,5},{5,1},{9,13},{13,9},{2,6},{6,2},{1... | collective-permute-start | bytes 196616 | tf_op jit(solution)/shard_map/ppermute | solution.py:49

commit v3 on v0

--- a/solution.py
+++ b/solution.py
@@ -1,9 +1,20 @@
+import functools
+
 import jax
 import jax.numpy as jnp
+import numpy as np
 from jax import lax
+from jax.experimental import pallas as pl
+from jax.experimental.pallas import tpu as pltpu
 from jax.sharding import PartitionSpec as P
 
 HD = 128
+LOW = -1e30
+TOGETHER = 8
+MIB = 1 << 20
+VMEM = pl.BlockSpec(memory_space=pltpu.VMEM)
+SMEM = pl.BlockSpec(memory_space=pltpu.SMEM)
+ANY = pl.BlockSpec(memory_space=pltpu.HBM)
 
 
 def locate(row_ids, lengths):
@@ -35,7 +46,57 @@
     )
 
 
-def per_device(activations, queries, key_weight, value_weight, lengths, owners):
+def swap(array, axis, distance):
+    count = lax.axis_size(axis)
+    return lax.ppermute(array, axis, [(i, i ^ distance) for i in range(count)])
+
+
+def is_power(count):
+    return count & (count - 1) == 0
+
+
+def call(body, out_shape, in_specs, vmem=8 * MIB, scratch=(), out_specs=None):
+    multiple = isinstance(out_shape, (list, tuple))
+    return pl.pallas_call(
+        body,
+        out_shape=out_shape,
+        in_specs=in_specs,
+        out_specs=out_specs or ([VMEM] * len(out_shape) if multiple else VMEM),
+        scratch_shapes=list(scratch),
+        compiler_params=pltpu.CompilerParams(vmem_limit_bytes=vmem),
+    )
+
+
+def first_rows(rows, lengths_ref):
+    first = jnp.zeros_like(rows)
+    start = jnp.int32(0)
+    for p in range(lengths_ref.shape[0]):
+        first = jnp.where(rows >= start, start, first)
+        start = start + lengths_ref[p]
+    return first
+
+
+def turn(vectors, cosines, sines):
+    return vectors * cosines + pltpu.roll(vectors, HD // 2, 1) * sines
+
+
+def prepare_body(place_ref, lengths_ref, inverse_ref, queries_ref, cos_ref, sin_ref, rotated_ref):
+    local_rows, width = queries_ref.shape
+    rows = place_ref[0] * local_rows + lax.broadcasted_iota(jnp.int32, (local_rows, HD), 0)
+    positions = rows - first_rows(rows, lengths_ref)
+    angles = positions.astype(jnp.float32) * inverse_ref[...]
+    lanes = lax.broadcasted_iota(jnp.int32, (local_rows, HD), 1)
+    cosines = jnp.cos(angles)
+    sines = jnp.sin(angles)
+    sines = jnp.where(lanes < HD // 2, -sines, sines)
+    cos_ref[...] = cosines
+    sin_ref[...] = sines
+    for h in range(width // HD):
+        vectors = queries_ref[:, h * HD : (h + 1) * HD].astype(jnp.float32)
+        rotated_ref[:, h * HD : (h + 1) * HD] = turn(vectors, cosines, sines).astype(jnp.bfloat16)
+
+
+def gathered_device(activations, queries, key_weight, value_weight, lengths, owners):
     local_rows = activations.shape[0]
     devices = lax.axis_size("seq")
     own_index = lax.axis_index("seq")
@@ -64,7 +125,7 @@
         key_part = paired[:, :, :HD]
         value_part = paired[:, :, HD:]
         key_rows = offset + jnp.arange(amount, dtype=jnp.int32)
-        key_segment, unused = locate(key_rows, lengths)
+        key_segment, _ = locate(key_rows, lengths)
         allowed = (
             (key_segment[None, :] == segment[:, None])
             & (key_rows[None, :] <= row_ids[:, None])
@@ -95,7 +156,7 @@
                 return (attend_block(carried, sub_portion, offset + sub_offset), None)
 
             offsets = jnp.arange(amount // 512, dtype=jnp.int32) * 512
-            running, unused = lax.scan(
+            running, _ = lax.scan(
                 advance, running, (portion.reshape(amount // 512, 512, portion.shape[1]), offsets)
             )
             return running
@@ -126,7 +187,7 @@
     )
     taken = jnp.dot(choose, portion, preferred_element_type=jnp.float32)
     kv_cache = taken.astype(jnp.bfloat16).reshape(local_rows, kv_heads, 2 * HD)
-    running_max, running_sum, running_out = running
+    _, running_sum, running_out = running
     attention = (
         (running_out / running_sum[..., None])
         .astype(jnp.bfloat16)
@@ -135,16 +196,298 @@
     return (attention, kv_cache)
 
 
+def add_products(piece, key_ref, value_ref, sums):
+    kv_width = key_ref.shape[1]
+    for at, ref in ((0, key_ref), (kv_width, value_ref)):
+        sums[at] = sums[at] + jnp.dot(piece, ref[...], preferred_element_type=jnp.float32)
+
+
+def early_body(offsets, place_ref, key_hbm, value_hbm, own_hbm, *refs):
+    near_refs = refs[: len(offsets) - 1]
+    keys_ref, values_ref, sums_ref, own_ref, weight_sems, own_sem = refs[len(offsets) - 1 :]
+    parts, width, kv_width = keys_ref.shape
+    copies = []
+    own_copy = pltpu.make_async_copy(own_hbm, own_ref, own_sem)
+    order = list(offsets) + [o for o in range(parts) if o not in offsets]
+    for n, offset in enumerate(order):
+        start = pl.multiple_of((place_ref[1] ^ offset) * width, width)
+        pair = [
+            pltpu.make_async_copy(hbm.at[pl.ds(start, width)], ref.at[offset], weight_sems.at[side, offset])
+            for side, (hbm, ref) in enumerate(((key_hbm, keys_ref), (value_hbm, values_ref)))
+        ]
+        for copy in pair:
+            copy.start()
+        copies.append(pair)
+        if n == 0:
+            own_copy.start()
+    own_copy.wait()
+    sums = {0: 0.0, kv_width: 0.0}
+    pieces = [own_ref] + list(near_refs)
+    for n, offset in enumerate(order):
+        for copy in copies[n]:
+            copy.wait()
+        if n < len(offsets):
+            add_products(pieces[n][...], keys_ref.at[offset], values_ref.at[offset], sums)
+    for at in sums:
+        sums_ref[:, at : at + kv_width] = sums[at]
+
+
+def far_body(offset, start, keys_ref, values_ref, sums_ref, piece_ref, out_ref):
+    size = piece_ref.shape[0]
+    kv_width = keys_ref.shape[2]
+    rows = slice(start, start + size)
+    sums = {at: sums_ref[rows, at : at + kv_width] for at in (0, kv_width)}
+    add_products(piece_ref[...], keys_ref.at[offset], values_ref.at[offset], sums)
+    for at in sums:
+        out_ref[:, at : at + kv_width] = sums[at]
+
+
+def late_body(offsets, start, keys_ref, values_ref, sums_ref, cos_ref, sin_ref, *refs):
+    packed_ref = refs[-1]
+    size = packed_ref.shape[0]
+    kv_width = keys_ref.shape[2]
+    rows = slice(start, start + size)
+    sums = {at: sums_ref[:, at : at + kv_width] for at in (0, kv_width)}
+    for offset, ref in zip(offsets, refs):
+        add_products(ref[...], keys_ref.at[offset], values_ref.at[offset], sums)
+    cosines = cos_ref[rows, :]
+    sines = sin_ref[rows, :]
+    for h in range(kv_width // HD):
+        part = slice(h * HD, (h + 1) * HD)
+        base = 2 * h * HD
+        packed_ref[:, base : base + HD] = turn(sums[0][:, part], cosines, sines).astype(jnp.bfloat16)
+        packed_ref[:, base + HD : base + 2 * HD] = sums[kv_width][:, part].astype(jnp.bfloat16)
+
+
+def widen(column, amount):
+    count = -(-amount // HD)
+    wide = jnp.concatenate([column] * count, axis=1) if count > 1 else column
+    return wide[:, :amount]
+
+
+def attend_body(held, starts, carried, final, devices, place_ref, lengths_ref, owners_ref, rotated_ref, *refs):
+    local_rows, width = rotated_ref.shape
+    own = place_ref[0]
+    count = devices * len(starts) if final else len(held)
+    blocks = refs[:count]
+    rest = refs[count:]
+    old = rest[:3] if carried else ()
+    rest = rest[len(old) :]
+    parts = [blocks[c * devices + k] for k, c in held] if final else blocks
+    amount = sum(ref.shape[0] for ref in parts)
+    columns = lax.broadcasted_iota(jnp.int32, (local_rows, amount), 1)
+    rows = own * local_rows + lax.broadcasted_iota(jnp.int32, (local_rows, amount), 0)
+    key_rows = columns
+    at = 0
+    for (k, c), ref in zip(held, parts):
+        moved = columns + ((own ^ k) * local_rows + (starts[c] - at))
+        key_rows = jnp.where(columns >= at, moved, key_rows) if at else moved
+        at += ref.shape[0]
+    allowed = (key_rows >= first_rows(rows, lengths_ref)) & (key_rows <= rows)
+    scale = float(HD) ** -0.5
+    kv_heads = parts[0].shape[1] // (2 * HD)
+    query_heads = width // HD
+    group_size = query_heads // kv_heads
+    for j in range(kv_heads):
+        base = 2 * j * HD
+        keys = jnp.concatenate([ref[:, base : base + HD] for ref in parts], axis=0)
+        values = jnp.concatenate([ref[:, base + HD : base + 2 * HD] for ref in parts], axis=0)
+        heads = range(j * group_size, (j + 1) * group_size)
+        for at in range(0, group_size, TOGETHER):
+            some = [slice(h * HD, (h + 1) * HD) for h in heads[at : at + TOGETHER]]
+            scores = [
+                lax.dot_general(
+                    rotated_ref[:, lanes],
+                    keys,
+                    (((1,), (1,)), ((), ())),
+                    preferred_element_type=jnp.float32,
+                )
+                for lanes in some
+            ]
+            olds = [[ref[:, lanes] for ref in old] for lanes in some]
+            scores = [jnp.where(allowed, score, LOW) for score in scores]
+            tops = [
+                jnp.broadcast_to(jnp.max(score, axis=1, keepdims=True), (local_rows, HD))
+                for score in scores
+            ]
+            if carried:
+                tops = [jnp.maximum(top, past[0]) for top, past in zip(tops, olds)]
+            weights = [
+                jnp.exp((score - widen(top, amount)) * scale) for score, top in zip(scores, tops)
+            ]
+            totals = [
+                jnp.broadcast_to(jnp.sum(weight, axis=1, keepdims=True), (local_rows, HD))
+                for weight in weights
+            ]
+            outs = [
+                jnp.dot(weight.astype(jnp.bfloat16), values, preferred_element_type=jnp.float32)
+                for weight in weights
+            ]
+            if carried:
+                factors = [jnp.exp((past[0] - top) * scale) for top, past in zip(tops, olds)]
+                totals = [t + past[1] * f for t, past, f in zip(totals, olds, factors)]
+                outs = [out + past[2] * f for out, past, f in zip(outs, olds, factors)]
+            if final:
+                for lanes, total, out in zip(some, totals, outs):
+                    rest[0][:, lanes] = (out * (1.0 / total)).astype(jnp.bfloat16)
+            else:
+                for lanes, top, total, out in zip(some, tops, totals, outs):
+                    rest[0][:, lanes] = top
+                    rest[1][:, lanes] = total
+                    rest[2][:, lanes] = out
+    if final:
+        fill_cache(blocks, starts, own, devices, local_rows, owners_ref, *rest[1:])
+
+
+def fill_cache(blocks, starts, own, devices, local_rows, owners_ref, cache_ref, leading_ref):
+    total_blocks = owners_ref.shape[0]
+    blocks_dev = total_blocks // devices
+    block_len = local_rows // blocks_dev
+    count = jnp.int32(0)
+    for b in range(total_blocks):
+        hit = owners_ref[b] == own
+
+        @pl.when(hit)
+        def _(b=b, count=count):
+            leading_ref[count] = b
+
+        count = count + hit.astype(jnp.int32)
+    for r in range(blocks_dev):
+        block = leading_ref[r]
+        distance = (block // blocks_dev) ^ own
+        row = (block % blocks_dev) * block_len
+        for c, start in enumerate(starts):
+            for k in range(devices):
+                ref = blocks[c * devices + k]
+                inside = (distance == k) & (row >= start) & (row < start + ref.shape[0])
+
+                @pl.when(inside)
+                def _(ref=ref, start=start, row=row, r=r):
+                    source = pl.ds(pl.multiple_of(row - start, block_len), block_len)
+                    cache_ref[r * block_len : (r + 1) * block_len, :] = ref[source, :]
+
+
+def chunked_device(activations, queries, key_weight, value_weight, lengths, owners, sizes):
+    local_rows, width = activations.shape
+    devices = lax.axis_size("seq")
+    parts = lax.axis_size("tp")
+    kv_width = key_weight.shape[1]
+    place = jnp.stack([lax.axis_index("seq"), lax.axis_index("tp")]).astype(jnp.int32)
+    starts = [sum(sizes[:c]) for c in range(len(sizes))]
+    far = parts // 2
+
+    def spread_over(pieces, distance):
+        while distance:
+            for offset in list(pieces):
+                pieces[offset ^ distance] = swap(pieces[offset], "tp", distance)
+            distance //= 2
+        return pieces
+
+    crossed = []
+    for start, size in zip(starts, sizes):
+        crossed.append(swap(activations[start : start + size], "tp", far))
+    near = spread_over({0: activations}, far // 2)
+
+    exponent = np.arange(HD // 2) * (2.0 / HD)
+    inverse = np.exp(-exponent * np.log(500000.0)).astype(np.float32)
+    inverse = jnp.asarray(np.concatenate([inverse, inverse])[None, :])
+    table = jax.ShapeDtypeStruct((local_rows, HD), jnp.float32)
+    cosines, sines, rotated = call(
+        prepare_body,
+        [table, table, jax.ShapeDtypeStruct(queries.shape, jnp.bfloat16)],
+        [SMEM, SMEM, VMEM, VMEM],
+    )(place, lengths, inverse, queries)
+    offsets = sorted(near)
+    stays = [pltpu.with_memory_space_constraint(a, pltpu.HBM) for a in (key_weight, value_weight, activations)]
+    weights = jax.ShapeDtypeStruct((parts, width, kv_width), jnp.bfloat16)
+    keys, values, sums = call(
+        functools.partial(early_body, offsets),
+        [weights, weights, jax.ShapeDtypeStruct((local_rows, 2 * kv_width), jnp.float32)],
+        [SMEM] + [ANY] * 3 + [VMEM] * (len(offsets) - 1),
+        scratch=[
+            pltpu.VMEM(activations.shape, activations.dtype),
+            pltpu.SemaphoreType.DMA((2, parts)),
+            pltpu.SemaphoreType.DMA,
+        ],
+    )(place, *stays, *[near[o] for o in offsets[1:]])
+
+    arrived = []
+    ready = sums
+    for piece, start, size in zip(crossed, starts, sizes):
+        piece = lax.optimization_barrier((piece, ready))[0]
+        late = spread_over({far: piece}, far // 2)
+        del late[far]
+        partial = call(
+            functools.partial(far_body, far, start),
+            jax.ShapeDtypeStruct((size, 2 * kv_width), jnp.float32),
+            [VMEM] * 4,
+        )(keys, values, sums, piece)
+        offsets = sorted(late)
+        packed = call(
+            functools.partial(late_body, offsets, start),
+            jax.ShapeDtypeStruct((size, 2 * kv_width), jnp.bfloat16),
+            [VMEM] * (5 + len(offsets)),
+        )(keys, values, partial, cosines, sines, *[late[o] for o in offsets])
+        ready = packed
+        blocks = [packed]
+        for k in range(1, devices):
+            blocks.append(swap(packed, "seq", k))
+        arrived.append(blocks)
+
+    last = len(sizes) - 1
+    half = devices // 2
+    stages = [[(k, c) for k in range(devices)] for c in range(last)]
+    if half:
+        stages.append([(k, last) for k in range(half)])
+    stages.append([(k, last) for k in range(half, devices)])
+    state = ()
+    for n, held in enumerate(stages):
+        final = n == len(stages) - 1
+        if final:
+            taken = [block for blocks in arrived for block in blocks]
+            results = [
+                jax.ShapeDtypeStruct(queries.shape, jnp.bfloat16),
+                jax.ShapeDtypeStruct((local_rows, 2 * kv_width), jnp.bfloat16),
+            ]
+        else:
+            taken = [arrived[c][k] for k, c in held]
+            results = [jax.ShapeDtypeStruct(queries.shape, jnp.float32)] * 3
+        state = call(
+            functools.partial(attend_body, held, starts, n > 0, final, devices),
+            results,
+            [SMEM] * 3 + [VMEM] * (1 + len(taken) + len(state)),
+            scratch=[pltpu.SMEM((owners.shape[0] // devices,), jnp.int32)] if final else (),
+        )(place, lengths, owners, rotated, *taken, *state)
+    attention, cache = state
+    return attention, cache.reshape(local_rows, kv_width // HD, 2 * HD)
+
+
+def chunk_sizes(local_rows, block_len):
+    first = (local_rows // block_len // 2) * block_len
+    return [first, local_rows - first]
+
+
+def per_device(activations, queries, key_weight, value_weight, lengths, owners):
+    local_rows = activations.shape[0]
+    devices = lax.axis_size("seq")
+    parts = lax.axis_size("tp")
+    blocks_dev = owners.shape[0] // devices
+    block_len = local_rows // blocks_dev
+    few = devices <= 8 and 1 < parts <= 8 and is_power(devices) and is_power(parts)
+    if not few or block_len % 16 or blocks_dev < 2:
+        return gathered_device(activations, queries, key_weight, value_weight, lengths, owners)
+    sizes = chunk_sizes(local_rows, block_len)
+    return chunked_device(activations, queries, key_weight, value_weight, lengths, owners, sizes)
+
+
 def solution(mesh):
-    in_specs = (
-        P(("groups", "seq"), "tp"),
-        P(("groups", "seq"), "tp"),
-        P(None, "tp"),
-        P(None, "tp"),
-        P("groups"),
-        P("groups"),
-    )
-    out_specs = (P(("groups", "seq"), "tp"), P(("groups", "seq"), "tp", None))
+    rows = P(("groups", "seq"), "tp")
+    columns = P(None, "tp")
+
     return jax.shard_map(
-        per_device, mesh=mesh, in_specs=in_specs, out_specs=out_specs, check_vma=False
-    )
+        per_device,
+        mesh=mesh,
+        in_specs=(rows, rows, columns, columns, P("groups"), P("groups")),
+        out_specs=(rows, P(("groups", "seq"), "tp", None)),
+        check_vma=False,
+    )

time: 71.9 us -> 40.1 us (0.56)
  blocking collectives: 15.3 us -> 0 us
  waiting for transfers between devices: 23.8 us -> 9.71 us
  Pallas kernels: 0 us -> 14 us
  starting transfers between devices: 0.04 us -> 13.7 us
  between operations: 14.2 us -> 0.73 us
  matrix products: 9.66 us -> 0 us
  other arithmetic: 5.07 us -> 0.07 us
  local copies, waits for them, and re-layouts: 3.61 us -> 1.77 us
    all_gather x1 -> x0, waiting for transfers between devices: 23.1 us -> none  [per_device(): portion = lax.all_gather(activations, 'tp', axis=1, tiled=True)]
    all_gather x1 -> x0, blocking collectives: 15.3 us -> none  [per_device(): portion = lax.all_gather(packed, 'seq', axis=0, tiled=True)]
    pallas_call x0 -> x9, Pallas kernels: none -> 14 us  [the longest x3 6 us: chunked_device(): call(functools.partial(attend_body, held, starts, n > 0, final, devices),...]
    ppermute x0 -> x11, starting transfers between devices: none -> 13.7 us  [swap(): return lax.ppermute(array, axis, [(i, i ^ distance) for i in range(count)])]
    ppermute x0 -> x11, waiting for transfers between devices: none -> 9.71 us  [swap(): return lax.ppermute(array, axis, [(i, i ^ distance) for i in range(count)])]
    dot_general x5 -> x0, matrix products: 9.66 us -> none  [the longest x1 4.34 us: per_device(): key_sums = jnp.dot(portion, key_rows, preferred_element_type=jnp.float32)]
    another operation x7 -> x1, other arithmetic: 1.79 us -> 0.07 us  [chunked_device(): jnp.stack([lax.axis_index('seq'), lax.axis_index('tp')]).astype(jnp.int32)]
    reduce_sum x5 -> x0, other arithmetic: 1.25 us -> none  [the longest x1 0.87 us: attend_block(): running_sum = running_sum * factor + jnp.sum(weights, axis=-1)]
  transfers between devices with their start and end apart: 1 -> 11, of which waited for: 1 -> 5; matrix products, arithmetic and copies ran while one was open for 5% -> 3% of each run, Pallas kernels for 0% -> 28%
where the time goes in v3:
time: 40.1 us; the launch traced here: 40 us
  Pallas kernels  14 us (35%)
  starting transfers between devices  13.7 us (34%)
  waiting for transfers between devices  9.71 us (24%)
  local copies, waits for them, and re-layouts  1.77 us (4%)
  between operations  0.73 us (2%)
    ppermute x11, starting transfers between devices, swap(): return lax.ppermute(array, axis, [(i, i ^ distance) for i in range(count)])  13.7 us
    ppermute x11, waiting for transfers between devices, swap(): return lax.ppermute(array, axis, [(i, i ^ distance) for i in range(count)])  9.71 us
    pallas_call x3, Pallas kernels, chunked_device(): call(functools.partial(attend_body, held, starts, n > 0, final, devices),...  6 us
    pallas_call x1, Pallas kernels, chunked_device(): call(functools.partial(early_body, offsets), [weights, weights, jax.Shape...  4.8 us
    pallas_call x2, Pallas kernels, chunked_device(): call(functools.partial(late_body, offsets, start), jax.ShapeDtypeStruct((...  1.12 us
    pallas_call x1, Pallas kernels, chunked_device(): call(prepare_body, [table, table, jax.ShapeDtypeStruct(queries.shape, jnp...  1.08 us
    slice x1, local copies, waits for them, and re-layouts, chunked_device(): crossed.append(swap(activations[start:start + size], 'tp', far))  1.06 us
    pallas_call x2, Pallas kernels, chunked_device(): call(functools.partial(far_body, far, start), jax.ShapeDtypeStruct((size,...  0.97 us
  transfers between devices with their start and end apart: 11, of which 5 were waited for; matrix products, arithmetic and copies ran while one was open for 3% of the time, Pallas kernels for 28%

profile of v3, /device:TPU:0, one launch (start us, length us, event | category | flops | bytes accessed | tf_op | source)
XLA Modules:
  0.0 40.0 jit_solution(2537549484308308327)
XLA Ops:
  0.6 0.6 %collective-permute-start = (bf16[128,2048]{1,0:T(8,128)(2,1)}, bf16[128,2048]{1,0:T(8,128)(2,1)S(1)}, u32[]{:S(2)}, u32[]{:S(2)}) collective-permute-start(bf16[128,2048]{1,0:T(8,128)(2,1)} %own_hbm.1), channel_id=1, source_target_pairs={{0,1},{1,0},{2,3},{3,2},{4,5},{5,4},{6,7},{7,6},{8,9},{9,8},{10,11... | collective-permute-start | bytes 1572872 | tf_op jit(solution)/shard_map/ppermute | solution.py:51
  1.2 1.1 %fusion = (bf16[64,2048]{1,0:T(8,128)(2,1)S(1)}, bf16[64,2048]{1,0:T(8,128)(2,1)S(1)}) fusion(bf16[128,2048]{1,0:T(8,128)(2,1)} %own_hbm.1), kind=kLoop, calls=%fused_computation.1 | loop fusion | bytes 1048576 | tf_op jit(solution)/shard_map/slice | solution.py:388
  2.3 2.6 %collective-permute-start.1 = (bf16[64,2048]{1,0:T(8,128)(2,1)S(1)}, bf16[64,2048]{1,0:T(8,128)(2,1)S(1)}, u32[]{:S(2)}, u32[]{:S(2)}) collective-permute-start(bf16[64,2048]{1,0:T(8,128)(2,1)S(1)} %get-tuple-element.35), channel_id=1, source_target_pairs={{0,2},{1,3},{2,0},{3,1},{4,6},{5,7},{6,4},{7,5},{8,10},{9,11},{10,... | collective-permute-start | bytes 786440 | tf_op jit(solution)/shard_map/ppermute | solution.py:51
  4.8 0.1 pad_add_fusion.place_ref
  4.9 0.0 copy-start
  4.9 0.0 copy-start.1
  4.9 0.0 copy-start.3
  4.9 0.0 collective-permute-done.refs_0_
  4.9 4.8 %shard_map.87 = (bf16[4,2048,256]{2,1,0:T(8,128)(2,1)S(1)}, bf16[4,2048,256]{2,1,0:T(8,128)(2,1)S(1)}, f32[128,512]{1,0:T(8,128)S(1)}) custom-call(s32[2]{0:T(128)S(1)} %pad_add_fusion.place_ref, bf16[8192,256]{1,0:T(8,128)(2,1)} %key_hbm.1, bf16[8192,256]{1,0:T(8,128)(2,1)} %value_hbm.1, bf16[128,2048]{1,0:T(8,128)(2,1)} %own_hbm.1, ...), custom_call_target="tpu_custom_call" | custom-call | tf_op jit(solution)/shard_map/pallas_call | solution.py:403
  9.7 2.1 %collective-permute-done.1.piece_ref = bf16[64,2048]{1,0:T(8,128)(2,1)S(1)} collective-permute-done((bf16[64,2048]{1,0:T(8,128)(2,1)S(1)}, bf16[64,2048]{1,0:T(8,128)(2,1)S(1)}, u32[]{:S(2)}, u32[]{:S(2)}) %collective-permute-start.1) | collective-permute-done | bytes 262176 | tf_op jit(solution)/shard_map/ppermute | solution.py:51
  11.8 0.0 collective-permute-start.2
  11.8 1.7 %collective-permute-start.6 = (bf16[64,2048]{1,0:T(8,128)(2,1)S(1)}, bf16[64,2048]{1,0:T(8,128)(2,1)S(1)}, u32[]{:S(2)}, u32[]{:S(2)}) collective-permute-start(bf16[64,2048]{1,0:T(8,128)(2,1)S(1)} %get-tuple-element.34), channel_id=1, source_target_pairs={{0,2},{1,3},{2,0},{3,1},{4,6},{5,7},{6,4},{7,5},{8,10},{9,11},{10,... | collective-permute-start | bytes 786440 | tf_op jit(solution)/shard_map/ppermute | solution.py:51
  13.5 0.0 copy-done
  13.5 0.0 copy-done.1
  13.5 0.0 copy-done.3
  13.5 1.1 %shard_map.86 = (f32[128,128]{1,0:T(8,128)S(1)}, f32[128,128]{1,0:T(8,128)S(1)}, bf16[128,2048]{1,0:T(8,128)(2,1)S(1)}) custom-call(s32[2]{0:T(128)S(1)} %pad_add_fusion.place_ref, s32[4]{0:T(128)S(1)} %copy-done.1, f32[1,128]{1,0:T(1,128)S(1)} %copy-done.3, bf16[128,2048]{1,0:T(8,128)(2,1)S(1)} %copy-done), custom_call_target="tpu_custom_call" | custom-call | tf_op jit(solution)/shard_map/pallas_call | solution.py:395
  14.6 0.5 %shard_map.88.sums_ref = f32[64,512]{1,0:T(8,128)S(1)} custom-call(bf16[4,2048,256]{2,1,0:T(8,128)(2,1)S(1)} %get-tuple-element.19.keys_ref, bf16[4,2048,256]{2,1,0:T(8,128)(2,1)S(1)} %get-tuple-element.20.values_ref, f32[128,512]{1,0:T(8,128)S(1)} %get-tuple-element.21.sums_ref, bf16[64,2048]{1,0:T(8,128)(2,1)S(1)} %collective-permute-done.1.piece_ref), custom_call_target="tpu_custom_call" | custom-call | tf_op jit(solution)/shard_map/pallas_call | solution.py:420
  15.1 0.0 collective-permute-done.2.refs_0_
  15.1 0.6 %shard_map.89.refs_0_ = bf16[64,512]{1,0:T(8,128)(2,1)S(1)} custom-call(bf16[4,2048,256]{2,1,0:T(8,128)(2,1)S(1)} %get-tuple-element.19.keys_ref, bf16[4,2048,256]{2,1,0:T(8,128)(2,1)S(1)} %get-tuple-element.20.values_ref, f32[64,512]{1,0:T(8,128)S(1)} %shard_map.88.sums_ref, f32[128,128]{1,0:T(8,128)S(1)} %get-tuple-element.23.cos_ref, ...), custom_call_target="tpu_custom_call" | custom-call | tf_op jit(solution)/shard_map/pallas_call | solution.py:426
  15.7 4.8 %collective-permute-done.6.piece_ref = bf16[64,2048]{1,0:T(8,128)(2,1)S(1)} collective-permute-done((bf16[64,2048]{1,0:T(8,128)(2,1)S(1)}, bf16[64,2048]{1,0:T(8,128)(2,1)S(1)}, u32[]{:S(2)}, u32[]{:S(2)}) %collective-permute-start.6) | collective-permute-done | bytes 262176 | tf_op jit(solution)/shard_map/ppermute | solution.py:51
  20.5 0.0 collective-permute-start.7
  20.5 1.8 %collective-permute-start.3 = (bf16[64,512]{1,0:T(8,128)(2,1)S(1)}, bf16[64,512]{1,0:T(8,128)(2,1)S(1)}, u32[]{:S(2)}, u32[]{:S(2)}) collective-permute-start(bf16[64,512]{1,0:T(8,128)(2,1)S(1)} %shard_map.89.refs_0_), channel_id=1, source_target_pairs={{0,4},{4,0},{8,12},{12,8},{1,5},{5,1},{9,13},{13,9},{2,6},{6,2},{1... | collective-permute-start | bytes 196616 | tf_op jit(solution)/shard_map/ppermute | solution.py:51
  22.3 2.6 %collective-permute-start.4 = (bf16[64,512]{1,0:T(8,128)(2,1)S(1)}, bf16[64,512]{1,0:T(8,128)(2,1)S(1)}, u32[]{:S(2)}, u32[]{:S(2)}) collective-permute-start(bf16[64,512]{1,0:T(8,128)(2,1)S(1)} %shard_map.89.refs_0_), channel_id=1, source_target_pairs={{0,8},{4,12},{8,0},{12,4},{1,9},{5,13},{9,1},{13,5},{2,10},{6,14},... | collective-permute-start | bytes 196616 | tf_op jit(solution)/shard_map/ppermute | solution.py:51
  24.9 0.0 collective-permute-start.5
  24.9 0.5 %shard_map.90.sums_ref = f32[64,512]{1,0:T(8,128)S(1)} custom-call(bf16[4,2048,256]{2,1,0:T(8,128)(2,1)S(1)} %get-tuple-element.19.keys_ref, bf16[4,2048,256]{2,1,0:T(8,128)(2,1)S(1)} %get-tuple-element.20.values_ref, f32[128,512]{1,0:T(8,128)S(1)} %get-tuple-element.21.sums_ref, bf16[64,2048]{1,0:T(8,128)(2,1)S(1)} %collective-permute-done.6.piece_ref), custom_call_target="tpu_custom_call" | custom-call | tf_op jit(solution)/shard_map/pallas_call | solution.py:420
  25.4 0.0 copy-start.2
  25.4 0.0 collective-permute-done.7.refs_0_
  25.4 0.6 %shard_map.91.refs_0_.refs_4_ = bf16[64,512]{1,0:T(8,128)(2,1)S(1)} custom-call(bf16[4,2048,256]{2,1,0:T(8,128)(2,1)S(1)} %get-tuple-element.19.keys_ref, bf16[4,2048,256]{2,1,0:T(8,128)(2,1)S(1)} %get-tuple-element.20.values_ref, f32[64,512]{1,0:T(8,128)S(1)} %shard_map.90.sums_ref, f32[128,128]{1,0:T(8,128)S(1)} %get-tuple-element.23.cos_ref, ...), custom_call_target="tpu_custom_call" | custom-call | tf_op jit(solution)/shard_map/pallas_call | solution.py:426
  26.0 1.0 %collective-permute-start.8 = (bf16[64,512]{1,0:T(8,128)(2,1)S(1)}, bf16[64,512]{1,0:T(8,128)(2,1)S(1)}, u32[]{:S(2)}, u32[]{:S(2)}) collective-permute-start(bf16[64,512]{1,0:T(8,128)(2,1)S(1)} %shard_map.91.refs_0_.refs_4_), channel_id=1, source_target_pairs={{0,4},{4,0},{8,12},{12,8},{1,5},{5,1},{9,13},{13,9},{2,6},{6,2},{1... | collective-permute-start | bytes 196616 | tf_op jit(solution)/shard_map/ppermute | solution.py:51
  27.0 3.5 %collective-permute-start.9 = (bf16[64,512]{1,0:T(8,128)(2,1)S(1)}, bf16[64,512]{1,0:T(8,128)(2,1)S(1)}, u32[]{:S(2)}, u32[]{:S(2)}) collective-permute-start(bf16[64,512]{1,0:T(8,128)(2,1)S(1)} %shard_map.91.refs_0_.refs_4_), channel_id=1, source_target_pairs={{0,8},{4,12},{8,0},{12,4},{1,9},{5,13},{9,1},{13,5},{2,10},{6,14},... | collective-permute-start | bytes 196616 | tf_op jit(solution)/shard_map/ppermute | solution.py:51
  30.4 0.0 collective-permute-done.3.refs_1_
  30.4 0.0 collective-permute-start.10
  30.5 0.0 collective-permute-done.4.refs_2_
  30.5 1.1 %collective-permute-done.5.refs_3_ = bf16[64,512]{1,0:T(8,128)(2,1)S(1)} collective-permute-done((bf16[64,512]{1,0:T(8,128)(2,1)S(1)}, bf16[64,512]{1,0:T(8,128)(2,1)S(1)}, u32[]{:S(2)}, u32[]{:S(2)}) %collective-permute-start.5) | collective-permute-done | bytes 65568 | tf_op jit(solution)/shard_map/ppermute | solution.py:51
  31.6 0.0 copy-done.2
  31.6 1.6 %shard_map.92 = (f32[128,2048]{1,0:T(8,128)S(1)}, f32[128,2048]{1,0:T(8,128)S(1)}, f32[128,2048]{1,0:T(8,128)S(1)}) custom-call(s32[2]{0:T(128)S(1)} %pad_add_fusion.place_ref, s32[4]{0:T(128)S(1)} %copy-done.1, s32[16]{0:T(128)S(1)} %copy-done.2, bf16[128,2048]{1,0:T(8,128)(2,1)S(1)} %get-tuple-element.18.rotated_ref, ...), custom_call_target="tpu_custom_call" | custom-call | tf_op jit(solution)/shard_map/pallas_call | solution.py:455
  33.2 0.0 collective-permute-done.8.refs_1_.refs_5_
  33.2 1.7 %shard_map.93 = (f32[128,2048]{1,0:T(8,128)S(1)}, f32[128,2048]{1,0:T(8,128)S(1)}, f32[128,2048]{1,0:T(8,128)S(1)}) custom-call(s32[2]{0:T(128)S(1)} %pad_add_fusion.place_ref, s32[4]{0:T(128)S(1)} %copy-done.1, s32[16]{0:T(128)S(1)} %copy-done.2, bf16[128,2048]{1,0:T(8,128)(2,1)S(1)} %get-tuple-element.18.rotated_ref, ...), custom_call_target="tpu_custom_call" | custom-call | tf_op jit(solution)/shard_map/pallas_call | solution.py:455
  34.9 0.7 %collective-permute-done.9.refs_6_ = bf16[64,512]{1,0:T(8,128)(2,1)S(1)} collective-permute-done((bf16[64,512]{1,0:T(8,128)(2,1)S(1)}, bf16[64,512]{1,0:T(8,128)(2,1)S(1)}, u32[]{:S(2)}, u32[]{:S(2)}) %collective-permute-start.9) | collective-permute-done | bytes 65568 | tf_op jit(solution)/shard_map/ppermute | solution.py:51
  35.6 1.0 %collective-permute-done.10.refs_7_ = bf16[64,512]{1,0:T(8,128)(2,1)S(1)} collective-permute-done((bf16[64,512]{1,0:T(8,128)(2,1)S(1)}, bf16[64,512]{1,0:T(8,128)(2,1)S(1)}, u32[]{:S(2)}, u32[]{:S(2)}) %collective-permute-start.10) | collective-permute-done | bytes 65568 | tf_op jit(solution)/shard_map/ppermute | solution.py:51
  36.6 2.7 %shard_map.94 = (bf16[128,2048]{1,0:T(8,128)(2,1)}, bf16[128,512]{1,0:T(8,128)(2,1)S(1)}) custom-call(s32[2]{0:T(128)S(1)} %pad_add_fusion.place_ref, s32[4]{0:T(128)S(1)} %copy-done.1, s32[16]{0:T(128)S(1)} %copy-done.2, bf16[128,2048]{1,0:T(8,128)(2,1)S(1)} %get-tuple-element.18.rotated_ref, bf16[64,512]{1,0:T(8,128)(2,1)S(1)} %shard_map.89.refs_0_, ...), custom_call_target="tpu_custom_call" | custom-call | tf_op jit(solution)/shard_map/pallas_call | solution.py:455
  39.3 0.7 %reshape.7 = bf16[128,2,256]{2,1,0:T(2,128)(2,1)} reshape(bf16[128,512]{1,0:T(8,128)(2,1)S(1)} %get-tuple-element.33) | data formatting | bytes 262144 | tf_op jit(solution)/shard_map/reshape | solution.py:462
Async XLA Ops:
  0.6 4.3 %collective-permute-start = (bf16[128,2048]{1,0:T(8,128)(2,1)}, bf16[128,2048]{1,0:T(8,128)(2,1)S(1)}, u32[]{:S(2)}, u32[]{:S(2)}) collective-permute-start(bf16[128,2048]{1,0:T(8,128)(2,1)} %own_hbm.1), channel_id=1, source_target_pairs={{0,1},{1,0},{2,3},{3,2},{4,5},{5,4},{6,7},{7,6},{8,9},{9,8},{10,11... | collective-permute-start | bytes 1572872 | tf_op jit(solution)/shard_map/ppermute | solution.py:51
  2.3 9.5 %collective-permute-start.1 = (bf16[64,2048]{1,0:T(8,128)(2,1)S(1)}, bf16[64,2048]{1,0:T(8,128)(2,1)S(1)}, u32[]{:S(2)}, u32[]{:S(2)}) collective-permute-start(bf16[64,2048]{1,0:T(8,128)(2,1)S(1)} %get-tuple-element.35), channel_id=1, source_target_pairs={{0,2},{1,3},{2,0},{3,1},{4,6},{5,7},{6,4},{7,5},{8,10},{9,11},{10,... | collective-permute-start | bytes 786440 | tf_op jit(solution)/shard_map/ppermute | solution.py:51
  4.9 8.6 %copy-start = (bf16[128,2048]{1,0:T(8,128)(2,1)S(1)}, bf16[128,2048]{1,0:T(8,128)(2,1)}, u32[]{:S(2)}) copy-start(bf16[128,2048]{1,0:T(8,128)(2,1)} %queries_ref.1) | copy-start | bytes 1572868
  4.9 8.6 %copy-start.1 = (s32[4]{0:T(128)S(1)}, s32[4]{0:T(128)}, u32[]{:S(2)}) copy-start(s32[4]{0:T(128)} %lengths_ref.7) | copy-start | bytes 52
  4.9 8.6 %copy-start.3 = (f32[1,128]{1,0:T(1,128)S(1)}, f32[1,128]{1,0:T(1,128)}, u32[]{:S(2)}) copy-start(f32[1,128]{1,0:T(1,128)} %constant.9.clone.inverse_ref) | copy-start | bytes 1540
  11.8 3.3 %collective-permute-start.2 = (bf16[64,2048]{1,0:T(8,128)(2,1)S(1)}, bf16[64,2048]{1,0:T(8,128)(2,1)S(1)}, u32[]{:S(2)}, u32[]{:S(2)}) collective-permute-start(bf16[64,2048]{1,0:T(8,128)(2,1)S(1)} %collective-permute-done.1.piece_ref), channel_id=1, source_target_pairs={{0,1},{1,0},{2,3},{3,2},{4,5},{5,4},{6,7},{7,6},{8,9},{9,8},{10,11... | collective-permute-start | bytes 786440 | tf_op jit(solution)/shard_map/ppermute | solution.py:51
  11.8 8.7 %collective-permute-start.6 = (bf16[64,2048]{1,0:T(8,128)(2,1)S(1)}, bf16[64,2048]{1,0:T(8,128)(2,1)S(1)}, u32[]{:S(2)}, u32[]{:S(2)}) collective-permute-start(bf16[64,2048]{1,0:T(8,128)(2,1)S(1)} %get-tuple-element.34), channel_id=1, source_target_pairs={{0,2},{1,3},{2,0},{3,1},{4,6},{5,7},{6,4},{7,5},{8,10},{9,11},{10,... | collective-permute-start | bytes 786440 | tf_op jit(solution)/shard_map/ppermute | solution.py:51
  20.5 4.9 %collective-permute-start.7 = (bf16[64,2048]{1,0:T(8,128)(2,1)S(1)}, bf16[64,2048]{1,0:T(8,128)(2,1)S(1)}, u32[]{:S(2)}, u32[]{:S(2)}) collective-permute-start(bf16[64,2048]{1,0:T(8,128)(2,1)S(1)} %collective-permute-done.6.piece_ref), channel_id=1, source_target_pairs={{0,1},{1,0},{2,3},{3,2},{4,5},{5,4},{6,7},{7,6},{8,9},{9,8},{10,11... | collective-permute-start | bytes 786440 | tf_op jit(solution)/shard_map/ppermute | solution.py:51
  20.5 9.9 %collective-permute-start.3 = (bf16[64,512]{1,0:T(8,128)(2,1)S(1)}, bf16[64,512]{1,0:T(8,128)(2,1)S(1)}, u32[]{:S(2)}, u32[]{:S(2)}) collective-permute-start(bf16[64,512]{1,0:T(8,128)(2,1)S(1)} %shard_map.89.refs_0_), channel_id=1, source_target_pairs={{0,4},{4,0},{8,12},{12,8},{1,5},{5,1},{9,13},{13,9},{2,6},{6,2},{1... | collective-permute-start | bytes 196616 | tf_op jit(solution)/shard_map/ppermute | solution.py:51
  22.3 8.1 %collective-permute-start.4 = (bf16[64,512]{1,0:T(8,128)(2,1)S(1)}, bf16[64,512]{1,0:T(8,128)(2,1)S(1)}, u32[]{:S(2)}, u32[]{:S(2)}) collective-permute-start(bf16[64,512]{1,0:T(8,128)(2,1)S(1)} %shard_map.89.refs_0_), channel_id=1, source_target_pairs={{0,8},{4,12},{8,0},{12,4},{1,9},{5,13},{9,1},{13,5},{2,10},{6,14},... | collective-permute-start | bytes 196616 | tf_op jit(solution)/shard_map/ppermute | solution.py:51
  24.9 6.6 %collective-permute-start.5 = (bf16[64,512]{1,0:T(8,128)(2,1)S(1)}, bf16[64,512]{1,0:T(8,128)(2,1)S(1)}, u32[]{:S(2)}, u32[]{:S(2)}) collective-permute-start(bf16[64,512]{1,0:T(8,128)(2,1)S(1)} %shard_map.89.refs_0_), channel_id=1, source_target_pairs={{0,12},{4,8},{8,4},{12,0},{1,13},{5,9},{9,5},{13,1},{2,14},{6,10},... | collective-permute-start | bytes 196616 | tf_op jit(solution)/shard_map/ppermute | solution.py:51
  25.4 6.1 %copy-start.2 = (s32[16]{0:T(128)S(1)}, s32[16]{0:T(128)}, u32[]{:S(2)}) copy-start(s32[16]{0:T(128)} %owners_ref.5) | copy-start | bytes 196
  26.0 7.2 %collective-permute-start.8 = (bf16[64,512]{1,0:T(8,128)(2,1)S(1)}, bf16[64,512]{1,0:T(8,128)(2,1)S(1)}, u32[]{:S(2)}, u32[]{:S(2)}) collective-permute-start(bf16[64,512]{1,0:T(8,128)(2,1)S(1)} %shard_map.91.refs_0_.refs_4_), channel_id=1, source_target_pairs={{0,4},{4,0},{8,12},{12,8},{1,5},{5,1},{9,13},{13,9},{2,6},{6,2},{1... | collective-permute-start | bytes 196616 | tf_op jit(solution)/shard_map/ppermute | solution.py:51
  27.0 8.7 %collective-permute-start.9 = (bf16[64,512]{1,0:T(8,128)(2,1)S(1)}, bf16[64,512]{1,0:T(8,128)(2,1)S(1)}, u32[]{:S(2)}, u32[]{:S(2)}) collective-permute-start(bf16[64,512]{1,0:T(8,128)(2,1)S(1)} %shard_map.91.refs_0_.refs_4_), channel_id=1, source_target_pairs={{0,8},{4,12},{8,0},{12,4},{1,9},{5,13},{9,1},{13,5},{2,10},{6,14},... | collective-permute-start | bytes 196616 | tf_op jit(solution)/shard_map/ppermute | solution.py:51
  30.4 6.2 %collective-permute-start.10 = (bf16[64,512]{1,0:T(8,128)(2,1)S(1)}, bf16[64,512]{1,0:T(8,128)(2,1)S(1)}, u32[]{:S(2)}, u32[]{:S(2)}) collective-permute-start(bf16[64,512]{1,0:T(8,128)(2,1)S(1)} %shard_map.91.refs_0_.refs_4_), channel_id=1, source_target_pairs={{0,12},{4,8},{8,4},{12,0},{1,13},{5,9},{9,5},{13,1},{2,14},{6,10},... | collective-permute-start | bytes 196616 | tf_op jit(solution)/shard_map/ppermute | solution.py:51

commit v4 on v3

--- a/solution.py
+++ b/solution.py
@@ -10,7 +10,7 @@
 
 HD = 128
 LOW = -1e30
-TOGETHER = 8
+TOGETHER = 16
 MIB = 1 << 20
 VMEM = pl.BlockSpec(memory_space=pltpu.VMEM)
 SMEM = pl.BlockSpec(memory_space=pltpu.SMEM)
@@ -55,7 +55,7 @@
     return count & (count - 1) == 0
 
 
-def call(body, out_shape, in_specs, vmem=8 * MIB, scratch=(), out_specs=None):
+def call(body, out_shape, in_specs, vmem=8 * MIB, scratch=(), out_specs=None, aliases={}):
     multiple = isinstance(out_shape, (list, tuple))
     return pl.pallas_call(
         body,
@@ -63,6 +63,7 @@
         in_specs=in_specs,
         out_specs=out_specs or ([VMEM] * len(out_shape) if multiple else VMEM),
         scratch_shapes=list(scratch),
+        input_output_aliases=aliases,
         compiler_params=pltpu.CompilerParams(vmem_limit_bytes=vmem),
     )
 
@@ -78,22 +79,6 @@
 
 def turn(vectors, cosines, sines):
     return vectors * cosines + pltpu.roll(vectors, HD // 2, 1) * sines
-
-
-def prepare_body(place_ref, lengths_ref, inverse_ref, queries_ref, cos_ref, sin_ref, rotated_ref):
-    local_rows, width = queries_ref.shape
-    rows = place_ref[0] * local_rows + lax.broadcasted_iota(jnp.int32, (local_rows, HD), 0)
-    positions = rows - first_rows(rows, lengths_ref)
-    angles = positions.astype(jnp.float32) * inverse_ref[...]
-    lanes = lax.broadcasted_iota(jnp.int32, (local_rows, HD), 1)
-    cosines = jnp.cos(angles)
-    sines = jnp.sin(angles)
-    sines = jnp.where(lanes < HD // 2, -sines, sines)
-    cos_ref[...] = cosines
-    sin_ref[...] = sines
-    for h in range(width // HD):
-        vectors = queries_ref[:, h * HD : (h + 1) * HD].astype(jnp.float32)
-        rotated_ref[:, h * HD : (h + 1) * HD] = turn(vectors, cosines, sines).astype(jnp.bfloat16)
 
 
 def gathered_device(activations, queries, key_weight, value_weight, lengths, owners):
@@ -196,20 +181,64 @@
     return (attention, kv_cache)
 
 
+def prepare(own, lengths_ref, owners_ref, queries_ref, cos_ref, sin_ref, rotated_ref, facts_ref, slots_ref):
+    local_rows, width = queries_ref.shape
+    rows = own * local_rows + lax.broadcasted_iota(jnp.int32, (local_rows, HD), 0)
+    positions = rows - first_rows(rows, lengths_ref)
+    half = HD // 2
+    lanes = lax.broadcasted_iota(jnp.int32, (local_rows, HD), 1)
+    exponent = jnp.where(lanes < half, lanes, lanes - half).astype(jnp.float32) * (2.0 / HD)
+    inverse = jnp.exp(-exponent * jnp.log(jnp.float32(500000.0)))
+    angles = positions.astype(jnp.float32) * inverse
+    cosines = jnp.cos(angles)
+    sines = jnp.sin(angles)
+    sines = jnp.where(lanes < half, -sines, sines)
+    cos_ref[...] = cosines
+    sin_ref[...] = sines
+    for h in range(width // HD):
+        vectors = queries_ref[:, h * HD : (h + 1) * HD].astype(jnp.float32)
+        rotated_ref[:, h * HD : (h + 1) * HD] = turn(vectors, cosines, sines).astype(jnp.bfloat16)
+    rows = own * local_rows + lax.broadcasted_iota(jnp.int32, (1, local_rows), 1)
+    facts_ref[0:1, :] = first_rows(rows, lengths_ref)
+    facts_ref[1:2, :] = rows
+    facts_ref[2:3, :] = jnp.zeros_like(rows) + own
+    count = jnp.int32(0)
+    for b in range(owners_ref.shape[0]):
+        hit = owners_ref[b] == own
+        slots_ref[b] = jnp.where(hit, count, -1)
+        count = count + hit.astype(jnp.int32)
+    slots_ref[owners_ref.shape[0]] = own
+
+
 def add_products(piece, key_ref, value_ref, sums):
     kv_width = key_ref.shape[1]
     for at, ref in ((0, key_ref), (kv_width, value_ref)):
         sums[at] = sums[at] + jnp.dot(piece, ref[...], preferred_element_type=jnp.float32)
 
 
-def early_body(offsets, place_ref, key_hbm, value_hbm, own_hbm, *refs):
+def early_body(offsets, place_ref, key_hbm, value_hbm, own_hbm, queries_hbm, lengths_hbm, owners_hbm, *refs):
     near_refs = refs[: len(offsets) - 1]
-    keys_ref, values_ref, sums_ref, own_ref, weight_sems, own_sem = refs[len(offsets) - 1 :]
+    outs = refs[len(offsets) - 1 :]
+    keys_ref, values_ref, sums_ref = outs[:3]
+    tables = outs[3:8]
+    own_ref, queries_ref, lengths_ref, owners_ref, weight_sems, sems = outs[8:]
     parts, width, kv_width = keys_ref.shape
+    small = [
+        pltpu.make_async_copy(source, goal, sems.at[n])
+        for n, (source, goal) in enumerate(
+            (
+                (lengths_hbm, lengths_ref),
+                (owners_hbm, owners_ref),
+                (queries_hbm, queries_ref),
+                (own_hbm, own_ref),
+            )
+        )
+    ]
+    for copy in small:
+        copy.start()
     copies = []
-    own_copy = pltpu.make_async_copy(own_hbm, own_ref, own_sem)
     order = list(offsets) + [o for o in range(parts) if o not in offsets]
-    for n, offset in enumerate(order):
+    for offset in order:
         start = pl.multiple_of((place_ref[1] ^ offset) * width, width)
         pair = [
             pltpu.make_async_copy(hbm.at[pl.ds(start, width)], ref.at[offset], weight_sems.at[side, offset])
@@ -218,9 +247,9 @@
         for copy in pair:
             copy.start()
         copies.append(pair)
-        if n == 0:
-            own_copy.start()
-    own_copy.wait()
+    for copy in small:
+        copy.wait()
+    prepare(place_ref[0], lengths_ref, owners_ref, queries_ref, *tables)
     sums = {0: 0.0, kv_width: 0.0}
     pieces = [own_ref] + list(near_refs)
     for n, offset in enumerate(order):
@@ -259,112 +288,109 @@
         packed_ref[:, base + HD : base + 2 * HD] = sums[kv_width][:, part].astype(jnp.bfloat16)
 
 
-def widen(column, amount):
-    count = -(-amount // HD)
-    wide = jnp.concatenate([column] * count, axis=1) if count > 1 else column
-    return wide[:, :amount]
-
-
-def attend_body(held, starts, carried, final, devices, place_ref, lengths_ref, owners_ref, rotated_ref, *refs):
+def attend_body(held, spans, carried, final, facts_ref, slots_hbm, rotated_ref, *refs):
     local_rows, width = rotated_ref.shape
-    own = place_ref[0]
-    count = devices * len(starts) if final else len(held)
-    blocks = refs[:count]
-    rest = refs[count:]
-    old = rest[:3] if carried else ()
+    starts, block_len = spans
+    parts = refs[: len(held)]
+    rest = refs[len(held) :]
+    old = rest[:4] if carried else ()
     rest = rest[len(old) :]
-    parts = [blocks[c * devices + k] for k, c in held] if final else blocks
+    slots_ref, slots_sem = rest[-2:]
+    cache_ref = rest[-3]
+    fetch = pltpu.make_async_copy(slots_hbm, slots_ref, slots_sem)
+    fetch.start()
     amount = sum(ref.shape[0] for ref in parts)
-    columns = lax.broadcasted_iota(jnp.int32, (local_rows, amount), 1)
-    rows = own * local_rows + lax.broadcasted_iota(jnp.int32, (local_rows, amount), 0)
-    key_rows = columns
+    order = lax.broadcasted_iota(jnp.int32, (amount, local_rows), 0)
+    own = facts_ref[2:3, :]
+    key_rows = order
     at = 0
     for (k, c), ref in zip(held, parts):
-        moved = columns + ((own ^ k) * local_rows + (starts[c] - at))
-        key_rows = jnp.where(columns >= at, moved, key_rows) if at else moved
+        moved = order + ((own ^ k) * local_rows + (starts[c] - at))
+        key_rows = jnp.where(order >= at, moved, key_rows) if at else moved
         at += ref.shape[0]
-    allowed = (key_rows >= first_rows(rows, lengths_ref)) & (key_rows <= rows)
-    scale = float(HD) ** -0.5
+    allowed = (key_rows >= facts_ref[0:1, :]) & (key_rows <= facts_ref[1:2, :])
+    scale = float(HD**-0.5 * np.log2(np.e))
     kv_heads = parts[0].shape[1] // (2 * HD)
     query_heads = width // HD
     group_size = query_heads // kv_heads
+    if final:
+        lines = lax.broadcasted_iota(jnp.int32, (local_rows, local_rows), 0)
+        lanes = lax.broadcasted_iota(jnp.int32, (local_rows, local_rows), 1)
+        identity = (lines == lanes).astype(jnp.bfloat16)
+    keys = []
+    values = []
     for j in range(kv_heads):
         base = 2 * j * HD
-        keys = jnp.concatenate([ref[:, base : base + HD] for ref in parts], axis=0)
-        values = jnp.concatenate([ref[:, base + HD : base + 2 * HD] for ref in parts], axis=0)
-        heads = range(j * group_size, (j + 1) * group_size)
-        for at in range(0, group_size, TOGETHER):
-            some = [slice(h * HD, (h + 1) * HD) for h in heads[at : at + TOGETHER]]
-            scores = [
-                lax.dot_general(
-                    rotated_ref[:, lanes],
-                    keys,
+        keys.append(jnp.concatenate([ref[:, base : base + HD] for ref in parts], axis=0))
+        value = jnp.concatenate([ref[:, base + HD : base + 2 * HD] for ref in parts], axis=0)
+        values.append(value.T)
+    for at in range(0, query_heads, TOGETHER):
+        some = range(query_heads)[at : at + TOGETHER]
+        parts_of = [slice(h * HD, (h + 1) * HD) for h in some]
+        scores = [
+            lax.dot_general(
+                keys[h // group_size],
+                rotated_ref[:, part],
+                (((1,), (1,)), ((), ())),
+                preferred_element_type=jnp.float32,
+            )
+            for h, part in zip(some, parts_of)
+        ]
+        if carried:
+            old_tops = [old[0][h : h + 1, :] for h in some]
+            old_totals = [old[1][h : h + 1, :] for h in some]
+            old_outs = [old[2][part, :] for part in parts_of]
+        scores = [jnp.where(allowed, score, LOW) for score in scores]
+        tops = [jnp.max(score, axis=0, keepdims=True) for score in scores]
+        if carried:
+            tops = [jnp.maximum(top, past) for top, past in zip(tops, old_tops)]
+        weights = [jnp.exp2((score - top) * scale) for score, top in zip(scores, tops)]
+        totals = [jnp.sum(weight, axis=0, keepdims=True) for weight in weights]
+        outs = [
+            jnp.dot(
+                values[h // group_size],
+                weight.astype(jnp.bfloat16),
+                preferred_element_type=jnp.float32,
+            )
+            for h, weight in zip(some, weights)
+        ]
+        if carried:
+            factors = [jnp.exp2((past - top) * scale) for top, past in zip(tops, old_tops)]
+            totals = [t + past * f for t, past, f in zip(totals, old_totals, factors)]
+            outs = [out + past * f for out, past, f in zip(outs, old_outs, factors)]
+        if final:
+            outs = [(out * (1.0 / total)).astype(jnp.bfloat16) for out, total in zip(outs, totals)]
+            for part, out in zip(parts_of, outs):
+                rest[0][:, part] = lax.dot_general(
+                    identity,
+                    out,
                     (((1,), (1,)), ((), ())),
                     preferred_element_type=jnp.float32,
-                )
-                for lanes in some
-            ]
-            olds = [[ref[:, lanes] for ref in old] for lanes in some]
-            scores = [jnp.where(allowed, score, LOW) for score in scores]
-            tops = [
-                jnp.broadcast_to(jnp.max(score, axis=1, keepdims=True), (local_rows, HD))
-                for score in scores
-            ]
-            if carried:
-                tops = [jnp.maximum(top, past[0]) for top, past in zip(tops, olds)]
-            weights = [
-                jnp.exp((score - widen(top, amount)) * scale) for score, top in zip(scores, tops)
-            ]
-            totals = [
-                jnp.broadcast_to(jnp.sum(weight, axis=1, keepdims=True), (local_rows, HD))
-                for weight in weights
-            ]
-            outs = [
-                jnp.dot(weight.astype(jnp.bfloat16), values, preferred_element_type=jnp.float32)
-                for weight in weights
-            ]
-            if carried:
-                factors = [jnp.exp((past[0] - top) * scale) for top, past in zip(tops, olds)]
-                totals = [t + past[1] * f for t, past, f in zip(totals, olds, factors)]
-                outs = [out + past[2] * f for out, past, f in zip(outs, olds, factors)]
-            if final:
-                for lanes, total, out in zip(some, totals, outs):
-                    rest[0][:, lanes] = (out * (1.0 / total)).astype(jnp.bfloat16)
-            else:
-                for lanes, top, total, out in zip(some, tops, totals, outs):
-                    rest[0][:, lanes] = top
-                    rest[1][:, lanes] = total
-                    rest[2][:, lanes] = out
-    if final:
-        fill_cache(blocks, starts, own, devices, local_rows, owners_ref, *rest[1:])
-
-
-def fill_cache(blocks, starts, own, devices, local_rows, owners_ref, cache_ref, leading_ref):
-    total_blocks = owners_ref.shape[0]
-    blocks_dev = total_blocks // devices
-    block_len = local_rows // blocks_dev
-    count = jnp.int32(0)
-    for b in range(total_blocks):
-        hit = owners_ref[b] == own
-
-        @pl.when(hit)
-        def _(b=b, count=count):
-            leading_ref[count] = b
-
-        count = count + hit.astype(jnp.int32)
-    for r in range(blocks_dev):
-        block = leading_ref[r]
-        distance = (block // blocks_dev) ^ own
-        row = (block % blocks_dev) * block_len
-        for c, start in enumerate(starts):
-            for k in range(devices):
-                ref = blocks[c * devices + k]
-                inside = (distance == k) & (row >= start) & (row < start + ref.shape[0])
-
-                @pl.when(inside)
-                def _(ref=ref, start=start, row=row, r=r):
-                    source = pl.ds(pl.multiple_of(row - start, block_len), block_len)
-                    cache_ref[r * block_len : (r + 1) * block_len, :] = ref[source, :]
+                ).astype(jnp.bfloat16)
+        else:
+            for h, part, top, total, out in zip(some, parts_of, tops, totals, outs):
+                rest[0][h : h + 1, :] = top
+                rest[1][h : h + 1, :] = total
+                rest[2][part, :] = out
+    if carried:
+        cache_ref[...] = old[3][...]
+    fetch.wait()
+    own = slots_ref[slots_ref.shape[0] - 1]
+    blocks_dev = local_rows // block_len
+    for (k, c), ref in zip(held, parts):
+        at = 0
+        while at < ref.shape[0]:
+            row = starts[c] + at
+            size = min(block_len - row % block_len, ref.shape[0] - at)
+            slot = slots_ref[(own ^ k) * blocks_dev + row // block_len]
+
+            @pl.when(slot >= 0)
+            def _(ref=ref, at=at, row=row, size=size, slot=slot):
+                goal = pl.multiple_of(slot * block_len + row % block_len, 16)
+                block = ref[at : at + size, :]
+                cache_ref[pl.ds(goal, size)] = block.reshape((size,) + cache_ref.shape[1:])
+
+            at += size
 
 
 def chunked_device(activations, queries, key_weight, value_weight, lengths, owners, sizes):
@@ -384,31 +410,40 @@
         return pieces
 
     crossed = []
+    stays = [
+        pltpu.with_memory_space_constraint(a, pltpu.HBM)
+        for a in (key_weight, value_weight, activations, queries, lengths, owners)
+    ]
     for start, size in zip(starts, sizes):
-        crossed.append(swap(activations[start : start + size], "tp", far))
+        piece = activations[start : start + size]
+        crossed.append(swap(piece, "tp", far))
     near = spread_over({0: activations}, far // 2)
 
-    exponent = np.arange(HD // 2) * (2.0 / HD)
-    inverse = np.exp(-exponent * np.log(500000.0)).astype(np.float32)
-    inverse = jnp.asarray(np.concatenate([inverse, inverse])[None, :])
+    offsets = sorted(near)
     table = jax.ShapeDtypeStruct((local_rows, HD), jnp.float32)
-    cosines, sines, rotated = call(
-        prepare_body,
-        [table, table, jax.ShapeDtypeStruct(queries.shape, jnp.bfloat16)],
-        [SMEM, SMEM, VMEM, VMEM],
-    )(place, lengths, inverse, queries)
-    offsets = sorted(near)
-    stays = [pltpu.with_memory_space_constraint(a, pltpu.HBM) for a in (key_weight, value_weight, activations)]
     weights = jax.ShapeDtypeStruct((parts, width, kv_width), jnp.bfloat16)
-    keys, values, sums = call(
+    keys, values, sums, cosines, sines, rotated, facts, slots = call(
         functools.partial(early_body, offsets),
-        [weights, weights, jax.ShapeDtypeStruct((local_rows, 2 * kv_width), jnp.float32)],
-        [SMEM] + [ANY] * 3 + [VMEM] * (len(offsets) - 1),
+        [
+            weights,
+            weights,
+            jax.ShapeDtypeStruct((local_rows, 2 * kv_width), jnp.float32),
+            table,
+            table,
+            jax.ShapeDtypeStruct(queries.shape, queries.dtype),
+            jax.ShapeDtypeStruct((8, local_rows), jnp.int32),
+            jax.ShapeDtypeStruct((owners.shape[0] + 1,), jnp.int32),
+        ],
+        [SMEM] + [ANY] * 6 + [VMEM] * (len(offsets) - 1),
         scratch=[
             pltpu.VMEM(activations.shape, activations.dtype),
+            pltpu.VMEM(queries.shape, queries.dtype),
+            pltpu.SMEM(lengths.shape, jnp.int32),
+            pltpu.SMEM(owners.shape, jnp.int32),
             pltpu.SemaphoreType.DMA((2, parts)),
-            pltpu.SemaphoreType.DMA,
+            pltpu.SemaphoreType.DMA((4,)),
         ],
+        out_specs=[VMEM] * 7 + [SMEM],
     )(place, *stays, *[near[o] for o in offsets[1:]])
 
     arrived = []
@@ -441,25 +476,24 @@
         stages.append([(k, last) for k in range(half)])
     stages.append([(k, last) for k in range(half, devices)])
     state = ()
+    spans = (starts, local_rows * devices // owners.shape[0])
+    cache = jax.ShapeDtypeStruct((local_rows, kv_width // HD, 2 * HD), jnp.bfloat16)
+    query_width = queries.shape[1]
+    line = jax.ShapeDtypeStruct((query_width // HD, local_rows), jnp.float32)
     for n, held in enumerate(stages):
         final = n == len(stages) - 1
+        taken = [arrived[c][k] for k, c in held]
         if final:
-            taken = [block for blocks in arrived for block in blocks]
-            results = [
-                jax.ShapeDtypeStruct(queries.shape, jnp.bfloat16),
-                jax.ShapeDtypeStruct((local_rows, 2 * kv_width), jnp.bfloat16),
-            ]
+            results = [jax.ShapeDtypeStruct(queries.shape, jnp.bfloat16)]
         else:
-            taken = [arrived[c][k] for k, c in held]
-            results = [jax.ShapeDtypeStruct(queries.shape, jnp.float32)] * 3
+            results = [line, line, jax.ShapeDtypeStruct((query_width, local_rows), jnp.float32)]
         state = call(
-            functools.partial(attend_body, held, starts, n > 0, final, devices),
-            results,
-            [SMEM] * 3 + [VMEM] * (1 + len(taken) + len(state)),
-            scratch=[pltpu.SMEM((owners.shape[0] // devices,), jnp.int32)] if final else (),
-        )(place, lengths, owners, rotated, *taken, *state)
-    attention, cache = state
-    return attention, cache.reshape(local_rows, kv_width // HD, 2 * HD)
+            functools.partial(attend_body, held, spans, n > 0, final),
+            results + [cache],
+            [VMEM, ANY] + [VMEM] * (1 + len(taken) + len(state)),
+            scratch=[pltpu.SMEM(slots.shape, jnp.int32), pltpu.SemaphoreType.DMA],
+        )(facts, slots, rotated, *taken, *state)
+    return state
 
 
 def chunk_sizes(local_rows, block_len):

time: 40.1 us -> 38.8 us (0.968)
  Pallas kernels: 14 us -> 12.3 us
  waiting for transfers between devices: 9.71 us -> 10.7 us
  local copies, waits for them, and re-layouts: 1.77 us -> 1.06 us
    pallas_call x4 -> x3, Pallas kernels: 7.08 us -> 4.1 us  [chunked_device(): call(functools.partial(attend_body, held, spans, n > 0, final), results +...]
    pallas_call x1, Pallas kernels: 4.8 us -> 6.14 us  [chunked_device(): call(functools.partial(early_body, offsets), [weights, weights, jax.Shape...]
    ppermute x11, waiting for transfers between devices: 9.71 us -> 10.7 us  [swap(): return lax.ppermute(array, axis, [(i, i ^ distance) for i in range(count)])]
    reshape x1 -> x0, local copies, waits for them, and re-layouts: 0.69 us -> none  [chunked_device(): return (attention, cache.reshape(local_rows, kv_width // HD, 2 * HD))]
  transfers between devices with their start and end apart: 11 -> 11, of which waited for: 5 -> 5; matrix products, arithmetic and copies ran while one was open for 3% -> 3% of each run, Pallas kernels for 28% -> 27%
where the time goes in v4:
time: 38.8 us; the launch traced here: 38.6 us
  starting transfers between devices  13.7 us (35%)
  Pallas kernels  12.3 us (32%)
  waiting for transfers between devices  10.7 us (28%)
  local copies, waits for them, and re-layouts  1.06 us (3%)
  between operations  0.72 us (2%)
    ppermute x11, starting transfers between devices, swap(): return lax.ppermute(array, axis, [(i, i ^ distance) for i in range(count)])  13.7 us
    ppermute x11, waiting for transfers between devices, swap(): return lax.ppermute(array, axis, [(i, i ^ distance) for i in range(count)])  10.7 us
    pallas_call x1, Pallas kernels, chunked_device(): call(functools.partial(early_body, offsets), [weights, weights, jax.Shape...  6.14 us
    pallas_call x3, Pallas kernels, chunked_device(): call(functools.partial(attend_body, held, spans, n > 0, final), results +...  4.1 us
    pallas_call x2, Pallas kernels, chunked_device(): call(functools.partial(late_body, offsets, start), jax.ShapeDtypeStruct((...  1.11 us
    slice x1, local copies, waits for them, and re-layouts, chunked_device(): piece = activations[start:start + size]  1.06 us
    pallas_call x2, Pallas kernels, chunked_device(): call(functools.partial(far_body, far, start), jax.ShapeDtypeStruct((size,...  0.96 us
  transfers between devices with their start and end apart: 11, of which 5 were waited for; matrix products, arithmetic and copies ran while one was open for 3% of the time, Pallas kernels for 27%

profile of v4, /device:TPU:0, one launch (start us, length us, event | category | flops | bytes accessed | tf_op | source)
XLA Modules:
  0.0 38.6 jit_solution(11709763303437630501)
XLA Ops:
  0.6 0.6 %collective-permute-start = (bf16[128,2048]{1,0:T(8,128)(2,1)}, bf16[128,2048]{1,0:T(8,128)(2,1)S(1)}, u32[]{:S(2)}, u32[]{:S(2)}) collective-permute-start(bf16[128,2048]{1,0:T(8,128)(2,1)} %own_hbm.1), channel_id=1, source_target_pairs={{0,1},{1,0},{2,3},{3,2},{4,5},{5,4},{6,7},{7,6},{8,9},{9,8},{10,11... | collective-permute-start | bytes 1572872 | tf_op jit(solution)/shard_map/ppermute | solution.py:51
  1.2 1.1 %fusion = (bf16[64,2048]{1,0:T(8,128)(2,1)S(1)}, bf16[64,2048]{1,0:T(8,128)(2,1)S(1)}) fusion(bf16[128,2048]{1,0:T(8,128)(2,1)} %own_hbm.1), kind=kLoop, calls=%fused_computation.1 | loop fusion | bytes 1048576 | tf_op jit(solution)/shard_map/slice | solution.py:418
  2.3 2.6 %collective-permute-start.2 = (bf16[64,2048]{1,0:T(8,128)(2,1)S(1)}, bf16[64,2048]{1,0:T(8,128)(2,1)S(1)}, u32[]{:S(2)}, u32[]{:S(2)}) collective-permute-start(bf16[64,2048]{1,0:T(8,128)(2,1)S(1)} %get-tuple-element.38), channel_id=1, source_target_pairs={{0,2},{1,3},{2,0},{3,1},{4,6},{5,7},{6,4},{7,5},{8,10},{9,11},{10,... | collective-permute-start | bytes 786440 | tf_op jit(solution)/shard_map/ppermute | solution.py:51
  4.8 0.1 pad_add_fusion.place_ref
  4.9 0.0 collective-permute-done.refs_0_
  4.9 6.1 %shard_map.77 = (bf16[4,2048,256]{2,1,0:T(8,128)(2,1)S(1)}, bf16[4,2048,256]{2,1,0:T(8,128)(2,1)S(1)}, f32[128,512]{1,0:T(8,128)S(1)}, f32[128,128]{1,0:T(8,128)...) custom-call(s32[2]{0:T(128)S(1)} %pad_add_fusion.place_ref, ...), custom_call_target="tpu_custom_call" | custom-call | tf_op jit(solution)/shard_map/pallas_call | solution.py:425
  11.0 0.7 %collective-permute-done.2.piece_ref = bf16[64,2048]{1,0:T(8,128)(2,1)S(1)} collective-permute-done((bf16[64,2048]{1,0:T(8,128)(2,1)S(1)}, bf16[64,2048]{1,0:T(8,128)(2,1)S(1)}, u32[]{:S(2)}, u32[]{:S(2)}) %collective-permute-start.2) | collective-permute-done | bytes 262176 | tf_op jit(solution)/shard_map/ppermute | solution.py:51
  11.8 0.0 collective-permute-start.3
  11.8 1.7 %collective-permute-start.1 = (bf16[64,2048]{1,0:T(8,128)(2,1)S(1)}, bf16[64,2048]{1,0:T(8,128)(2,1)S(1)}, u32[]{:S(2)}, u32[]{:S(2)}) collective-permute-start(bf16[64,2048]{1,0:T(8,128)(2,1)S(1)} %get-tuple-element.39), channel_id=1, source_target_pairs={{0,2},{1,3},{2,0},{3,1},{4,6},{5,7},{6,4},{7,5},{8,10},{9,11},{10,... | collective-permute-start | bytes 786440 | tf_op jit(solution)/shard_map/ppermute | solution.py:51
  13.5 0.5 %shard_map.78.sums_ref = f32[64,512]{1,0:T(8,128)S(1)} custom-call(bf16[4,2048,256]{2,1,0:T(8,128)(2,1)S(1)} %get-tuple-element.23.keys_ref, bf16[4,2048,256]{2,1,0:T(8,128)(2,1)S(1)} %get-tuple-element.24.values_ref, f32[128,512]{1,0:T(8,128)S(1)} %get-tuple-element.25.sums_ref, bf16[64,2048]{1,0:T(8,128)(2,1)S(1)} %collective-permute-done.2.piece_ref), custom_call_target="tpu_custom_call" | custom-call | tf_op jit(solution)/shard_map/pallas_call | solution.py:455
  14.0 0.0 collective-permute-done.3.refs_0_
  14.0 0.6 %shard_map.79.refs_0_ = bf16[64,512]{1,0:T(8,128)(2,1)S(1)} custom-call(bf16[4,2048,256]{2,1,0:T(8,128)(2,1)S(1)} %get-tuple-element.23.keys_ref, bf16[4,2048,256]{2,1,0:T(8,128)(2,1)S(1)} %get-tuple-element.24.values_ref, f32[64,512]{1,0:T(8,128)S(1)} %shard_map.78.sums_ref, f32[128,128]{1,0:T(8,128)S(1)} %get-tuple-element.27.cos_ref, ...), custom_call_target="tpu_custom_call" | custom-call | tf_op jit(solution)/shard_map/pallas_call | solution.py:461
  14.6 5.9 %collective-permute-done.1.piece_ref = bf16[64,2048]{1,0:T(8,128)(2,1)S(1)} collective-permute-done((bf16[64,2048]{1,0:T(8,128)(2,1)S(1)}, bf16[64,2048]{1,0:T(8,128)(2,1)S(1)}, u32[]{:S(2)}, u32[]{:S(2)}) %collective-permute-start.1) | collective-permute-done | bytes 262176 | tf_op jit(solution)/shard_map/ppermute | solution.py:51
  20.5 0.0 collective-permute-start.4
  20.5 1.8 %collective-permute-start.8 = (bf16[64,512]{1,0:T(8,128)(2,1)S(1)}, bf16[64,512]{1,0:T(8,128)(2,1)S(1)}, u32[]{:S(2)}, u32[]{:S(2)}) collective-permute-start(bf16[64,512]{1,0:T(8,128)(2,1)S(1)} %shard_map.79.refs_0_), channel_id=1, source_target_pairs={{0,4},{4,0},{8,12},{12,8},{1,5},{5,1},{9,13},{13,9},{2,6},{6,2},{1... | collective-permute-start | bytes 196616 | tf_op jit(solution)/shard_map/ppermute | solution.py:51
  22.3 2.6 %collective-permute-start.9 = (bf16[64,512]{1,0:T(8,128)(2,1)S(1)}, bf16[64,512]{1,0:T(8,128)(2,1)S(1)}, u32[]{:S(2)}, u32[]{:S(2)}) collective-permute-start(bf16[64,512]{1,0:T(8,128)(2,1)S(1)} %shard_map.79.refs_0_), channel_id=1, source_target_pairs={{0,8},{4,12},{8,0},{12,4},{1,9},{5,13},{9,1},{13,5},{2,10},{6,14},... | collective-permute-start | bytes 196616 | tf_op jit(solution)/shard_map/ppermute | solution.py:51
  24.9 0.0 collective-permute-start.10
  24.9 0.5 %shard_map.80.sums_ref = f32[64,512]{1,0:T(8,128)S(1)} custom-call(bf16[4,2048,256]{2,1,0:T(8,128)(2,1)S(1)} %get-tuple-element.23.keys_ref, bf16[4,2048,256]{2,1,0:T(8,128)(2,1)S(1)} %get-tuple-element.24.values_ref, f32[128,512]{1,0:T(8,128)S(1)} %get-tuple-element.25.sums_ref, bf16[64,2048]{1,0:T(8,128)(2,1)S(1)} %collective-permute-done.1.piece_ref), custom_call_target="tpu_custom_call" | custom-call | tf_op jit(solution)/shard_map/pallas_call | solution.py:455
  25.4 0.0 collective-permute-done.4.refs_0_
  25.4 0.6 %shard_map.81.refs_0_ = bf16[64,512]{1,0:T(8,128)(2,1)S(1)} custom-call(bf16[4,2048,256]{2,1,0:T(8,128)(2,1)S(1)} %get-tuple-element.23.keys_ref, bf16[4,2048,256]{2,1,0:T(8,128)(2,1)S(1)} %get-tuple-element.24.values_ref, f32[64,512]{1,0:T(8,128)S(1)} %shard_map.80.sums_ref, f32[128,128]{1,0:T(8,128)S(1)} %get-tuple-element.27.cos_ref, ...), custom_call_target="tpu_custom_call" | custom-call | tf_op jit(solution)/shard_map/pallas_call | solution.py:461
  26.0 1.0 %collective-permute-start.7 = (bf16[64,512]{1,0:T(8,128)(2,1)S(1)}, bf16[64,512]{1,0:T(8,128)(2,1)S(1)}, u32[]{:S(2)}, u32[]{:S(2)}) collective-permute-start(bf16[64,512]{1,0:T(8,128)(2,1)S(1)} %shard_map.81.refs_0_), channel_id=1, source_target_pairs={{0,4},{4,0},{8,12},{12,8},{1,5},{5,1},{9,13},{13,9},{2,6},{6,2},{1... | collective-permute-start | bytes 196616 | tf_op jit(solution)/shard_map/ppermute | solution.py:51
  26.9 3.5 %collective-permute-start.5 = (bf16[64,512]{1,0:T(8,128)(2,1)S(1)}, bf16[64,512]{1,0:T(8,128)(2,1)S(1)}, u32[]{:S(2)}, u32[]{:S(2)}) collective-permute-start(bf16[64,512]{1,0:T(8,128)(2,1)S(1)} %shard_map.81.refs_0_), channel_id=1, source_target_pairs={{0,8},{4,12},{8,0},{12,4},{1,9},{5,13},{9,1},{13,5},{2,10},{6,14},... | collective-permute-start | bytes 196616 | tf_op jit(solution)/shard_map/ppermute | solution.py:51
  30.4 0.0 collective-permute-done.8.refs_1_
  30.4 0.0 collective-permute-start.6
  30.4 0.0 collective-permute-done.9.refs_2_
  30.4 1.1 %collective-permute-done.10.refs_3_ = bf16[64,512]{1,0:T(8,128)(2,1)S(1)} collective-permute-done((bf16[64,512]{1,0:T(8,128)(2,1)S(1)}, bf16[64,512]{1,0:T(8,128)(2,1)S(1)}, u32[]{:S(2)}, u32[]{:S(2)}) %collective-permute-start.10) | collective-permute-done | bytes 65568 | tf_op jit(solution)/shard_map/ppermute | solution.py:51
  31.6 1.2 %shard_map.82 = (f32[16,128]{1,0:T(8,128)S(1)}, f32[16,128]{1,0:T(8,128)S(1)}, f32[2048,128]{1,0:T(8,128)S(1)}, bf16[128,2,256]{2,1,0:T(2,128)(2,1)S(1)}) custom-call(s32[8,128]{1,0:T(8,128)S(1)} %get-tuple-element.20.facts_ref, s32[17]{0:T(128)S(1)} %get-tuple-element.21.slots_hbm, bf16[128,2048]{1,0:T(8,128)(2,1)S(1)} %get-tuple-element.22.rotated_ref, ...), custom_call_target="tpu_custom_call" | custom-call | tf_op jit(solution)/shard_map/pallas_call | solution.py:490
  32.8 0.0 collective-permute-done.7.refs_1_
  32.8 0.8 %shard_map.83 = (f32[16,128]{1,0:T(8,128)S(1)}, f32[16,128]{1,0:T(8,128)S(1)}, f32[2048,128]{1,0:T(8,128)S(1)}, bf16[128,2,256]{2,1,0:T(2,128)(2,1)S(1)}) custom-call(s32[8,128]{1,0:T(8,128)S(1)} %get-tuple-element.20.facts_ref, s32[17]{0:T(128)S(1)} %get-tuple-element.21.slots_hbm, bf16[128,2048]{1,0:T(8,128)(2,1)S(1)} %get-tuple-element.22.rotated_ref, ...), custom_call_target="tpu_custom_call" | custom-call | tf_op jit(solution)/shard_map/pallas_call | solution.py:490
  33.7 1.9 %collective-permute-done.5.refs_0_ = bf16[64,512]{1,0:T(8,128)(2,1)S(1)} collective-permute-done((bf16[64,512]{1,0:T(8,128)(2,1)S(1)}, bf16[64,512]{1,0:T(8,128)(2,1)S(1)}, u32[]{:S(2)}, u32[]{:S(2)}) %collective-permute-start.5) | collective-permute-done | bytes 65568 | tf_op jit(solution)/shard_map/ppermute | solution.py:51
  35.6 1.0 %collective-permute-done.6.refs_1_ = bf16[64,512]{1,0:T(8,128)(2,1)S(1)} collective-permute-done((bf16[64,512]{1,0:T(8,128)(2,1)S(1)}, bf16[64,512]{1,0:T(8,128)(2,1)S(1)}, u32[]{:S(2)}, u32[]{:S(2)}) %collective-permute-start.6) | collective-permute-done | bytes 65568 | tf_op jit(solution)/shard_map/ppermute | solution.py:51
  36.6 2.0 %shard_map.84 = (bf16[128,2048]{1,0:T(8,128)(2,1)}, bf16[128,2,256]{2,1,0:T(2,128)(2,1)}) custom-call(s32[8,128]{1,0:T(8,128)S(1)} %get-tuple-element.20.facts_ref, s32[17]{0:T(128)S(1)} %get-tuple-element.21.slots_hbm, bf16[128,2048]{1,0:T(8,128)(2,1)S(1)} %get-tuple-element.22.rotated_ref, bf16[64,512]{1,0:T(8,128)(2,1)S(1)} %collective-permute-done.5.refs_0_, ...), custom_call_target="tpu_custom_call" | custom-call | tf_op jit(solution)/shard_map/pallas_call | solution.py:490
Async XLA Ops:
  0.6 4.3 %collective-permute-start = (bf16[128,2048]{1,0:T(8,128)(2,1)}, bf16[128,2048]{1,0:T(8,128)(2,1)S(1)}, u32[]{:S(2)}, u32[]{:S(2)}) collective-permute-start(bf16[128,2048]{1,0:T(8,128)(2,1)} %own_hbm.1), channel_id=1, source_target_pairs={{0,1},{1,0},{2,3},{3,2},{4,5},{5,4},{6,7},{7,6},{8,9},{9,8},{10,11... | collective-permute-start | bytes 1572872 | tf_op jit(solution)/shard_map/ppermute | solution.py:51
  2.3 9.5 %collective-permute-start.2 = (bf16[64,2048]{1,0:T(8,128)(2,1)S(1)}, bf16[64,2048]{1,0:T(8,128)(2,1)S(1)}, u32[]{:S(2)}, u32[]{:S(2)}) collective-permute-start(bf16[64,2048]{1,0:T(8,128)(2,1)S(1)} %get-tuple-element.38), channel_id=1, source_target_pairs={{0,2},{1,3},{2,0},{3,1},{4,6},{5,7},{6,4},{7,5},{8,10},{9,11},{10,... | collective-permute-start | bytes 786440 | tf_op jit(solution)/shard_map/ppermute | solution.py:51
  11.8 2.2 %collective-permute-start.3 = (bf16[64,2048]{1,0:T(8,128)(2,1)S(1)}, bf16[64,2048]{1,0:T(8,128)(2,1)S(1)}, u32[]{:S(2)}, u32[]{:S(2)}) collective-permute-start(bf16[64,2048]{1,0:T(8,128)(2,1)S(1)} %collective-permute-done.2.piece_ref), channel_id=1, source_target_pairs={{0,1},{1,0},{2,3},{3,2},{4,5},{5,4},{6,7},{7,6},{8,9},{9,8},{10,11... | collective-permute-start | bytes 786440 | tf_op jit(solution)/shard_map/ppermute | solution.py:51
  11.8 8.7 %collective-permute-start.1 = (bf16[64,2048]{1,0:T(8,128)(2,1)S(1)}, bf16[64,2048]{1,0:T(8,128)(2,1)S(1)}, u32[]{:S(2)}, u32[]{:S(2)}) collective-permute-start(bf16[64,2048]{1,0:T(8,128)(2,1)S(1)} %get-tuple-element.39), channel_id=1, source_target_pairs={{0,2},{1,3},{2,0},{3,1},{4,6},{5,7},{6,4},{7,5},{8,10},{9,11},{10,... | collective-permute-start | bytes 786440 | tf_op jit(solution)/shard_map/ppermute | solution.py:51
  20.5 4.9 %collective-permute-start.4 = (bf16[64,2048]{1,0:T(8,128)(2,1)S(1)}, bf16[64,2048]{1,0:T(8,128)(2,1)S(1)}, u32[]{:S(2)}, u32[]{:S(2)}) collective-permute-start(bf16[64,2048]{1,0:T(8,128)(2,1)S(1)} %collective-permute-done.1.piece_ref), channel_id=1, source_target_pairs={{0,1},{1,0},{2,3},{3,2},{4,5},{5,4},{6,7},{7,6},{8,9},{9,8},{10,11... | collective-permute-start | bytes 786440 | tf_op jit(solution)/shard_map/ppermute | solution.py:51
  20.5 9.9 %collective-permute-start.8 = (bf16[64,512]{1,0:T(8,128)(2,1)S(1)}, bf16[64,512]{1,0:T(8,128)(2,1)S(1)}, u32[]{:S(2)}, u32[]{:S(2)}) collective-permute-start(bf16[64,512]{1,0:T(8,128)(2,1)S(1)} %shard_map.79.refs_0_), channel_id=1, source_target_pairs={{0,4},{4,0},{8,12},{12,8},{1,5},{5,1},{9,13},{13,9},{2,6},{6,2},{1... | collective-permute-start | bytes 196616 | tf_op jit(solution)/shard_map/ppermute | solution.py:51
  22.3 8.1 %collective-permute-start.9 = (bf16[64,512]{1,0:T(8,128)(2,1)S(1)}, bf16[64,512]{1,0:T(8,128)(2,1)S(1)}, u32[]{:S(2)}, u32[]{:S(2)}) collective-permute-start(bf16[64,512]{1,0:T(8,128)(2,1)S(1)} %shard_map.79.refs_0_), channel_id=1, source_target_pairs={{0,8},{4,12},{8,0},{12,4},{1,9},{5,13},{9,1},{13,5},{2,10},{6,14},... | collective-permute-start | bytes 196616 | tf_op jit(solution)/shard_map/ppermute | solution.py:51
  24.9 6.7 %collective-permute-start.10 = (bf16[64,512]{1,0:T(8,128)(2,1)S(1)}, bf16[64,512]{1,0:T(8,128)(2,1)S(1)}, u32[]{:S(2)}, u32[]{:S(2)}) collective-permute-start(bf16[64,512]{1,0:T(8,128)(2,1)S(1)} %shard_map.79.refs_0_), channel_id=1, source_target_pairs={{0,12},{4,8},{8,4},{12,0},{1,13},{5,9},{9,5},{13,1},{2,14},{6,10},... | collective-permute-start | bytes 196616 | tf_op jit(solution)/shard_map/ppermute | solution.py:51
  26.0 6.8 %collective-permute-start.7 = (bf16[64,512]{1,0:T(8,128)(2,1)S(1)}, bf16[64,512]{1,0:T(8,128)(2,1)S(1)}, u32[]{:S(2)}, u32[]{:S(2)}) collective-permute-start(bf16[64,512]{1,0:T(8,128)(2,1)S(1)} %shard_map.81.refs_0_), channel_id=1, source_target_pairs={{0,4},{4,0},{8,12},{12,8},{1,5},{5,1},{9,13},{13,9},{2,6},{6,2},{1... | collective-permute-start | bytes 196616 | tf_op jit(solution)/shard_map/ppermute | solution.py:51
  26.9 8.7 %collective-permute-start.5 = (bf16[64,512]{1,0:T(8,128)(2,1)S(1)}, bf16[64,512]{1,0:T(8,128)(2,1)S(1)}, u32[]{:S(2)}, u32[]{:S(2)}) collective-permute-start(bf16[64,512]{1,0:T(8,128)(2,1)S(1)} %shard_map.81.refs_0_), channel_id=1, source_target_pairs={{0,8},{4,12},{8,0},{12,4},{1,9},{5,13},{9,1},{13,5},{2,10},{6,14},... | collective-permute-start | bytes 196616 | tf_op jit(solution)/shard_map/ppermute | solution.py:51
  30.4 6.2 %collective-permute-start.6 = (bf16[64,512]{1,0:T(8,128)(2,1)S(1)}, bf16[64,512]{1,0:T(8,128)(2,1)S(1)}, u32[]{:S(2)}, u32[]{:S(2)}) collective-permute-start(bf16[64,512]{1,0:T(8,128)(2,1)S(1)} %shard_map.81.refs_0_), channel_id=1, source_target_pairs={{0,12},{4,8},{8,4},{12,0},{1,13},{5,9},{9,5},{13,1},{2,14},{6,10},... | collective-permute-start | bytes 196616 | tf_op jit(solution)/shard_map/ppermute | solution.py:51

commit v5 on v4

--- a/solution.py
+++ b/solution.py
@@ -10,7 +10,8 @@
 
 HD = 128
 LOW = -1e30
-TOGETHER = 16
+SHARE = 2
+STAGES = ('acg', 'bf', 'd', 'e')
 MIB = 1 << 20
 VMEM = pl.BlockSpec(memory_space=pltpu.VMEM)
 SMEM = pl.BlockSpec(memory_space=pltpu.SMEM)
@@ -272,7 +273,7 @@
 
 
 def late_body(offsets, start, keys_ref, values_ref, sums_ref, cos_ref, sin_ref, *refs):
-    packed_ref = refs[-1]
+    *refs, packed_ref = refs
     size = packed_ref.shape[0]
     kv_width = keys_ref.shape[2]
     rows = slice(start, start + size)
@@ -284,13 +285,15 @@
     for h in range(kv_width // HD):
         part = slice(h * HD, (h + 1) * HD)
         base = 2 * h * HD
-        packed_ref[:, base : base + HD] = turn(sums[0][:, part], cosines, sines).astype(jnp.bfloat16)
-        packed_ref[:, base + HD : base + 2 * HD] = sums[kv_width][:, part].astype(jnp.bfloat16)
-
-
-def attend_body(held, spans, carried, final, facts_ref, slots_hbm, rotated_ref, *refs):
+        both = (turn(sums[0][:, part], cosines, sines), sums[kv_width][:, part])
+        for side, block in enumerate(both):
+            goal = slice(base + side * HD, base + (side + 1) * HD)
+            block = block.astype(jnp.bfloat16)
+            packed_ref[:, goal] = block
+
+
+def attend_body(held, block_len, carried, final, facts_ref, slots_hbm, rotated_ref, *refs):
     local_rows, width = rotated_ref.shape
-    starts, block_len = spans
     parts = refs[: len(held)]
     rest = refs[len(held) :]
     old = rest[:4] if carried else ()
@@ -304,10 +307,11 @@
     own = facts_ref[2:3, :]
     key_rows = order
     at = 0
-    for (k, c), ref in zip(held, parts):
-        moved = order + ((own ^ k) * local_rows + (starts[c] - at))
-        key_rows = jnp.where(order >= at, moved, key_rows) if at else moved
-        at += ref.shape[0]
+    for segments in held:
+        for k, first, size in segments:
+            moved = order + ((own ^ k) * local_rows + (first - at))
+            key_rows = jnp.where(order >= at, moved, key_rows) if at else moved
+            at += size
     allowed = (key_rows >= facts_ref[0:1, :]) & (key_rows <= facts_ref[1:2, :])
     scale = float(HD**-0.5 * np.log2(np.e))
     kv_heads = parts[0].shape[1] // (2 * HD)
@@ -324,8 +328,8 @@
         keys.append(jnp.concatenate([ref[:, base : base + HD] for ref in parts], axis=0))
         value = jnp.concatenate([ref[:, base + HD : base + 2 * HD] for ref in parts], axis=0)
         values.append(value.T)
-    for at in range(0, query_heads, TOGETHER):
-        some = range(query_heads)[at : at + TOGETHER]
+    for at in (0,):
+        some = range(query_heads)
         parts_of = [slice(h * HD, (h + 1) * HD) for h in some]
         scores = [
             lax.dot_general(
@@ -377,20 +381,30 @@
     fetch.wait()
     own = slots_ref[slots_ref.shape[0] - 1]
     blocks_dev = local_rows // block_len
-    for (k, c), ref in zip(held, parts):
-        at = 0
-        while at < ref.shape[0]:
-            row = starts[c] + at
-            size = min(block_len - row % block_len, ref.shape[0] - at)
-            slot = slots_ref[(own ^ k) * blocks_dev + row // block_len]
-
-            @pl.when(slot >= 0)
-            def _(ref=ref, at=at, row=row, size=size, slot=slot):
-                goal = pl.multiple_of(slot * block_len + row % block_len, 16)
-                block = ref[at : at + size, :]
-                cache_ref[pl.ds(goal, size)] = block.reshape((size,) + cache_ref.shape[1:])
-
-            at += size
+    for segments, ref in zip(held, parts):
+        before = 0
+        for k, first, length in segments:
+            at = 0
+            while at < length:
+                row = first + at
+                size = min(block_len - row % block_len, length - at)
+                slot = slots_ref[(own ^ k) * blocks_dev + row // block_len]
+
+                @pl.when(slot >= 0)
+                def _(ref=ref, at=before + at, row=row, size=size, slot=slot):
+                    goal = pl.multiple_of(slot * block_len + row % block_len, 16)
+                    block = ref[at : at + size, :]
+                    cache_ref[pl.ds(goal, size)] = block.reshape((size,) + cache_ref.shape[1:])
+
+                at += size
+            before += length
+
+
+def join_body(*refs):
+    at = 0
+    for ref in refs[:-1]:
+        refs[-1][at : at + ref.shape[0], :] = ref[...]
+        at += ref.shape[0]
 
 
 def chunked_device(activations, queries, key_weight, value_weight, lengths, owners, sizes):
@@ -464,31 +478,46 @@
             [VMEM] * (5 + len(offsets)),
         )(keys, values, partial, cosines, sines, *[late[o] for o in offsets])
         ready = packed
-        blocks = [packed]
-        for k in range(1, devices):
-            blocks.append(swap(packed, "seq", k))
-        arrived.append(blocks)
-
-    last = len(sizes) - 1
-    half = devices // 2
-    stages = [[(k, c) for k in range(devices)] for c in range(last)]
-    if half:
-        stages.append([(k, last) for k in range(half)])
-    stages.append([(k, last) for k in range(half, devices)])
+        arrived.append(packed)
+
+    def spread(block, k):
+        return swap(block, "seq", k)
+
+    (first_at, second_at), (first_size, second_size) = starts, sizes
+    mine, mine_too = arrived
+    across = spread(mine, 2)
+    across_too = spread(mine_too, 2)
+    joined = call(
+        join_body, jax.ShapeDtypeStruct((local_rows, 2 * kv_width), jnp.bfloat16), [VMEM] * 2
+    )(across, mine_too)
+    near_by = spread(mine, 1)
+    beside = spread(joined, 1)
+    opposite = spread(mine_too, 3)
+    blocks = {
+        "a": (mine, ((0, first_at, first_size),)),
+        "b": (mine_too, ((0, second_at, second_size),)),
+        "c": (across, ((2, first_at, first_size),)),
+        "d": (across_too, ((2, second_at, second_size),)),
+        "e": (beside, ((3, first_at, first_size), (1, second_at, second_size))),
+        "g": (near_by, ((1, first_at, first_size),)),
+        "f": (opposite, ((3, second_at, second_size),)),
+    }
+    stages = STAGES
     state = ()
-    spans = (starts, local_rows * devices // owners.shape[0])
+    block_len = local_rows * devices // owners.shape[0]
     cache = jax.ShapeDtypeStruct((local_rows, kv_width // HD, 2 * HD), jnp.bfloat16)
     query_width = queries.shape[1]
     line = jax.ShapeDtypeStruct((query_width // HD, local_rows), jnp.float32)
     for n, held in enumerate(stages):
         final = n == len(stages) - 1
-        taken = [arrived[c][k] for k, c in held]
+        taken = [blocks[name][0] for name in held]
+        held = [blocks[name][1] for name in held]
         if final:
             results = [jax.ShapeDtypeStruct(queries.shape, jnp.bfloat16)]
         else:
             results = [line, line, jax.ShapeDtypeStruct((query_width, local_rows), jnp.float32)]
         state = call(
-            functools.partial(attend_body, held, spans, n > 0, final),
+            functools.partial(attend_body, held, block_len, n > 0, final),
             results + [cache],
             [VMEM, ANY] + [VMEM] * (1 + len(taken) + len(state)),
             scratch=[pltpu.SMEM(slots.shape, jnp.int32), pltpu.SemaphoreType.DMA],
@@ -497,7 +526,7 @@
 
 
 def chunk_sizes(local_rows, block_len):
-    first = (local_rows // block_len // 2) * block_len
+    first = max(1, local_rows // block_len * SHARE // 4) * block_len
     return [first, local_rows - first]
 
 
@@ -507,7 +536,7 @@
     parts = lax.axis_size("tp")
     blocks_dev = owners.shape[0] // devices
     block_len = local_rows // blocks_dev
-    few = devices <= 8 and 1 < parts <= 8 and is_power(devices) and is_power(parts)
+    few = devices == 4 and 1 < parts <= 8 and is_power(parts)
     if not few or block_len % 16 or blocks_dev < 2:
         return gathered_device(activations, queries, key_weight, value_weight, lengths, owners)
     sizes = chunk_sizes(local_rows, block_len)

time: 38.8 us -> 42.9 us (1.11)
  waiting for transfers between devices: 10.7 us -> 14.4 us
  Pallas kernels: 12.3 us -> 13.1 us
    ppermute x11 -> x10, waiting for transfers between devices: 10.7 us -> 14.4 us  [swap(): return lax.ppermute(array, axis, [(i, i ^ distance) for i in range(count)])]
    pallas_call x3 -> x5, Pallas kernels: 4.1 us -> 4.89 us  [the longest x4 4.88 us: chunked_device(): call(functools.partial(attend_body, held, block_len, n > 0, final), resul...]
    ppermute x11 -> x10, starting transfers between devices: 13.7 us -> 13.3 us  [swap(): return lax.ppermute(array, axis, [(i, i ^ distance) for i in range(count)])]
  transfers between devices with their start and end apart: 11 -> 10, of which waited for: 5 -> 6; matrix products, arithmetic and copies ran while one was open for 3% -> 3% of each run, Pallas kernels for 27% -> 26%
where the time goes in v5:
time: 42.9 us; the launch traced here: 42.7 us
  waiting for transfers between devices  14.4 us (34%)
  starting transfers between devices  13.3 us (31%)
  Pallas kernels  13.1 us (31%)
  local copies, waits for them, and re-layouts  1.06 us (2%)
  between operations  0.72 us (2%)
    ppermute x10, waiting for transfers between devices, swap(): return lax.ppermute(array, axis, [(i, i ^ distance) for i in range(count)])  14.4 us
    ppermute x10, starting transfers between devices, swap(): return lax.ppermute(array, axis, [(i, i ^ distance) for i in range(count)])  13.3 us
    pallas_call x1, Pallas kernels, chunked_device(): call(functools.partial(early_body, offsets), [weights, weights, jax.Shape...  6.14 us
    pallas_call x4, Pallas kernels, chunked_device(): call(functools.partial(attend_body, held, block_len, n > 0, final), resul...  4.88 us
    pallas_call x2, Pallas kernels, chunked_device(): call(functools.partial(late_body, offsets, start), jax.ShapeDtypeStruct((...  1.11 us
    slice x1, local copies, waits for them, and re-layouts, chunked_device(): piece = activations[start:start + size]  1.06 us
    pallas_call x2, Pallas kernels, chunked_device(): call(functools.partial(far_body, far, start), jax.ShapeDtypeStruct((size,...  0.96 us
  transfers between devices with their start and end apart: 10, of which 6 were waited for; matrix products, arithmetic and copies ran while one was open for 3% of the time, Pallas kernels for 26%

profile of v5, /device:TPU:0, one launch (start us, length us, event | category | flops | bytes accessed | tf_op | source)
XLA Modules:
  0.0 42.7 jit_solution(15329547690248783018)
XLA Ops:
  0.6 0.6 %collective-permute-start = (bf16[128,2048]{1,0:T(8,128)(2,1)}, bf16[128,2048]{1,0:T(8,128)(2,1)S(1)}, u32[]{:S(2)}, u32[]{:S(2)}) collective-permute-start(bf16[128,2048]{1,0:T(8,128)(2,1)} %own_hbm.1), channel_id=1, source_target_pairs={{0,1},{1,0},{2,3},{3,2},{4,5},{5,4},{6,7},{7,6},{8,9},{9,8},{10,11... | collective-permute-start | bytes 1572872 | tf_op jit(solution)/shard_map/ppermute | solution.py:52
  1.2 1.1 %fusion = (bf16[64,2048]{1,0:T(8,128)(2,1)S(1)}, bf16[64,2048]{1,0:T(8,128)(2,1)S(1)}) fusion(bf16[128,2048]{1,0:T(8,128)(2,1)} %own_hbm.1), kind=kLoop, calls=%fused_computation.1 | loop fusion | bytes 1048576 | tf_op jit(solution)/shard_map/slice | solution.py:432
  2.3 2.6 %collective-permute-start.1 = (bf16[64,2048]{1,0:T(8,128)(2,1)S(1)}, bf16[64,2048]{1,0:T(8,128)(2,1)S(1)}, u32[]{:S(2)}, u32[]{:S(2)}) collective-permute-start(bf16[64,2048]{1,0:T(8,128)(2,1)S(1)} %get-tuple-element.47), channel_id=1, source_target_pairs={{0,2},{1,3},{2,0},{3,1},{4,6},{5,7},{6,4},{7,5},{8,10},{9,11},{10,... | collective-permute-start | bytes 786440 | tf_op jit(solution)/shard_map/ppermute | solution.py:52
  4.8 0.1 pad_add_fusion.place_ref
  4.9 0.0 collective-permute-done.refs_0_
  4.9 6.1 %shard_map.77 = (bf16[4,2048,256]{2,1,0:T(8,128)(2,1)S(1)}, bf16[4,2048,256]{2,1,0:T(8,128)(2,1)S(1)}, f32[128,512]{1,0:T(8,128)S(1)}, f32[128,128]{1,0:T(8,128)...) custom-call(s32[2]{0:T(128)S(1)} %pad_add_fusion.place_ref, ...), custom_call_target="tpu_custom_call" | custom-call | tf_op jit(solution)/shard_map/pallas_call | solution.py:439
  11.0 0.7 %collective-permute-done.1.piece_ref = bf16[64,2048]{1,0:T(8,128)(2,1)S(1)} collective-permute-done((bf16[64,2048]{1,0:T(8,128)(2,1)S(1)}, bf16[64,2048]{1,0:T(8,128)(2,1)S(1)}, u32[]{:S(2)}, u32[]{:S(2)}) %collective-permute-start.1) | collective-permute-done | bytes 262176 | tf_op jit(solution)/shard_map/ppermute | solution.py:52
  11.8 0.0 collective-permute-start.2
  11.8 1.7 %collective-permute-start.4 = (bf16[64,2048]{1,0:T(8,128)(2,1)S(1)}, bf16[64,2048]{1,0:T(8,128)(2,1)S(1)}, u32[]{:S(2)}, u32[]{:S(2)}) collective-permute-start(bf16[64,2048]{1,0:T(8,128)(2,1)S(1)} %get-tuple-element.46), channel_id=1, source_target_pairs={{0,2},{1,3},{2,0},{3,1},{4,6},{5,7},{6,4},{7,5},{8,10},{9,11},{10,... | collective-permute-start | bytes 786440 | tf_op jit(solution)/shard_map/ppermute | solution.py:52
  13.5 0.5 %shard_map.78.sums_ref = f32[64,512]{1,0:T(8,128)S(1)} custom-call(bf16[4,2048,256]{2,1,0:T(8,128)(2,1)S(1)} %get-tuple-element.27.keys_ref, bf16[4,2048,256]{2,1,0:T(8,128)(2,1)S(1)} %get-tuple-element.28.values_ref, f32[128,512]{1,0:T(8,128)S(1)} %get-tuple-element.29.sums_ref, bf16[64,2048]{1,0:T(8,128)(2,1)S(1)} %collective-permute-done.1.piece_ref), custom_call_target="tpu_custom_call" | custom-call | tf_op jit(solution)/shard_map/pallas_call | solution.py:469
  14.0 0.0 collective-permute-done.2.refs_0_
  14.0 0.6 %shard_map.79.refs_0_ = bf16[64,512]{1,0:T(8,128)(2,1)S(1)} custom-call(bf16[4,2048,256]{2,1,0:T(8,128)(2,1)S(1)} %get-tuple-element.27.keys_ref, bf16[4,2048,256]{2,1,0:T(8,128)(2,1)S(1)} %get-tuple-element.28.values_ref, f32[64,512]{1,0:T(8,128)S(1)} %shard_map.78.sums_ref, f32[128,128]{1,0:T(8,128)S(1)} %get-tuple-element.31.cos_ref, ...), custom_call_target="tpu_custom_call" | custom-call | tf_op jit(solution)/shard_map/pallas_call | solution.py:475
  14.6 5.9 %collective-permute-done.4.piece_ref = bf16[64,2048]{1,0:T(8,128)(2,1)S(1)} collective-permute-done((bf16[64,2048]{1,0:T(8,128)(2,1)S(1)}, bf16[64,2048]{1,0:T(8,128)(2,1)S(1)}, u32[]{:S(2)}, u32[]{:S(2)}) %collective-permute-start.4) | collective-permute-done | bytes 262176 | tf_op jit(solution)/shard_map/ppermute | solution.py:52
  20.5 0.0 collective-permute-start.5
  20.5 2.8 %collective-permute-start.3 = (bf16[64,512]{1,0:T(8,128)(2,1)S(1)}, bf16[64,512]{1,0:T(8,128)(2,1)S(1)}, u32[]{:S(2)}, u32[]{:S(2)}) collective-permute-start(bf16[64,512]{1,0:T(8,128)(2,1)S(1)} %shard_map.79.refs_0_), channel_id=1, source_target_pairs={{0,8},{4,12},{8,0},{12,4},{1,9},{5,13},{9,1},{13,5},{2,10},{6,14},... | collective-permute-start | bytes 196616 | tf_op jit(solution)/shard_map/ppermute | solution.py:52
  23.3 0.5 %shard_map.80.sums_ref = f32[64,512]{1,0:T(8,128)S(1)} custom-call(bf16[4,2048,256]{2,1,0:T(8,128)(2,1)S(1)} %get-tuple-element.27.keys_ref, bf16[4,2048,256]{2,1,0:T(8,128)(2,1)S(1)} %get-tuple-element.28.values_ref, f32[128,512]{1,0:T(8,128)S(1)} %get-tuple-element.29.sums_ref, bf16[64,2048]{1,0:T(8,128)(2,1)S(1)} %collective-permute-done.4.piece_ref), custom_call_target="tpu_custom_call" | custom-call | tf_op jit(solution)/shard_map/pallas_call | solution.py:469
  23.8 0.0 collective-permute-done.5.refs_0_
  23.8 0.6 %shard_map.81.refs_1_.refs_0_ = bf16[64,512]{1,0:T(8,128)(2,1)S(1)} custom-call(bf16[4,2048,256]{2,1,0:T(8,128)(2,1)S(1)} %get-tuple-element.27.keys_ref, bf16[4,2048,256]{2,1,0:T(8,128)(2,1)S(1)} %get-tuple-element.28.values_ref, f32[64,512]{1,0:T(8,128)S(1)} %shard_map.80.sums_ref, f32[128,128]{1,0:T(8,128)S(1)} %get-tuple-element.31.cos_ref, ...), custom_call_target="tpu_custom_call" | custom-call | tf_op jit(solution)/shard_map/pallas_call | solution.py:475
  24.4 3.1 %collective-permute-done.3.refs_0_.refs_1_ = bf16[64,512]{1,0:T(8,128)(2,1)S(1)} collective-permute-done((bf16[64,512]{1,0:T(8,128)(2,1)S(1)}, bf16[64,512]{1,0:T(8,128)(2,1)S(1)}, u32[]{:S(2)}, u32[]{:S(2)}) %collective-permute-start.3) | collective-permute-done | bytes 65568 | tf_op jit(solution)/shard_map/ppermute | solution.py:52
  27.5 0.8 %collective-permute-start.6 = (bf16[128,512]{1,0:T(8,128)(2,1)S(1)}, bf16[128,512]{1,0:T(8,128)(2,1)S(1)}, u32[]{:S(2)}, u32[]{:S(2)}) collective-permute-start(bf16[128,512]{1,0:T(8,128)(2,1)S(1)} %shard_map.82), channel_id=1, source_target_pairs={{0,4},{4,0},{8,12},{12,8},{1,5},{5,1},{9,13},{13,9},{2,6},{6,2},{1... | collective-permute-start | bytes 393224 | tf_op jit(solution)/shard_map/ppermute | solution.py:52
  28.3 1.3 %collective-permute-start.9 = (bf16[64,512]{1,0:T(8,128)(2,1)S(1)}, bf16[64,512]{1,0:T(8,128)(2,1)S(1)}, u32[]{:S(2)}, u32[]{:S(2)}) collective-permute-start(bf16[64,512]{1,0:T(8,128)(2,1)S(1)} %shard_map.79.refs_0_), channel_id=1, source_target_pairs={{0,4},{4,0},{8,12},{12,8},{1,5},{5,1},{9,13},{13,9},{2,6},{6,2},{1... | collective-permute-start | bytes 196616 | tf_op jit(solution)/shard_map/ppermute | solution.py:52
  29.6 3.5 %collective-permute-start.8 = (bf16[64,512]{1,0:T(8,128)(2,1)S(1)}, bf16[64,512]{1,0:T(8,128)(2,1)S(1)}, u32[]{:S(2)}, u32[]{:S(2)}) collective-permute-start(bf16[64,512]{1,0:T(8,128)(2,1)S(1)} %shard_map.81.refs_1_.refs_0_), channel_id=1, source_target_pairs={{0,12},{4,8},{8,4},{12,0},{1,13},{5,9},{9,5},{13,1},{2,14},{6,10},... | collective-permute-start | bytes 196616 | tf_op jit(solution)/shard_map/ppermute | solution.py:52
  33.2 0.0 collective-permute-start.7
  33.2 0.3 collective-permute-done.9.refs_2_
  33.5 1.3 %shard_map.83 = (f32[16,128]{1,0:T(8,128)S(1)}, f32[16,128]{1,0:T(8,128)S(1)}, f32[2048,128]{1,0:T(8,128)S(1)}, bf16[128,2,256]{2,1,0:T(2,128)(2,1)S(1)}) custom-call(s32[8,128]{1,0:T(8,128)S(1)} %get-tuple-element.24.facts_ref, s32[17]{0:T(128)S(1)} %get-tuple-element.25.slots_hbm, bf16[128,2048]{1,0:T(8,128)(2,1)S(1)} %get-tuple-element.26.rotated_ref, ...), custom_call_target="tpu_custom_call" | custom-call | tf_op jit(solution)/shard_map/pallas_call | solution.py:519
  34.8 3.6 %collective-permute-done.8.refs_1_ = bf16[64,512]{1,0:T(8,128)(2,1)S(1)} collective-permute-done((bf16[64,512]{1,0:T(8,128)(2,1)S(1)}, bf16[64,512]{1,0:T(8,128)(2,1)S(1)}, u32[]{:S(2)}, u32[]{:S(2)}) %collective-permute-start.8) | collective-permute-done | bytes 65568 | tf_op jit(solution)/shard_map/ppermute | solution.py:52
  38.4 0.8 %shard_map.84 = (f32[16,128]{1,0:T(8,128)S(1)}, f32[16,128]{1,0:T(8,128)S(1)}, f32[2048,128]{1,0:T(8,128)S(1)}, bf16[128,2,256]{2,1,0:T(2,128)(2,1)S(1)}) custom-call(s32[8,128]{1,0:T(8,128)S(1)} %get-tuple-element.24.facts_ref, s32[17]{0:T(128)S(1)} %get-tuple-element.25.slots_hbm, bf16[128,2048]{1,0:T(8,128)(2,1)S(1)} %get-tuple-element.26.rotated_ref, ...), custom_call_target="tpu_custom_call" | custom-call | tf_op jit(solution)/shard_map/pallas_call | solution.py:519
  39.2 0.7 %collective-permute-done.7.refs_0_ = bf16[64,512]{1,0:T(8,128)(2,1)S(1)} collective-permute-done((bf16[64,512]{1,0:T(8,128)(2,1)S(1)}, bf16[64,512]{1,0:T(8,128)(2,1)S(1)}, u32[]{:S(2)}, u32[]{:S(2)}) %collective-permute-start.7) | collective-permute-done | bytes 65568 | tf_op jit(solution)/shard_map/ppermute | solution.py:52
  40.0 0.7 %shard_map.85 = (f32[16,128]{1,0:T(8,128)S(1)}, f32[16,128]{1,0:T(8,128)S(1)}, f32[2048,128]{1,0:T(8,128)S(1)}, bf16[128,2,256]{2,1,0:T(2,128)(2,1)S(1)}) custom-call(s32[8,128]{1,0:T(8,128)S(1)} %get-tuple-element.24.facts_ref, s32[17]{0:T(128)S(1)} %get-tuple-element.25.slots_hbm, bf16[128,2048]{1,0:T(8,128)(2,1)S(1)} %get-tuple-element.26.rotated_ref, ...), custom_call_target="tpu_custom_call" | custom-call | tf_op jit(solution)/shard_map/pallas_call | solution.py:519
  40.7 0.0 collective-permute-done.6.refs_0_
  40.7 2.0 %shard_map.86 = (bf16[128,2048]{1,0:T(8,128)(2,1)}, bf16[128,2,256]{2,1,0:T(2,128)(2,1)}) custom-call(s32[8,128]{1,0:T(8,128)S(1)} %get-tuple-element.24.facts_ref, s32[17]{0:T(128)S(1)} %get-tuple-element.25.slots_hbm, bf16[128,2048]{1,0:T(8,128)(2,1)S(1)} %get-tuple-element.26.rotated_ref, bf16[128,512]{1,0:T(8,128)(2,1)S(1)} %collective-permute-done.6.refs_0_, ...), custom_call_target="tpu_custom_call" | custom-call | tf_op jit(solution)/shard_map/pallas_call | solution.py:519
  (1 shorter events, 0.0 us)
Async XLA Ops:
  0.6 4.3 %collective-permute-start = (bf16[128,2048]{1,0:T(8,128)(2,1)}, bf16[128,2048]{1,0:T(8,128)(2,1)S(1)}, u32[]{:S(2)}, u32[]{:S(2)}) collective-permute-start(bf16[128,2048]{1,0:T(8,128)(2,1)} %own_hbm.1), channel_id=1, source_target_pairs={{0,1},{1,0},{2,3},{3,2},{4,5},{5,4},{6,7},{7,6},{8,9},{9,8},{10,11... | collective-permute-start | bytes 1572872 | tf_op jit(solution)/shard_map/ppermute | solution.py:52
  2.3 9.5 %collective-permute-start.1 = (bf16[64,2048]{1,0:T(8,128)(2,1)S(1)}, bf16[64,2048]{1,0:T(8,128)(2,1)S(1)}, u32[]{:S(2)}, u32[]{:S(2)}) collective-permute-start(bf16[64,2048]{1,0:T(8,128)(2,1)S(1)} %get-tuple-element.47), channel_id=1, source_target_pairs={{0,2},{1,3},{2,0},{3,1},{4,6},{5,7},{6,4},{7,5},{8,10},{9,11},{10,... | collective-permute-start | bytes 786440 | tf_op jit(solution)/shard_map/ppermute | solution.py:52
  11.8 2.2 %collective-permute-start.2 = (bf16[64,2048]{1,0:T(8,128)(2,1)S(1)}, bf16[64,2048]{1,0:T(8,128)(2,1)S(1)}, u32[]{:S(2)}, u32[]{:S(2)}) collective-permute-start(bf16[64,2048]{1,0:T(8,128)(2,1)S(1)} %collective-permute-done.1.piece_ref), channel_id=1, source_target_pairs={{0,1},{1,0},{2,3},{3,2},{4,5},{5,4},{6,7},{7,6},{8,9},{9,8},{10,11... | collective-permute-start | bytes 786440 | tf_op jit(solution)/shard_map/ppermute | solution.py:52
  11.8 8.7 %collective-permute-start.4 = (bf16[64,2048]{1,0:T(8,128)(2,1)S(1)}, bf16[64,2048]{1,0:T(8,128)(2,1)S(1)}, u32[]{:S(2)}, u32[]{:S(2)}) collective-permute-start(bf16[64,2048]{1,0:T(8,128)(2,1)S(1)} %get-tuple-element.46), channel_id=1, source_target_pairs={{0,2},{1,3},{2,0},{3,1},{4,6},{5,7},{6,4},{7,5},{8,10},{9,11},{10,... | collective-permute-start | bytes 786440 | tf_op jit(solution)/shard_map/ppermute | solution.py:52
  20.5 3.3 %collective-permute-start.5 = (bf16[64,2048]{1,0:T(8,128)(2,1)S(1)}, bf16[64,2048]{1,0:T(8,128)(2,1)S(1)}, u32[]{:S(2)}, u32[]{:S(2)}) collective-permute-start(bf16[64,2048]{1,0:T(8,128)(2,1)S(1)} %collective-permute-done.4.piece_ref), channel_id=1, source_target_pairs={{0,1},{1,0},{2,3},{3,2},{4,5},{5,4},{6,7},{7,6},{8,9},{9,8},{10,11... | collective-permute-start | bytes 786440 | tf_op jit(solution)/shard_map/ppermute | solution.py:52
  20.5 7.0 %collective-permute-start.3 = (bf16[64,512]{1,0:T(8,128)(2,1)S(1)}, bf16[64,512]{1,0:T(8,128)(2,1)S(1)}, u32[]{:S(2)}, u32[]{:S(2)}) collective-permute-start(bf16[64,512]{1,0:T(8,128)(2,1)S(1)} %shard_map.79.refs_0_), channel_id=1, source_target_pairs={{0,8},{4,12},{8,0},{12,4},{1,9},{5,13},{9,1},{13,5},{2,10},{6,14},... | collective-permute-start | bytes 196616 | tf_op jit(solution)/shard_map/ppermute | solution.py:52
  27.5 13.2 %collective-permute-start.6 = (bf16[128,512]{1,0:T(8,128)(2,1)S(1)}, bf16[128,512]{1,0:T(8,128)(2,1)S(1)}, u32[]{:S(2)}, u32[]{:S(2)}) collective-permute-start(bf16[128,512]{1,0:T(8,128)(2,1)S(1)} %shard_map.82), channel_id=1, source_target_pairs={{0,4},{4,0},{8,12},{12,8},{1,5},{5,1},{9,13},{13,9},{2,6},{6,2},{1... | collective-permute-start | bytes 393224 | tf_op jit(solution)/shard_map/ppermute | solution.py:52
  28.3 5.2 %collective-permute-start.9 = (bf16[64,512]{1,0:T(8,128)(2,1)S(1)}, bf16[64,512]{1,0:T(8,128)(2,1)S(1)}, u32[]{:S(2)}, u32[]{:S(2)}) collective-permute-start(bf16[64,512]{1,0:T(8,128)(2,1)S(1)} %shard_map.79.refs_0_), channel_id=1, source_target_pairs={{0,4},{4,0},{8,12},{12,8},{1,5},{5,1},{9,13},{13,9},{2,6},{6,2},{1... | collective-permute-start | bytes 196616 | tf_op jit(solution)/shard_map/ppermute | solution.py:52
  29.6 8.8 %collective-permute-start.8 = (bf16[64,512]{1,0:T(8,128)(2,1)S(1)}, bf16[64,512]{1,0:T(8,128)(2,1)S(1)}, u32[]{:S(2)}, u32[]{:S(2)}) collective-permute-start(bf16[64,512]{1,0:T(8,128)(2,1)S(1)} %shard_map.81.refs_1_.refs_0_), channel_id=1, source_target_pairs={{0,12},{4,8},{8,4},{12,0},{1,13},{5,9},{9,5},{13,1},{2,14},{6,10},... | collective-permute-start | bytes 196616 | tf_op jit(solution)/shard_map/ppermute | solution.py:52
  33.2 6.8 %collective-permute-start.7 = (bf16[64,512]{1,0:T(8,128)(2,1)S(1)}, bf16[64,512]{1,0:T(8,128)(2,1)S(1)}, u32[]{:S(2)}, u32[]{:S(2)}) collective-permute-start(bf16[64,512]{1,0:T(8,128)(2,1)S(1)} %shard_map.81.refs_1_.refs_0_), channel_id=1, source_target_pairs={{0,8},{4,12},{8,0},{12,4},{1,9},{5,13},{9,1},{13,5},{2,10},{6,14},... | collective-permute-start | bytes 196616 | tf_op jit(solution)/shard_map/ppermute | solution.py:52

commit v6 on v5

--- a/solution.py
+++ b/solution.py
@@ -12,6 +12,7 @@
 LOW = -1e30
 SHARE = 2
 STAGES = ('acg', 'bf', 'd', 'e')
+GATE = True
 MIB = 1 << 20
 VMEM = pl.BlockSpec(memory_space=pltpu.VMEM)
 SMEM = pl.BlockSpec(memory_space=pltpu.SMEM)
@@ -217,69 +218,78 @@
         sums[at] = sums[at] + jnp.dot(piece, ref[...], preferred_element_type=jnp.float32)
 
 
-def early_body(offsets, place_ref, key_hbm, value_hbm, own_hbm, queries_hbm, lengths_hbm, owners_hbm, *refs):
-    near_refs = refs[: len(offsets) - 1]
-    outs = refs[len(offsets) - 1 :]
-    keys_ref, values_ref, sums_ref = outs[:3]
-    tables = outs[3:8]
-    own_ref, queries_ref, lengths_ref, owners_ref, weight_sems, sems = outs[8:]
-    parts, width, kv_width = keys_ref.shape
+def bring(place_ref, offsets, sources, goals, sems):
+    pairs = []
+    for n, offset in enumerate(offsets):
+        width = goals[0].shape[1]
+        start = pl.multiple_of((place_ref[1] ^ offset) * width, width)
+        pair = [
+            pltpu.make_async_copy(source.at[pl.ds(start, width)], goal.at[n], sems.at[side, n])
+            for side, (source, goal) in enumerate(zip(sources, goals))
+        ]
+        for copy in pair:
+            copy.start()
+        pairs.append(pair)
+    return pairs
+
+
+def ahead_body(offsets, place_ref, key_hbm, value_hbm, queries_hbm, lengths_hbm, owners_hbm, *refs):
+    keys_ref, values_ref = refs[:2]
+    tables = refs[2:7]
+    queries_ref, lengths_ref, owners_ref, weight_sems, sems = refs[7:]
     small = [
         pltpu.make_async_copy(source, goal, sems.at[n])
         for n, (source, goal) in enumerate(
-            (
-                (lengths_hbm, lengths_ref),
-                (owners_hbm, owners_ref),
-                (queries_hbm, queries_ref),
-                (own_hbm, own_ref),
-            )
+            ((lengths_hbm, lengths_ref), (owners_hbm, owners_ref), (queries_hbm, queries_ref))
         )
     ]
     for copy in small:
         copy.start()
-    copies = []
-    order = list(offsets) + [o for o in range(parts) if o not in offsets]
-    for offset in order:
-        start = pl.multiple_of((place_ref[1] ^ offset) * width, width)
-        pair = [
-            pltpu.make_async_copy(hbm.at[pl.ds(start, width)], ref.at[offset], weight_sems.at[side, offset])
-            for side, (hbm, ref) in enumerate(((key_hbm, keys_ref), (value_hbm, values_ref)))
-        ]
-        for copy in pair:
-            copy.start()
-        copies.append(pair)
+    pairs = bring(place_ref, offsets, (key_hbm, value_hbm), (keys_ref, values_ref), weight_sems)
     for copy in small:
         copy.wait()
     prepare(place_ref[0], lengths_ref, owners_ref, queries_ref, *tables)
+    for pair in pairs:
+        for copy in pair:
+            copy.wait()
+
+
+def early_body(offsets, place_ref, key_hbm, value_hbm, own_hbm, near_keys_ref, near_values_ref, *refs):
+    *near_refs, keys_ref, values_ref, sums_ref, own_ref, weight_sems, own_sem = refs
+    kv_width = keys_ref.shape[2]
+    own_copy = pltpu.make_async_copy(own_hbm, own_ref, own_sem)
+    own_copy.start()
+    pairs = bring(place_ref, offsets, (key_hbm, value_hbm), (keys_ref, values_ref), weight_sems)
     sums = {0: 0.0, kv_width: 0.0}
-    pieces = [own_ref] + list(near_refs)
-    for n, offset in enumerate(order):
-        for copy in copies[n]:
-            copy.wait()
-        if n < len(offsets):
-            add_products(pieces[n][...], keys_ref.at[offset], values_ref.at[offset], sums)
+    for n, ref in reversed(list(enumerate([own_ref] + near_refs))):
+        if n == 0:
+            own_copy.wait()
+        add_products(ref[...], near_keys_ref.at[n], near_values_ref.at[n], sums)
     for at in sums:
         sums_ref[:, at : at + kv_width] = sums[at]
-
-
-def far_body(offset, start, keys_ref, values_ref, sums_ref, piece_ref, out_ref):
+    for pair in pairs:
+        for copy in pair:
+            copy.wait()
+
+
+def far_body(start, keys_ref, values_ref, sums_ref, piece_ref, out_ref):
     size = piece_ref.shape[0]
     kv_width = keys_ref.shape[2]
     rows = slice(start, start + size)
     sums = {at: sums_ref[rows, at : at + kv_width] for at in (0, kv_width)}
-    add_products(piece_ref[...], keys_ref.at[offset], values_ref.at[offset], sums)
+    add_products(piece_ref[...], keys_ref.at[0], values_ref.at[0], sums)
     for at in sums:
         out_ref[:, at : at + kv_width] = sums[at]
 
 
-def late_body(offsets, start, keys_ref, values_ref, sums_ref, cos_ref, sin_ref, *refs):
+def late_body(start, keys_ref, values_ref, sums_ref, cos_ref, sin_ref, *refs):
     *refs, packed_ref = refs
     size = packed_ref.shape[0]
     kv_width = keys_ref.shape[2]
     rows = slice(start, start + size)
     sums = {at: sums_ref[:, at : at + kv_width] for at in (0, kv_width)}
-    for offset, ref in zip(offsets, refs):
-        add_products(ref[...], keys_ref.at[offset], values_ref.at[offset], sums)
+    for n, ref in enumerate(refs):
+        add_products(ref[...], keys_ref.at[n + 1], values_ref.at[n + 1], sums)
     cosines = cos_ref[rows, :]
     sines = sin_ref[rows, :]
     for h in range(kv_width // HD):
@@ -428,37 +438,47 @@
         pltpu.with_memory_space_constraint(a, pltpu.HBM)
         for a in (key_weight, value_weight, activations, queries, lengths, owners)
     ]
-    for start, size in zip(starts, sizes):
-        piece = activations[start : start + size]
-        crossed.append(swap(piece, "tp", far))
-    near = spread_over({0: activations}, far // 2)
-
-    offsets = sorted(near)
+    near_offsets = list(range(far))
+    far_offsets = list(range(far, parts))
     table = jax.ShapeDtypeStruct((local_rows, HD), jnp.float32)
-    weights = jax.ShapeDtypeStruct((parts, width, kv_width), jnp.bfloat16)
-    keys, values, sums, cosines, sines, rotated, facts, slots = call(
-        functools.partial(early_body, offsets),
+    weights = jax.ShapeDtypeStruct((far, width, kv_width), jnp.bfloat16)
+    near_keys, near_values, cosines, sines, rotated, facts, slots = call(
+        functools.partial(ahead_body, near_offsets),
         [
             weights,
             weights,
-            jax.ShapeDtypeStruct((local_rows, 2 * kv_width), jnp.float32),
             table,
             table,
             jax.ShapeDtypeStruct(queries.shape, queries.dtype),
             jax.ShapeDtypeStruct((8, local_rows), jnp.int32),
             jax.ShapeDtypeStruct((owners.shape[0] + 1,), jnp.int32),
         ],
-        [SMEM] + [ANY] * 6 + [VMEM] * (len(offsets) - 1),
+        [SMEM] + [ANY] * 5,
         scratch=[
-            pltpu.VMEM(activations.shape, activations.dtype),
             pltpu.VMEM(queries.shape, queries.dtype),
             pltpu.SMEM(lengths.shape, jnp.int32),
             pltpu.SMEM(owners.shape, jnp.int32),
-            pltpu.SemaphoreType.DMA((2, parts)),
-            pltpu.SemaphoreType.DMA((4,)),
+            pltpu.SemaphoreType.DMA((2, far)),
+            pltpu.SemaphoreType.DMA((3,)),
         ],
-        out_specs=[VMEM] * 7 + [SMEM],
-    )(place, *stays, *[near[o] for o in offsets[1:]])
+        out_specs=[VMEM] * 6 + [SMEM],
+    )(place, *stays[:2], *stays[3:])
+    for c, (start, size) in enumerate(zip(starts, sizes)):
+        piece = activations[start : start + size]
+        if c and GATE:
+            piece = lax.optimization_barrier((piece, cosines))[0]
+        crossed.append(swap(piece, "tp", far))
+    near = spread_over({0: activations}, far // 2)
+    keys, values, sums = call(
+        functools.partial(early_body, far_offsets),
+        [weights, weights, jax.ShapeDtypeStruct((local_rows, 2 * kv_width), jnp.float32)],
+        [SMEM] + [ANY] * 3 + [VMEM] * (len(near_offsets) + 1),
+        scratch=[
+            pltpu.VMEM(activations.shape, activations.dtype),
+            pltpu.SemaphoreType.DMA((2, far)),
+            pltpu.SemaphoreType.DMA,
+        ],
+    )(place, *stays[:3], near_keys, near_values, *[near[o] for o in near_offsets[1:]])
 
     arrived = []
     ready = sums
@@ -467,13 +487,13 @@
         late = spread_over({far: piece}, far // 2)
         del late[far]
         partial = call(
-            functools.partial(far_body, far, start),
+            functools.partial(far_body, start),
             jax.ShapeDtypeStruct((size, 2 * kv_width), jnp.float32),
             [VMEM] * 4,
         )(keys, values, sums, piece)
         offsets = sorted(late)
         packed = call(
-            functools.partial(late_body, offsets, start),
+            functools.partial(late_body, start),
             jax.ShapeDtypeStruct((size, 2 * kv_width), jnp.bfloat16),
             [VMEM] * (5 + len(offsets)),
         )(keys, values, partial, cosines, sines, *[late[o] for o in offsets])

time: 42.9 us -> 42.9 us (level)
  Pallas kernels: 13.1 us -> 13.6 us
  waiting for transfers between devices: 14.4 us -> 13.9 us
    ppermute x10, waiting for transfers between devices: 14.4 us -> 13.9 us  [swap(): return lax.ppermute(array, axis, [(i, i ^ distance) for i in range(count)])]
    pallas_call x5 -> x6, Pallas kernels: 8.21 us -> 8.72 us  [the longest x1 3.72 us: chunked_device(): call(functools.partial(ahead_body, near_offsets), [weights, weights, tabl...]
  transfers between devices with their start and end apart: 10 -> 10, of which waited for: 6 -> 6; matrix products, arithmetic and copies ran while one was open for 3% -> 3% of each run, Pallas kernels for 26% -> 27%
where the time goes in v6:
time: 42.9 us; the launch traced here: 42.7 us
  waiting for transfers between devices  13.9 us (32%)
  Pallas kernels  13.6 us (32%)
  starting transfers between devices  13.3 us (31%)
  local copies, waits for them, and re-layouts  1.06 us (2%)
  between operations  0.74 us (2%)
    ppermute x10, waiting for transfers between devices, swap(): return lax.ppermute(array, axis, [(i, i ^ distance) for i in range(count)])  13.9 us
    ppermute x10, starting transfers between devices, swap(): return lax.ppermute(array, axis, [(i, i ^ distance) for i in range(count)])  13.3 us
    pallas_call x4, Pallas kernels, chunked_device(): call(functools.partial(attend_body, held, block_len, n > 0, final), resul...  4.86 us
    pallas_call x1, Pallas kernels, chunked_device(): call(functools.partial(ahead_body, near_offsets), [weights, weights, tabl...  3.72 us
    pallas_call x1, Pallas kernels, chunked_device(): call(functools.partial(early_body, far_offsets), [weights, weights, jax.S...  2.92 us
    pallas_call x2, Pallas kernels, chunked_device(): call(functools.partial(late_body, start), jax.ShapeDtypeStruct((size, 2 *...  1.11 us
    slice x1, local copies, waits for them, and re-layouts, chunked_device(): piece = activations[start:start + size]  1.06 us
    pallas_call x2, Pallas kernels, chunked_device(): call(functools.partial(far_body, start), jax.ShapeDtypeStruct((size, 2 *...  0.97 us
  transfers between devices with their start and end apart: 10, of which 6 were waited for; matrix products, arithmetic and copies ran while one was open for 3% of the time, Pallas kernels for 27%

profile of v6, /device:TPU:0, one launch (start us, length us, event | category | flops | bytes accessed | tf_op | source)
XLA Modules:
  0.0 42.7 jit_solution(13984203494934514165)
XLA Ops:
  0.6 0.6 %collective-permute-start = (bf16[128,2048]{1,0:T(8,128)(2,1)}, bf16[128,2048]{1,0:T(8,128)(2,1)S(1)}, u32[]{:S(2)}, u32[]{:S(2)}) collective-permute-start(bf16[128,2048]{1,0:T(8,128)(2,1)} %own_hbm.1), channel_id=1, source_target_pairs={{0,1},{1,0},{2,3},{3,2},{4,5},{5,4},{6,7},{7,6},{8,9},{9,8},{10,11... | collective-permute-start | bytes 1572872 | tf_op jit(solution)/shard_map/ppermute | solution.py:53
  1.2 1.1 %fusion = (bf16[64,2048]{1,0:T(8,128)(2,1)S(1)}, bf16[64,2048]{1,0:T(8,128)(2,1)S(1)}) fusion(bf16[128,2048]{1,0:T(8,128)(2,1)} %own_hbm.1), kind=kLoop, calls=%fused_computation.1 | loop fusion | bytes 1048576 | tf_op jit(solution)/shard_map/slice | solution.py:467
  2.3 2.6 %collective-permute-start.1 = (bf16[64,2048]{1,0:T(8,128)(2,1)S(1)}, bf16[64,2048]{1,0:T(8,128)(2,1)S(1)}, u32[]{:S(2)}, u32[]{:S(2)}) collective-permute-start(bf16[64,2048]{1,0:T(8,128)(2,1)S(1)} %get-tuple-element.53), channel_id=1, source_target_pairs={{0,2},{1,3},{2,0},{3,1},{4,6},{5,7},{6,4},{7,5},{8,10},{9,11},{10,... | collective-permute-start | bytes 786440 | tf_op jit(solution)/shard_map/ppermute | solution.py:53
  4.8 0.1 pad_add_fusion.place_ref
  4.9 3.7 %shard_map.77 = (bf16[2,2048,256]{2,1,0:T(8,128)(2,1)S(1)}, bf16[2,2048,256]{2,1,0:T(8,128)(2,1)S(1)}, f32[128,128]{1,0:T(8,128)S(1)}, f32[128,128]{1,0:T(8,128)...) custom-call(s32[2]{0:T(128)S(1)} %pad_add_fusion.place_ref, bf16[8192,256]{1,0:T(8,128)(2,1)} %key_hbm.3, ...), custom_call_target="tpu_custom_call" | custom-call | tf_op jit(solution)/shard_map/pallas_call | solution.py:445
  8.6 0.0 collective-permute-done.refs_0_
  8.6 2.9 %shard_map.78 = (bf16[2,2048,256]{2,1,0:T(8,128)(2,1)S(1)}, bf16[2,2048,256]{2,1,0:T(8,128)(2,1)S(1)}, f32[128,512]{1,0:T(8,128)S(1)}) custom-call(s32[2]{0:T(128)S(1)} %pad_add_fusion.place_ref, bf16[8192,256]{1,0:T(8,128)(2,1)} %key_hbm.3, bf16[8192,256]{1,0:T(8,128)(2,1)} %value_hbm.3, bf16[128,2048]{1,0:T(8,128)(2,1)} %own_hbm.1, ...), custom_call_target="tpu_custom_call" | custom-call | tf_op jit(solution)/shard_map/pallas_call | solution.py:472
  11.6 0.2 collective-permute-done.1.piece_ref
  11.8 0.1 collective-permute-start.2
  11.8 1.7 %collective-permute-start.4 = (bf16[64,2048]{1,0:T(8,128)(2,1)S(1)}, bf16[64,2048]{1,0:T(8,128)(2,1)S(1)}, u32[]{:S(2)}, u32[]{:S(2)}) collective-permute-start(bf16[64,2048]{1,0:T(8,128)(2,1)S(1)} %get-tuple-element.38), channel_id=1, source_target_pairs={{0,2},{1,3},{2,0},{3,1},{4,6},{5,7},{6,4},{7,5},{8,10},{9,11},{10,... | collective-permute-start | bytes 786440 | tf_op jit(solution)/shard_map/ppermute | solution.py:53
  13.5 0.5 %shard_map.79.sums_ref = f32[64,512]{1,0:T(8,128)S(1)} custom-call(bf16[2,2048,256]{2,1,0:T(8,128)(2,1)S(1)} %get-tuple-element.32.keys_ref, bf16[2,2048,256]{2,1,0:T(8,128)(2,1)S(1)} %get-tuple-element.33.values_ref, f32[128,512]{1,0:T(8,128)S(1)} %get-tuple-element.34.sums_ref, bf16[64,2048]{1,0:T(8,128)(2,1)S(1)} %collective-permute-done.1.piece_ref), custom_call_target="tpu_custom_call" | custom-call | tf_op jit(solution)/shard_map/pallas_call | solution.py:489
  14.0 0.0 collective-permute-done.2.refs_0_
  14.0 0.6 %shard_map.80.refs_0_ = bf16[64,512]{1,0:T(8,128)(2,1)S(1)} custom-call(bf16[2,2048,256]{2,1,0:T(8,128)(2,1)S(1)} %get-tuple-element.32.keys_ref, bf16[2,2048,256]{2,1,0:T(8,128)(2,1)S(1)} %get-tuple-element.33.values_ref, f32[64,512]{1,0:T(8,128)S(1)} %shard_map.79.sums_ref, f32[128,128]{1,0:T(8,128)S(1)} %get-tuple-element.36.cos_ref, ...), custom_call_target="tpu_custom_call" | custom-call | tf_op jit(solution)/shard_map/pallas_call | solution.py:495
  14.6 5.9 %collective-permute-done.4.piece_ref = bf16[64,2048]{1,0:T(8,128)(2,1)S(1)} collective-permute-done((bf16[64,2048]{1,0:T(8,128)(2,1)S(1)}, bf16[64,2048]{1,0:T(8,128)(2,1)S(1)}, u32[]{:S(2)}, u32[]{:S(2)}) %collective-permute-start.4) | collective-permute-done | bytes 262176 | tf_op jit(solution)/shard_map/ppermute | solution.py:53
  20.5 0.0 collective-permute-start.5
  20.5 2.8 %collective-permute-start.3 = (bf16[64,512]{1,0:T(8,128)(2,1)S(1)}, bf16[64,512]{1,0:T(8,128)(2,1)S(1)}, u32[]{:S(2)}, u32[]{:S(2)}) collective-permute-start(bf16[64,512]{1,0:T(8,128)(2,1)S(1)} %shard_map.80.refs_0_), channel_id=1, source_target_pairs={{0,8},{4,12},{8,0},{12,4},{1,9},{5,13},{9,1},{13,5},{2,10},{6,14},... | collective-permute-start | bytes 196616 | tf_op jit(solution)/shard_map/ppermute | solution.py:53
  23.3 0.5 %shard_map.81.sums_ref = f32[64,512]{1,0:T(8,128)S(1)} custom-call(bf16[2,2048,256]{2,1,0:T(8,128)(2,1)S(1)} %get-tuple-element.32.keys_ref, bf16[2,2048,256]{2,1,0:T(8,128)(2,1)S(1)} %get-tuple-element.33.values_ref, f32[128,512]{1,0:T(8,128)S(1)} %get-tuple-element.34.sums_ref, bf16[64,2048]{1,0:T(8,128)(2,1)S(1)} %collective-permute-done.4.piece_ref), custom_call_target="tpu_custom_call" | custom-call | tf_op jit(solution)/shard_map/pallas_call | solution.py:489
  23.8 0.0 collective-permute-done.5.refs_0_
  23.8 0.6 %shard_map.82.refs_1_.refs_0_ = bf16[64,512]{1,0:T(8,128)(2,1)S(1)} custom-call(bf16[2,2048,256]{2,1,0:T(8,128)(2,1)S(1)} %get-tuple-element.32.keys_ref, bf16[2,2048,256]{2,1,0:T(8,128)(2,1)S(1)} %get-tuple-element.33.values_ref, f32[64,512]{1,0:T(8,128)S(1)} %shard_map.81.sums_ref, f32[128,128]{1,0:T(8,128)S(1)} %get-tuple-element.36.cos_ref, ...), custom_call_target="tpu_custom_call" | custom-call | tf_op jit(solution)/shard_map/pallas_call | solution.py:495
  24.4 3.1 %collective-permute-done.3.refs_0_.refs_1_ = bf16[64,512]{1,0:T(8,128)(2,1)S(1)} collective-permute-done((bf16[64,512]{1,0:T(8,128)(2,1)S(1)}, bf16[64,512]{1,0:T(8,128)(2,1)S(1)}, u32[]{:S(2)}, u32[]{:S(2)}) %collective-permute-start.3) | collective-permute-done | bytes 65568 | tf_op jit(solution)/shard_map/ppermute | solution.py:53
  27.5 0.8 %collective-permute-start.6 = (bf16[128,512]{1,0:T(8,128)(2,1)S(1)}, bf16[128,512]{1,0:T(8,128)(2,1)S(1)}, u32[]{:S(2)}, u32[]{:S(2)}) collective-permute-start(bf16[128,512]{1,0:T(8,128)(2,1)S(1)} %shard_map.83), channel_id=1, source_target_pairs={{0,4},{4,0},{8,12},{12,8},{1,5},{5,1},{9,13},{13,9},{2,6},{6,2},{1... | collective-permute-start | bytes 393224 | tf_op jit(solution)/shard_map/ppermute | solution.py:53
  28.3 1.3 %collective-permute-start.9 = (bf16[64,512]{1,0:T(8,128)(2,1)S(1)}, bf16[64,512]{1,0:T(8,128)(2,1)S(1)}, u32[]{:S(2)}, u32[]{:S(2)}) collective-permute-start(bf16[64,512]{1,0:T(8,128)(2,1)S(1)} %shard_map.80.refs_0_), channel_id=1, source_target_pairs={{0,4},{4,0},{8,12},{12,8},{1,5},{5,1},{9,13},{13,9},{2,6},{6,2},{1... | collective-permute-start | bytes 196616 | tf_op jit(solution)/shard_map/ppermute | solution.py:53
  29.6 3.5 %collective-permute-start.8 = (bf16[64,512]{1,0:T(8,128)(2,1)S(1)}, bf16[64,512]{1,0:T(8,128)(2,1)S(1)}, u32[]{:S(2)}, u32[]{:S(2)}) collective-permute-start(bf16[64,512]{1,0:T(8,128)(2,1)S(1)} %shard_map.82.refs_1_.refs_0_), channel_id=1, source_target_pairs={{0,12},{4,8},{8,4},{12,0},{1,13},{5,9},{9,5},{13,1},{2,14},{6,10},... | collective-permute-start | bytes 196616 | tf_op jit(solution)/shard_map/ppermute | solution.py:53
  33.2 0.0 collective-permute-start.7
  33.2 0.3 collective-permute-done.9.refs_2_
  33.5 1.3 %shard_map.84 = (f32[16,128]{1,0:T(8,128)S(1)}, f32[16,128]{1,0:T(8,128)S(1)}, f32[2048,128]{1,0:T(8,128)S(1)}, bf16[128,2,256]{2,1,0:T(2,128)(2,1)S(1)}) custom-call(s32[8,128]{1,0:T(8,128)S(1)} %get-tuple-element.27.facts_ref, s32[17]{0:T(128)S(1)} %get-tuple-element.28.slots_hbm, bf16[128,2048]{1,0:T(8,128)(2,1)S(1)} %get-tuple-element.29.rotated_ref, ...), custom_call_target="tpu_custom_call" | custom-call | tf_op jit(solution)/shard_map/pallas_call | solution.py:539
  34.8 3.6 %collective-permute-done.8.refs_1_ = bf16[64,512]{1,0:T(8,128)(2,1)S(1)} collective-permute-done((bf16[64,512]{1,0:T(8,128)(2,1)S(1)}, bf16[64,512]{1,0:T(8,128)(2,1)S(1)}, u32[]{:S(2)}, u32[]{:S(2)}) %collective-permute-start.8) | collective-permute-done | bytes 65568 | tf_op jit(solution)/shard_map/ppermute | solution.py:53
  38.4 0.8 %shard_map.85 = (f32[16,128]{1,0:T(8,128)S(1)}, f32[16,128]{1,0:T(8,128)S(1)}, f32[2048,128]{1,0:T(8,128)S(1)}, bf16[128,2,256]{2,1,0:T(2,128)(2,1)S(1)}) custom-call(s32[8,128]{1,0:T(8,128)S(1)} %get-tuple-element.27.facts_ref, s32[17]{0:T(128)S(1)} %get-tuple-element.28.slots_hbm, bf16[128,2048]{1,0:T(8,128)(2,1)S(1)} %get-tuple-element.29.rotated_ref, ...), custom_call_target="tpu_custom_call" | custom-call | tf_op jit(solution)/shard_map/pallas_call | solution.py:539
  39.2 0.7 %collective-permute-done.7.refs_0_ = bf16[64,512]{1,0:T(8,128)(2,1)S(1)} collective-permute-done((bf16[64,512]{1,0:T(8,128)(2,1)S(1)}, bf16[64,512]{1,0:T(8,128)(2,1)S(1)}, u32[]{:S(2)}, u32[]{:S(2)}) %collective-permute-start.7) | collective-permute-done | bytes 65568 | tf_op jit(solution)/shard_map/ppermute | solution.py:53
  40.0 0.7 %shard_map.86 = (f32[16,128]{1,0:T(8,128)S(1)}, f32[16,128]{1,0:T(8,128)S(1)}, f32[2048,128]{1,0:T(8,128)S(1)}, bf16[128,2,256]{2,1,0:T(2,128)(2,1)S(1)}) custom-call(s32[8,128]{1,0:T(8,128)S(1)} %get-tuple-element.27.facts_ref, s32[17]{0:T(128)S(1)} %get-tuple-element.28.slots_hbm, bf16[128,2048]{1,0:T(8,128)(2,1)S(1)} %get-tuple-element.29.rotated_ref, ...), custom_call_target="tpu_custom_call" | custom-call | tf_op jit(solution)/shard_map/pallas_call | solution.py:539
  40.7 0.0 collective-permute-done.6.refs_0_
  40.7 2.0 %shard_map.87 = (bf16[128,2048]{1,0:T(8,128)(2,1)}, bf16[128,2,256]{2,1,0:T(2,128)(2,1)}) custom-call(s32[8,128]{1,0:T(8,128)S(1)} %get-tuple-element.27.facts_ref, s32[17]{0:T(128)S(1)} %get-tuple-element.28.slots_hbm, bf16[128,2048]{1,0:T(8,128)(2,1)S(1)} %get-tuple-element.29.rotated_ref, bf16[128,512]{1,0:T(8,128)(2,1)S(1)} %collective-permute-done.6.refs_0_, ...), custom_call_target="tpu_custom_call" | custom-call | tf_op jit(solution)/shard_map/pallas_call | solution.py:539
  (1 shorter events, 0.0 us)
Async XLA Ops:
  0.6 8.0 %collective-permute-start = (bf16[128,2048]{1,0:T(8,128)(2,1)}, bf16[128,2048]{1,0:T(8,128)(2,1)S(1)}, u32[]{:S(2)}, u32[]{:S(2)}) collective-permute-start(bf16[128,2048]{1,0:T(8,128)(2,1)} %own_hbm.1), channel_id=1, source_target_pairs={{0,1},{1,0},{2,3},{3,2},{4,5},{5,4},{6,7},{7,6},{8,9},{9,8},{10,11... | collective-permute-start | bytes 1572872 | tf_op jit(solution)/shard_map/ppermute | solution.py:53
  2.3 9.5 %collective-permute-start.1 = (bf16[64,2048]{1,0:T(8,128)(2,1)S(1)}, bf16[64,2048]{1,0:T(8,128)(2,1)S(1)}, u32[]{:S(2)}, u32[]{:S(2)}) collective-permute-start(bf16[64,2048]{1,0:T(8,128)(2,1)S(1)} %get-tuple-element.53), channel_id=1, source_target_pairs={{0,2},{1,3},{2,0},{3,1},{4,6},{5,7},{6,4},{7,5},{8,10},{9,11},{10,... | collective-permute-start | bytes 786440 | tf_op jit(solution)/shard_map/ppermute | solution.py:53
  11.8 2.2 %collective-permute-start.2 = (bf16[64,2048]{1,0:T(8,128)(2,1)S(1)}, bf16[64,2048]{1,0:T(8,128)(2,1)S(1)}, u32[]{:S(2)}, u32[]{:S(2)}) collective-permute-start(bf16[64,2048]{1,0:T(8,128)(2,1)S(1)} %collective-permute-done.1.piece_ref), channel_id=1, source_target_pairs={{0,1},{1,0},{2,3},{3,2},{4,5},{5,4},{6,7},{7,6},{8,9},{9,8},{10,11... | collective-permute-start | bytes 786440 | tf_op jit(solution)/shard_map/ppermute | solution.py:53
  11.8 8.7 %collective-permute-start.4 = (bf16[64,2048]{1,0:T(8,128)(2,1)S(1)}, bf16[64,2048]{1,0:T(8,128)(2,1)S(1)}, u32[]{:S(2)}, u32[]{:S(2)}) collective-permute-start(bf16[64,2048]{1,0:T(8,128)(2,1)S(1)} %get-tuple-element.38), channel_id=1, source_target_pairs={{0,2},{1,3},{2,0},{3,1},{4,6},{5,7},{6,4},{7,5},{8,10},{9,11},{10,... | collective-permute-start | bytes 786440 | tf_op jit(solution)/shard_map/ppermute | solution.py:53
  20.5 3.3 %collective-permute-start.5 = (bf16[64,2048]{1,0:T(8,128)(2,1)S(1)}, bf16[64,2048]{1,0:T(8,128)(2,1)S(1)}, u32[]{:S(2)}, u32[]{:S(2)}) collective-permute-start(bf16[64,2048]{1,0:T(8,128)(2,1)S(1)} %collective-permute-done.4.piece_ref), channel_id=1, source_target_pairs={{0,1},{1,0},{2,3},{3,2},{4,5},{5,4},{6,7},{7,6},{8,9},{9,8},{10,11... | collective-permute-start | bytes 786440 | tf_op jit(solution)/shard_map/ppermute | solution.py:53
  20.5 7.0 %collective-permute-start.3 = (bf16[64,512]{1,0:T(8,128)(2,1)S(1)}, bf16[64,512]{1,0:T(8,128)(2,1)S(1)}, u32[]{:S(2)}, u32[]{:S(2)}) collective-permute-start(bf16[64,512]{1,0:T(8,128)(2,1)S(1)} %shard_map.80.refs_0_), channel_id=1, source_target_pairs={{0,8},{4,12},{8,0},{12,4},{1,9},{5,13},{9,1},{13,5},{2,10},{6,14},... | collective-permute-start | bytes 196616 | tf_op jit(solution)/shard_map/ppermute | solution.py:53
  27.5 13.2 %collective-permute-start.6 = (bf16[128,512]{1,0:T(8,128)(2,1)S(1)}, bf16[128,512]{1,0:T(8,128)(2,1)S(1)}, u32[]{:S(2)}, u32[]{:S(2)}) collective-permute-start(bf16[128,512]{1,0:T(8,128)(2,1)S(1)} %shard_map.83), channel_id=1, source_target_pairs={{0,4},{4,0},{8,12},{12,8},{1,5},{5,1},{9,13},{13,9},{2,6},{6,2},{1... | collective-permute-start | bytes 393224 | tf_op jit(solution)/shard_map/ppermute | solution.py:53
  28.3 5.2 %collective-permute-start.9 = (bf16[64,512]{1,0:T(8,128)(2,1)S(1)}, bf16[64,512]{1,0:T(8,128)(2,1)S(1)}, u32[]{:S(2)}, u32[]{:S(2)}) collective-permute-start(bf16[64,512]{1,0:T(8,128)(2,1)S(1)} %shard_map.80.refs_0_), channel_id=1, source_target_pairs={{0,4},{4,0},{8,12},{12,8},{1,5},{5,1},{9,13},{13,9},{2,6},{6,2},{1... | collective-permute-start | bytes 196616 | tf_op jit(solution)/shard_map/ppermute | solution.py:53
  29.6 8.8 %collective-permute-start.8 = (bf16[64,512]{1,0:T(8,128)(2,1)S(1)}, bf16[64,512]{1,0:T(8,128)(2,1)S(1)}, u32[]{:S(2)}, u32[]{:S(2)}) collective-permute-start(bf16[64,512]{1,0:T(8,128)(2,1)S(1)} %shard_map.82.refs_1_.refs_0_), channel_id=1, source_target_pairs={{0,12},{4,8},{8,4},{12,0},{1,13},{5,9},{9,5},{13,1},{2,14},{6,10},... | collective-permute-start | bytes 196616 | tf_op jit(solution)/shard_map/ppermute | solution.py:53
  33.2 6.8 %collective-permute-start.7 = (bf16[64,512]{1,0:T(8,128)(2,1)S(1)}, bf16[64,512]{1,0:T(8,128)(2,1)S(1)}, u32[]{:S(2)}, u32[]{:S(2)}) collective-permute-start(bf16[64,512]{1,0:T(8,128)(2,1)S(1)} %shard_map.82.refs_1_.refs_0_), channel_id=1, source_target_pairs={{0,8},{4,12},{8,0},{12,4},{1,9},{5,13},{9,1},{13,5},{2,10},{6,14},... | collective-permute-start | bytes 196616 | tf_op jit(solution)/shard_map/ppermute | solution.py:53

commit v7 on v6

--- a/solution.py
+++ b/solution.py
@@ -10,8 +10,8 @@
 
 HD = 128
 LOW = -1e30
-SHARE = 2
-STAGES = ('acg', 'bf', 'd', 'e')
+SHARE = 5
+STAGES = ('abcg', 'fd', 'e')
 GATE = True
 MIB = 1 << 20
 VMEM = pl.BlockSpec(memory_space=pltpu.VMEM)
@@ -545,8 +545,8 @@
     return state
 
 
-def chunk_sizes(local_rows, block_len):
-    first = max(1, local_rows // block_len * SHARE // 4) * block_len
+def chunk_sizes(local_rows):
+    first = local_rows * SHARE // 8 // 16 * 16
     return [first, local_rows - first]
 
 
@@ -559,7 +559,7 @@
     few = devices == 4 and 1 < parts <= 8 and is_power(parts)
     if not few or block_len % 16 or blocks_dev < 2:
         return gathered_device(activations, queries, key_weight, value_weight, lengths, owners)
-    sizes = chunk_sizes(local_rows, block_len)
+    sizes = chunk_sizes(local_rows)
     return chunked_device(activations, queries, key_weight, value_weight, lengths, owners, sizes)
 
 

time: 42.9 us -> 43.9 us (1.023)
  local copies, waits for them, and re-layouts: 1.06 us -> 1.93 us
  waiting for transfers between devices: 13.9 us -> 14.6 us
  Pallas kernels: 13.6 us -> 13 us
    slice x1 -> x2, local copies, waits for them, and re-layouts: 1.06 us -> 1.93 us  [chunked_device(): piece = activations[start:start + size]]
    ppermute x10, waiting for transfers between devices: 13.9 us -> 14.6 us  [swap(): return lax.ppermute(array, axis, [(i, i ^ distance) for i in range(count)])]
    pallas_call x4 -> x3, Pallas kernels: 4.86 us -> 4.22 us  [chunked_device(): call(functools.partial(attend_body, held, block_len, n > 0, final), resul...]
  transfers between devices with their start and end apart: 10 -> 10, of which waited for: 6 -> 6; matrix products, arithmetic and copies ran while one was open for 3% -> 5% of each run, Pallas kernels for 27% -> 25%
where the time goes in v7:
time: 43.9 us; the launch traced here: 43.7 us
  waiting for transfers between devices  14.6 us (33%)
  starting transfers between devices  13.4 us (31%)
  Pallas kernels  13 us (30%)
  local copies, waits for them, and re-layouts  1.93 us (4%)
  between operations  0.72 us (2%)
    ppermute x10, waiting for transfers between devices, swap(): return lax.ppermute(array, axis, [(i, i ^ distance) for i in range(count)])  14.6 us
    ppermute x10, starting transfers between devices, swap(): return lax.ppermute(array, axis, [(i, i ^ distance) for i in range(count)])  13.4 us
    pallas_call x3, Pallas kernels, chunked_device(): call(functools.partial(attend_body, held, block_len, n > 0, final), resul...  4.22 us
    pallas_call x1, Pallas kernels, chunked_device(): call(functools.partial(ahead_body, near_offsets), [weights, weights, tabl...  3.72 us
    pallas_call x1, Pallas kernels, chunked_device(): call(functools.partial(early_body, far_offsets), [weights, weights, jax.S...  2.92 us
    slice x2, local copies, waits for them, and re-layouts, chunked_device(): piece = activations[start:start + size]  1.93 us
    pallas_call x2, Pallas kernels, chunked_device(): call(functools.partial(late_body, start), jax.ShapeDtypeStruct((size, 2 *...  1.12 us
    pallas_call x2, Pallas kernels, chunked_device(): call(functools.partial(far_body, start), jax.ShapeDtypeStruct((size, 2 *...  0.97 us
  transfers between devices with their start and end apart: 10, of which 6 were waited for; matrix products, arithmetic and copies ran while one was open for 5% of the time, Pallas kernels for 25%

profile of v7, /device:TPU:0, one launch (start us, length us, event | category | flops | bytes accessed | tf_op | source)
XLA Modules:
  0.0 43.7 jit_solution(18005243972057374389)
XLA Ops:
  0.6 0.6 %collective-permute-start = (bf16[128,2048]{1,0:T(8,128)(2,1)}, bf16[128,2048]{1,0:T(8,128)(2,1)S(1)}, u32[]{:S(2)}, u32[]{:S(2)}) collective-permute-start(bf16[128,2048]{1,0:T(8,128)(2,1)} %own_hbm.1), channel_id=1, source_target_pairs={{0,1},{1,0},{2,3},{3,2},{4,5},{5,4},{6,7},{7,6},{8,9},{9,8},{10,11... | collective-permute-start | bytes 1572872 | tf_op jit(solution)/shard_map/ppermute | solution.py:53
  1.2 1.0 %slice.6 = bf16[80,2048]{1,0:T(8,128)(2,1)S(1)} slice(bf16[128,2048]{1,0:T(8,128)(2,1)} %own_hbm.1), slice={[0:80], [0:2048]} | slice | bytes 655360 | tf_op jit(solution)/shard_map/slice | solution.py:467
  2.2 2.6 %collective-permute-start.1 = (bf16[80,2048]{1,0:T(8,128)(2,1)S(1)}, bf16[80,2048]{1,0:T(8,128)(2,1)S(1)}, u32[]{:S(2)}, u32[]{:S(2)}) collective-permute-start(bf16[80,2048]{1,0:T(8,128)(2,1)S(1)} %slice.6), channel_id=1, source_target_pairs={{0,2},{1,3},{2,0},{3,1},{4,6},{5,7},{6,4},{7,5},{8,10},{9,11},{10,... | collective-permute-start | bytes 983048 | tf_op jit(solution)/shard_map/ppermute | solution.py:53
  4.7 0.1 pad_add_fusion.place_ref
  4.8 3.7 %shard_map.77 = (bf16[2,2048,256]{2,1,0:T(8,128)(2,1)S(1)}, bf16[2,2048,256]{2,1,0:T(8,128)(2,1)S(1)}, f32[128,128]{1,0:T(8,128)S(1)}, f32[128,128]{1,0:T(8,128)...) custom-call(s32[2]{0:T(128)S(1)} %pad_add_fusion.place_ref, bf16[8192,256]{1,0:T(8,128)(2,1)} %key_hbm.3, ...), custom_call_target="tpu_custom_call" | custom-call | tf_op jit(solution)/shard_map/pallas_call | solution.py:445
  8.5 0.0 collective-permute-done.refs_0_
  8.6 2.9 %shard_map.78 = (bf16[2,2048,256]{2,1,0:T(8,128)(2,1)S(1)}, bf16[2,2048,256]{2,1,0:T(8,128)(2,1)S(1)}, f32[128,512]{1,0:T(8,128)S(1)}) custom-call(s32[2]{0:T(128)S(1)} %pad_add_fusion.place_ref, bf16[8192,256]{1,0:T(8,128)(2,1)} %key_hbm.3, bf16[8192,256]{1,0:T(8,128)(2,1)} %value_hbm.3, bf16[128,2048]{1,0:T(8,128)(2,1)} %own_hbm.1, ...), custom_call_target="tpu_custom_call" | custom-call | tf_op jit(solution)/shard_map/pallas_call | solution.py:472
  11.5 1.6 %collective-permute-done.1.piece_ref = bf16[80,2048]{1,0:T(8,128)(2,1)S(1)} collective-permute-done((bf16[80,2048]{1,0:T(8,128)(2,1)S(1)}, bf16[80,2048]{1,0:T(8,128)(2,1)S(1)}, u32[]{:S(2)}, u32[]{:S(2)}) %collective-permute-start.1) | collective-permute-done | bytes 327712 | tf_op jit(solution)/shard_map/ppermute | solution.py:53
  13.1 0.0 collective-permute-start.2
  13.1 0.9 %slice.7 = bf16[48,2048]{1,0:T(8,128)(2,1)S(1)} slice(bf16[128,2048]{1,0:T(8,128)(2,1)} %own_hbm.1), slice={[80:128], [0:2048]} | slice | bytes 393216 | tf_op jit(solution)/shard_map/slice | solution.py:467
  14.1 1.8 %collective-permute-start.4 = (bf16[48,2048]{1,0:T(8,128)(2,1)S(1)}, bf16[48,2048]{1,0:T(8,128)(2,1)S(1)}, u32[]{:S(2)}, u32[]{:S(2)}) collective-permute-start(bf16[48,2048]{1,0:T(8,128)(2,1)S(1)} %slice.7), channel_id=1, source_target_pairs={{0,2},{1,3},{2,0},{3,1},{4,6},{5,7},{6,4},{7,5},{8,10},{9,11},{10,... | collective-permute-start | bytes 589832 | tf_op jit(solution)/shard_map/ppermute | solution.py:53
  15.9 0.5 %shard_map.79.sums_ref = f32[80,512]{1,0:T(8,128)S(1)} custom-call(bf16[2,2048,256]{2,1,0:T(8,128)(2,1)S(1)} %get-tuple-element.28.keys_ref, bf16[2,2048,256]{2,1,0:T(8,128)(2,1)S(1)} %get-tuple-element.29.values_ref, f32[128,512]{1,0:T(8,128)S(1)} %get-tuple-element.30.sums_ref, bf16[80,2048]{1,0:T(8,128)(2,1)S(1)} %collective-permute-done.1.piece_ref), custom_call_target="tpu_custom_call" | custom-call | tf_op jit(solution)/shard_map/pallas_call | solution.py:489
  16.4 0.0 collective-permute-done.2.refs_0_
  16.4 0.6 %shard_map.80.refs_0_ = bf16[80,512]{1,0:T(8,128)(2,1)S(1)} custom-call(bf16[2,2048,256]{2,1,0:T(8,128)(2,1)S(1)} %get-tuple-element.28.keys_ref, bf16[2,2048,256]{2,1,0:T(8,128)(2,1)S(1)} %get-tuple-element.29.values_ref, f32[80,512]{1,0:T(8,128)S(1)} %shard_map.79.sums_ref, f32[128,128]{1,0:T(8,128)S(1)} %get-tuple-element.32.cos_ref, ...), custom_call_target="tpu_custom_call" | custom-call | tf_op jit(solution)/shard_map/pallas_call | solution.py:495
  16.9 4.5 %collective-permute-done.4.piece_ref = bf16[48,2048]{1,0:T(8,128)(2,1)S(1)} collective-permute-done((bf16[48,2048]{1,0:T(8,128)(2,1)S(1)}, bf16[48,2048]{1,0:T(8,128)(2,1)S(1)}, u32[]{:S(2)}, u32[]{:S(2)}) %collective-permute-start.4) | collective-permute-done | bytes 196640 | tf_op jit(solution)/shard_map/ppermute | solution.py:53
  21.4 0.0 collective-permute-start.5
  21.4 2.8 %collective-permute-start.3 = (bf16[80,512]{1,0:T(8,128)(2,1)S(1)}, bf16[80,512]{1,0:T(8,128)(2,1)S(1)}, u32[]{:S(2)}, u32[]{:S(2)}) collective-permute-start(bf16[80,512]{1,0:T(8,128)(2,1)S(1)} %shard_map.80.refs_0_), channel_id=1, source_target_pairs={{0,8},{4,12},{8,0},{12,4},{1,9},{5,13},{9,1},{13,5},{2,10},{6,14},... | collective-permute-start | bytes 245768 | tf_op jit(solution)/shard_map/ppermute | solution.py:53
  24.3 0.5 %shard_map.81.sums_ref = f32[48,512]{1,0:T(8,128)S(1)} custom-call(bf16[2,2048,256]{2,1,0:T(8,128)(2,1)S(1)} %get-tuple-element.28.keys_ref, bf16[2,2048,256]{2,1,0:T(8,128)(2,1)S(1)} %get-tuple-element.29.values_ref, f32[128,512]{1,0:T(8,128)S(1)} %get-tuple-element.30.sums_ref, bf16[48,2048]{1,0:T(8,128)(2,1)S(1)} %collective-permute-done.4.piece_ref), custom_call_target="tpu_custom_call" | custom-call | tf_op jit(solution)/shard_map/pallas_call | solution.py:489
  24.8 0.0 collective-permute-done.5.refs_0_
  24.8 0.6 %shard_map.82.refs_1_ = bf16[48,512]{1,0:T(8,128)(2,1)S(1)} custom-call(bf16[2,2048,256]{2,1,0:T(8,128)(2,1)S(1)} %get-tuple-element.28.keys_ref, bf16[2,2048,256]{2,1,0:T(8,128)(2,1)S(1)} %get-tuple-element.29.values_ref, f32[48,512]{1,0:T(8,128)S(1)} %shard_map.81.sums_ref, f32[128,128]{1,0:T(8,128)S(1)} %get-tuple-element.32.cos_ref, ...), custom_call_target="tpu_custom_call" | custom-call | tf_op jit(solution)/shard_map/pallas_call | solution.py:495
  25.3 3.8 %collective-permute-done.3.refs_0_.refs_2_ = bf16[80,512]{1,0:T(8,128)(2,1)S(1)} collective-permute-done((bf16[80,512]{1,0:T(8,128)(2,1)S(1)}, bf16[80,512]{1,0:T(8,128)(2,1)S(1)}, u32[]{:S(2)}, u32[]{:S(2)}) %collective-permute-start.3) | collective-permute-done | bytes 81952 | tf_op jit(solution)/shard_map/ppermute | solution.py:53
  29.2 0.8 %collective-permute-start.6 = (bf16[128,512]{1,0:T(8,128)(2,1)S(1)}, bf16[128,512]{1,0:T(8,128)(2,1)S(1)}, u32[]{:S(2)}, u32[]{:S(2)}) collective-permute-start(bf16[128,512]{1,0:T(8,128)(2,1)S(1)} %shard_map.83), channel_id=1, source_target_pairs={{0,4},{4,0},{8,12},{12,8},{1,5},{5,1},{9,13},{13,9},{2,6},{6,2},{1... | collective-permute-start | bytes 393224 | tf_op jit(solution)/shard_map/ppermute | solution.py:53
  30.0 1.3 %collective-permute-start.9 = (bf16[80,512]{1,0:T(8,128)(2,1)S(1)}, bf16[80,512]{1,0:T(8,128)(2,1)S(1)}, u32[]{:S(2)}, u32[]{:S(2)}) collective-permute-start(bf16[80,512]{1,0:T(8,128)(2,1)S(1)} %shard_map.80.refs_0_), channel_id=1, source_target_pairs={{0,4},{4,0},{8,12},{12,8},{1,5},{5,1},{9,13},{13,9},{2,6},{6,2},{1... | collective-permute-start | bytes 245768 | tf_op jit(solution)/shard_map/ppermute | solution.py:53
  31.3 3.5 %collective-permute-start.7 = (bf16[48,512]{1,0:T(8,128)(2,1)S(1)}, bf16[48,512]{1,0:T(8,128)(2,1)S(1)}, u32[]{:S(2)}, u32[]{:S(2)}) collective-permute-start(bf16[48,512]{1,0:T(8,128)(2,1)S(1)} %shard_map.82.refs_1_), channel_id=1, source_target_pairs={{0,12},{4,8},{8,4},{12,0},{1,13},{5,9},{9,5},{13,1},{2,14},{6,10},... | collective-permute-start | bytes 147464 | tf_op jit(solution)/shard_map/ppermute | solution.py:53
  34.8 0.0 collective-permute-start.8
  34.8 1.4 %collective-permute-done.9.refs_3_ = bf16[80,512]{1,0:T(8,128)(2,1)S(1)} collective-permute-done((bf16[80,512]{1,0:T(8,128)(2,1)S(1)}, bf16[80,512]{1,0:T(8,128)(2,1)S(1)}, u32[]{:S(2)}, u32[]{:S(2)}) %collective-permute-start.9) | collective-permute-done | bytes 81952 | tf_op jit(solution)/shard_map/ppermute | solution.py:53
  36.2 1.4 %shard_map.84 = (f32[16,128]{1,0:T(8,128)S(1)}, f32[16,128]{1,0:T(8,128)S(1)}, f32[2048,128]{1,0:T(8,128)S(1)}, bf16[128,2,256]{2,1,0:T(2,128)(2,1)S(1)}) custom-call(s32[8,128]{1,0:T(8,128)S(1)} %get-tuple-element.23.facts_ref, s32[17]{0:T(128)S(1)} %get-tuple-element.24.slots_hbm, bf16[128,2048]{1,0:T(8,128)(2,1)S(1)} %get-tuple-element.25.rotated_ref, ...), custom_call_target="tpu_custom_call" | custom-call | tf_op jit(solution)/shard_map/pallas_call | solution.py:539
  37.7 2.2 %collective-permute-done.7.refs_0_ = bf16[48,512]{1,0:T(8,128)(2,1)S(1)} collective-permute-done((bf16[48,512]{1,0:T(8,128)(2,1)S(1)}, bf16[48,512]{1,0:T(8,128)(2,1)S(1)}, u32[]{:S(2)}, u32[]{:S(2)}) %collective-permute-start.7) | collective-permute-done | bytes 49184 | tf_op jit(solution)/shard_map/ppermute | solution.py:53
  39.9 1.0 %collective-permute-done.8.refs_1_ = bf16[48,512]{1,0:T(8,128)(2,1)S(1)} collective-permute-done((bf16[48,512]{1,0:T(8,128)(2,1)S(1)}, bf16[48,512]{1,0:T(8,128)(2,1)S(1)}, u32[]{:S(2)}, u32[]{:S(2)}) %collective-permute-start.8) | collective-permute-done | bytes 49184 | tf_op jit(solution)/shard_map/ppermute | solution.py:53
  40.9 0.8 %shard_map.85 = (f32[16,128]{1,0:T(8,128)S(1)}, f32[16,128]{1,0:T(8,128)S(1)}, f32[2048,128]{1,0:T(8,128)S(1)}, bf16[128,2,256]{2,1,0:T(2,128)(2,1)S(1)}) custom-call(s32[8,128]{1,0:T(8,128)S(1)} %get-tuple-element.23.facts_ref, s32[17]{0:T(128)S(1)} %get-tuple-element.24.slots_hbm, bf16[128,2048]{1,0:T(8,128)(2,1)S(1)} %get-tuple-element.25.rotated_ref, ...), custom_call_target="tpu_custom_call" | custom-call | tf_op jit(solution)/shard_map/pallas_call | solution.py:539
  41.7 0.0 collective-permute-done.6.refs_0_
  41.7 2.0 %shard_map.86 = (bf16[128,2048]{1,0:T(8,128)(2,1)}, bf16[128,2,256]{2,1,0:T(2,128)(2,1)}) custom-call(s32[8,128]{1,0:T(8,128)S(1)} %get-tuple-element.23.facts_ref, s32[17]{0:T(128)S(1)} %get-tuple-element.24.slots_hbm, bf16[128,2048]{1,0:T(8,128)(2,1)S(1)} %get-tuple-element.25.rotated_ref, bf16[128,512]{1,0:T(8,128)(2,1)S(1)} %collective-permute-done.6.refs_0_, ...), custom_call_target="tpu_custom_call" | custom-call | tf_op jit(solution)/shard_map/pallas_call | solution.py:539
  (1 shorter events, 0.0 us)
Async XLA Ops:
  0.6 7.9 %collective-permute-start = (bf16[128,2048]{1,0:T(8,128)(2,1)}, bf16[128,2048]{1,0:T(8,128)(2,1)S(1)}, u32[]{:S(2)}, u32[]{:S(2)}) collective-permute-start(bf16[128,2048]{1,0:T(8,128)(2,1)} %own_hbm.1), channel_id=1, source_target_pairs={{0,1},{1,0},{2,3},{3,2},{4,5},{5,4},{6,7},{7,6},{8,9},{9,8},{10,11... | collective-permute-start | bytes 1572872 | tf_op jit(solution)/shard_map/ppermute | solution.py:53
  2.2 10.9 %collective-permute-start.1 = (bf16[80,2048]{1,0:T(8,128)(2,1)S(1)}, bf16[80,2048]{1,0:T(8,128)(2,1)S(1)}, u32[]{:S(2)}, u32[]{:S(2)}) collective-permute-start(bf16[80,2048]{1,0:T(8,128)(2,1)S(1)} %slice.6), channel_id=1, source_target_pairs={{0,2},{1,3},{2,0},{3,1},{4,6},{5,7},{6,4},{7,5},{8,10},{9,11},{10,... | collective-permute-start | bytes 983048 | tf_op jit(solution)/shard_map/ppermute | solution.py:53
  13.1 3.2 %collective-permute-start.2 = (bf16[80,2048]{1,0:T(8,128)(2,1)S(1)}, bf16[80,2048]{1,0:T(8,128)(2,1)S(1)}, u32[]{:S(2)}, u32[]{:S(2)}) collective-permute-start(bf16[80,2048]{1,0:T(8,128)(2,1)S(1)} %collective-permute-done.1.piece_ref), channel_id=1, source_target_pairs={{0,1},{1,0},{2,3},{3,2},{4,5},{5,4},{6,7},{7,6},{8,9},{9,8},{10,11... | collective-permute-start | bytes 983048 | tf_op jit(solution)/shard_map/ppermute | solution.py:53
  14.1 7.4 %collective-permute-start.4 = (bf16[48,2048]{1,0:T(8,128)(2,1)S(1)}, bf16[48,2048]{1,0:T(8,128)(2,1)S(1)}, u32[]{:S(2)}, u32[]{:S(2)}) collective-permute-start(bf16[48,2048]{1,0:T(8,128)(2,1)S(1)} %slice.7), channel_id=1, source_target_pairs={{0,2},{1,3},{2,0},{3,1},{4,6},{5,7},{6,4},{7,5},{8,10},{9,11},{10,... | collective-permute-start | bytes 589832 | tf_op jit(solution)/shard_map/ppermute | solution.py:53
  21.4 3.3 %collective-permute-start.5 = (bf16[48,2048]{1,0:T(8,128)(2,1)S(1)}, bf16[48,2048]{1,0:T(8,128)(2,1)S(1)}, u32[]{:S(2)}, u32[]{:S(2)}) collective-permute-start(bf16[48,2048]{1,0:T(8,128)(2,1)S(1)} %collective-permute-done.4.piece_ref), channel_id=1, source_target_pairs={{0,1},{1,0},{2,3},{3,2},{4,5},{5,4},{6,7},{7,6},{8,9},{9,8},{10,11... | collective-permute-start | bytes 589832 | tf_op jit(solution)/shard_map/ppermute | solution.py:53
  21.4 7.7 %collective-permute-start.3 = (bf16[80,512]{1,0:T(8,128)(2,1)S(1)}, bf16[80,512]{1,0:T(8,128)(2,1)S(1)}, u32[]{:S(2)}, u32[]{:S(2)}) collective-permute-start(bf16[80,512]{1,0:T(8,128)(2,1)S(1)} %shard_map.80.refs_0_), channel_id=1, source_target_pairs={{0,8},{4,12},{8,0},{12,4},{1,9},{5,13},{9,1},{13,5},{2,10},{6,14},... | collective-permute-start | bytes 245768 | tf_op jit(solution)/shard_map/ppermute | solution.py:53
  29.2 12.5 %collective-permute-start.6 = (bf16[128,512]{1,0:T(8,128)(2,1)S(1)}, bf16[128,512]{1,0:T(8,128)(2,1)S(1)}, u32[]{:S(2)}, u32[]{:S(2)}) collective-permute-start(bf16[128,512]{1,0:T(8,128)(2,1)S(1)} %shard_map.83), channel_id=1, source_target_pairs={{0,4},{4,0},{8,12},{12,8},{1,5},{5,1},{9,13},{13,9},{2,6},{6,2},{1... | collective-permute-start | bytes 393224 | tf_op jit(solution)/shard_map/ppermute | solution.py:53
  30.0 6.3 %collective-permute-start.9 = (bf16[80,512]{1,0:T(8,128)(2,1)S(1)}, bf16[80,512]{1,0:T(8,128)(2,1)S(1)}, u32[]{:S(2)}, u32[]{:S(2)}) collective-permute-start(bf16[80,512]{1,0:T(8,128)(2,1)S(1)} %shard_map.80.refs_0_), channel_id=1, source_target_pairs={{0,4},{4,0},{8,12},{12,8},{1,5},{5,1},{9,13},{13,9},{2,6},{6,2},{1... | collective-permute-start | bytes 245768 | tf_op jit(solution)/shard_map/ppermute | solution.py:53
  31.3 8.6 %collective-permute-start.7 = (bf16[48,512]{1,0:T(8,128)(2,1)S(1)}, bf16[48,512]{1,0:T(8,128)(2,1)S(1)}, u32[]{:S(2)}, u32[]{:S(2)}) collective-permute-start(bf16[48,512]{1,0:T(8,128)(2,1)S(1)} %shard_map.82.refs_1_), channel_id=1, source_target_pairs={{0,12},{4,8},{8,4},{12,0},{1,13},{5,9},{9,5},{13,1},{2,14},{6,10},... | collective-permute-start | bytes 147464 | tf_op jit(solution)/shard_map/ppermute | solution.py:53
  34.8 6.1 %collective-permute-start.8 = (bf16[48,512]{1,0:T(8,128)(2,1)S(1)}, bf16[48,512]{1,0:T(8,128)(2,1)S(1)}, u32[]{:S(2)}, u32[]{:S(2)}) collective-permute-start(bf16[48,512]{1,0:T(8,128)(2,1)S(1)} %shard_map.82.refs_1_), channel_id=1, source_target_pairs={{0,8},{4,12},{8,0},{12,4},{1,9},{5,13},{9,1},{13,5},{2,10},{6,14},... | collective-permute-start | bytes 147464 | tf_op jit(solution)/shard_map/ppermute | solution.py:53
